TPU v7x, 32 devices: a whole 2x2x4 slice. The times are simulated.
32 devices in a mesh: dp: 8 (over z, x), fsdp: 4 (over y, core).
Axes of the slice: x: 2, y: 2, z: 4, core: 2. Of those that a mesh axis runs over, the one named last changes fastest.
Arguments:
- tokens: bfloat16 [8192, 2048], P(('dp', 'fsdp')), may hold values from -6 to 6
- segments: int32 [8192], P(('dp', 'fsdp')), may hold values from 0 to 3, as said below
- gain_attn: float32 [2048], P('dp'), may hold values from 0.1 to 1.9
- w_query: float32 [2048, 2048], P('dp', 'fsdp'), may hold values from -0.125 to 0.125
- w_key: float32 [2048, 256], P('dp', 'fsdp'), may hold values from -0.125 to 0.125
- w_value: float32 [2048, 256], P('dp', 'fsdp'), may hold values from -0.125 to 0.125
- w_out: float32 [2048, 2048], P('fsdp', 'dp'), may hold values from -0.75 to 0.75
- gain_mlp: float32 [2048], P('dp'), may hold values from 0.1 to 1.9
- w_gate: float32 [2048, 5632], P('dp', 'fsdp'), may hold values from -0.125 to 0.125
- w_up: float32 [2048, 5632], P('dp', 'fsdp'), may hold values from -0.125 to 0.125
- w_down: float32 [5632, 2048], P('fsdp', 'dp'), may hold values from -0.078125 to 0.078125
- cotangent: bfloat16 [8192, 2048], P(('dp', 'fsdp')), may hold values from -6 to 6
Outputs:
- layer_out: bfloat16 [8192, 2048], P(('dp', 'fsdp'))
- grad_tokens: bfloat16 [8192, 2048], P(('dp', 'fsdp'))
- grad_gain_attn: float32 [2048], P('dp')
- grad_w_query: float32 [2048, 2048], P('dp', 'fsdp')
- grad_w_key: float32 [2048, 256], P('dp', 'fsdp')
- grad_w_value: float32 [2048, 256], P('dp', 'fsdp')
- grad_w_out: float32 [2048, 2048], P('fsdp', 'dp')
- grad_gain_mlp: float32 [2048], P('dp')
- grad_w_gate: float32 [2048, 5632], P('dp', 'fsdp')
- grad_w_up: float32 [2048, 5632], P('dp', 'fsdp')
- grad_w_down: float32 [5632, 2048], P('fsdp', 'dp')
Inputs may be any that keep to these rules, and one draw needn't show every extreme that they name: `segments`: on each device's 256 tokens the ids number 1 to 4 whole sequences from 0 up, never falling; every sequence has 64, 128 or 256 tokens; some device holds one sequence and some four.
All inputs are finite; a program needn't handle non-finite values.
Results may differ from a plain program's by a relative error of at most 0.02.
Values may be sent and summed in bfloat16 or wider, within the bound.
No kernel may reach another device: no remote copies, remote signals or barrier semaphores. Data moves between devices by JAX's collectives and lax.ppermute only.
A program may use at most 448 MiB of HBM per device.

v0:
```python
import math

import jax
import jax.numpy as jnp
from jax import lax
from jax.sharding import PartitionSpec as P

HEAD_DIM = 64


EPSILON = 1e-05
rope_base = 10000.0


def tables(segment_block):
    rows_here = segment_block.shape[0]
    places = jnp.arange(rows_here, dtype=jnp.int32)
    same_segment = segment_block[:, None] == segment_block[None, :]
    first_index = jnp.min(jnp.where(same_segment, places[None, :], rows_here), axis=1)
    offsets = (places - first_index).astype(jnp.float32)
    half_dim = HEAD_DIM // 2
    frequencies = jnp.exp(
        jnp.arange(half_dim, dtype=jnp.float32) * (-2.0 * math.log(rope_base) / HEAD_DIM)
    )
    angles = offsets[:, None] * frequencies[None, :]
    cosine = jnp.concatenate([jnp.cos(angles), jnp.cos(angles)], axis=1)[:, None, :]
    sine_part = jnp.concatenate([jnp.sin(angles), jnp.sin(angles)], axis=1)[:, None, :]
    allowed = same_segment & (places[:, None] >= places[None, :])
    return (cosine, sine_part, allowed)


def rotate(values, cosine, sine_part):
    half_dim = values.shape[-1] // 2
    turned = jnp.concatenate([-values[..., half_dim:], values[..., :half_dim]], axis=-1)
    return values * cosine + turned * sine_part


def group_inputs(tokens, segments, cotangent):
    return (tokens, segments, cotangent, 1)


def attention_weights(gain_attn, w_query, w_key, w_value, w_out):
    low_type = jnp.bfloat16
    rows_full = (
        lax.all_gather(gain_attn.astype(low_type), "dp", axis=0, tiled=True),
        lax.all_gather(w_query.astype(low_type), "dp", axis=0, tiled=True),
        lax.all_gather(w_key.astype(low_type), "dp", axis=0, tiled=True),
        lax.all_gather(w_value.astype(low_type), "dp", axis=0, tiled=True),
        lax.all_gather(w_out.astype(low_type), "dp", axis=1, tiled=True),
    )
    wide_cols = (
        lax.all_gather(rows_full[1], "fsdp", axis=1, tiled=True),
        lax.all_gather(rows_full[2], "fsdp", axis=1, tiled=True),
        lax.all_gather(rows_full[3], "fsdp", axis=1, tiled=True),
        lax.all_gather(rows_full[4], "fsdp", axis=0, tiled=True),
    )
    return (rows_full[0], wide_cols[0], wide_cols[1], wide_cols[2], wide_cols[3])


def feed_weights(gain_mlp, w_gate, w_up, w_down):
    low_type = jnp.bfloat16
    rows_full = (
        lax.all_gather(gain_mlp.astype(low_type), "dp", axis=0, tiled=True),
        lax.all_gather(w_gate.astype(low_type), "dp", axis=0, tiled=True),
        lax.all_gather(w_up.astype(low_type), "dp", axis=0, tiled=True),
        lax.all_gather(w_down.astype(low_type), "dp", axis=1, tiled=True),
    )
    wide_cols = (
        lax.all_gather(rows_full[1], "fsdp", axis=1, tiled=True),
        lax.all_gather(rows_full[2], "fsdp", axis=1, tiled=True),
        lax.all_gather(rows_full[3], "fsdp", axis=0, tiled=True),
    )
    return (rows_full[0], wide_cols[0], wide_cols[1], wide_cols[2])


def reduce_attention(grad_gain, grad_query, grad_key, grad_value, grad_output):
    terms = (
        lax.psum_scatter(
            jnp.tile(grad_gain, lax.axis_size("fsdp")).astype(jnp.bfloat16),
            "fsdp",
            scatter_dimension=0,
            tiled=True,
        ).astype(jnp.float32),
        lax.psum_scatter(
            grad_query.astype(jnp.bfloat16), "fsdp", scatter_dimension=1, tiled=True
        ).astype(jnp.float32),
        lax.psum_scatter(
            grad_key.astype(jnp.bfloat16), "fsdp", scatter_dimension=1, tiled=True
        ).astype(jnp.float32),
        lax.psum_scatter(
            grad_value.astype(jnp.bfloat16), "fsdp", scatter_dimension=1, tiled=True
        ).astype(jnp.float32),
        lax.psum_scatter(
            grad_output.astype(jnp.bfloat16), "fsdp", scatter_dimension=0, tiled=True
        ).astype(jnp.float32),
    )
    return (
        lax.psum_scatter(
            terms[0].astype(jnp.bfloat16), "dp", scatter_dimension=0, tiled=True
        ).astype(jnp.float32),
        lax.psum_scatter(
            terms[1].astype(jnp.bfloat16), "dp", scatter_dimension=0, tiled=True
        ).astype(jnp.float32),
        lax.psum_scatter(
            terms[2].astype(jnp.bfloat16), "dp", scatter_dimension=0, tiled=True
        ).astype(jnp.float32),
        lax.psum_scatter(
            terms[3].astype(jnp.bfloat16), "dp", scatter_dimension=0, tiled=True
        ).astype(jnp.float32),
        lax.psum_scatter(
            terms[4].astype(jnp.bfloat16), "dp", scatter_dimension=1, tiled=True
        ).astype(jnp.float32),
    )


def reduce_feed(grad_gain, grad_gate, grad_upward, grad_down):
    terms = (
        lax.psum_scatter(
            jnp.tile(grad_gain, lax.axis_size("fsdp")).astype(jnp.bfloat16),
            "fsdp",
            scatter_dimension=0,
            tiled=True,
        ).astype(jnp.float32),
        lax.psum_scatter(
            grad_gate.astype(jnp.bfloat16), "fsdp", scatter_dimension=1, tiled=True
        ).astype(jnp.float32),
        lax.psum_scatter(
            grad_upward.astype(jnp.bfloat16), "fsdp", scatter_dimension=1, tiled=True
        ).astype(jnp.float32),
        lax.psum_scatter(
            grad_down.astype(jnp.bfloat16), "fsdp", scatter_dimension=0, tiled=True
        ).astype(jnp.float32),
    )
    return (
        lax.psum_scatter(
            terms[0].astype(jnp.bfloat16), "dp", scatter_dimension=0, tiled=True
        ).astype(jnp.float32),
        lax.psum_scatter(
            terms[1].astype(jnp.bfloat16), "dp", scatter_dimension=0, tiled=True
        ).astype(jnp.float32),
        lax.psum_scatter(
            terms[2].astype(jnp.bfloat16), "dp", scatter_dimension=0, tiled=True
        ).astype(jnp.float32),
        lax.psum_scatter(
            terms[3].astype(jnp.bfloat16), "dp", scatter_dimension=1, tiled=True
        ).astype(jnp.float32),
    )


def on_device(
    tokens,
    segments,
    gain_attn,
    w_query,
    w_key,
    w_value,
    w_out,
    gain_mlp,
    w_gate,
    w_up,
    w_down,
    cotangent,
):
    low_type = jnp.bfloat16
    wide_type = jnp.float32
    score_scale = HEAD_DIM ** (-0.5)
    token_rows, segment_rows, cotangent_rows, blocks = group_inputs(tokens, segments, cotangent)
    rows_all = token_rows.shape[0]
    block_rows = rows_all // blocks
    attn_full = attention_weights(gain_attn, w_query, w_key, w_value, w_out)
    feed_full = feed_weights(gain_mlp, w_gate, w_up, w_down)
    gain_one = attn_full[0].astype(wide_type)
    query_full, key_full, value_full, out_full = (
        attn_full[1],
        attn_full[2],
        attn_full[3],
        attn_full[4],
    )
    gain_two = feed_full[0].astype(wide_type)
    gate_full, up_full, down_full = (feed_full[1], feed_full[2], feed_full[3])
    heads_here = query_full.shape[1] // HEAD_DIM
    kv_here = key_full.shape[1] // HEAD_DIM
    group_size = heads_here // kv_here
    token_float = token_rows.astype(wide_type)
    inv_first = lax.rsqrt(jnp.mean(token_float * token_float, axis=-1, keepdims=True) + EPSILON)
    unit_attn = token_float * inv_first
    normed = (unit_attn * gain_one).astype(low_type)
    cosine, sine_part, allowed = jax.vmap(tables)(segment_rows.reshape(blocks, block_rows))
    query_proj = jnp.dot(normed, query_full, preferred_element_type=wide_type).reshape(
        blocks, block_rows, heads_here, HEAD_DIM
    )
    keys_proj = jnp.dot(normed, key_full, preferred_element_type=wide_type).reshape(
        blocks, block_rows, kv_here, HEAD_DIM
    )
    values_low = (
        jnp.dot(normed, value_full, preferred_element_type=wide_type)
        .astype(low_type)
        .reshape(blocks, block_rows, kv_here, HEAD_DIM)
    )
    query_rot = (
        rotate(query_proj, cosine, sine_part)
        .astype(low_type)
        .reshape(blocks, block_rows, kv_here, group_size, HEAD_DIM)
    )
    keys_rot = rotate(keys_proj, cosine, sine_part).astype(low_type)
    scores = (
        jnp.einsum("btgrd,bugd->bgrtu", query_rot, keys_rot, preferred_element_type=wide_type)
        * score_scale
    )
    masked = jnp.where(allowed[:, None, None], scores, -1e30)
    row_peak = jnp.max(masked, axis=-1, keepdims=True)
    exponent = jnp.exp(masked - row_peak)
    row_total = jnp.sum(exponent, axis=-1, keepdims=True)
    weights_soft = exponent / row_total
    log_total = row_peak + jnp.log(row_total)
    mixed_heads = jnp.einsum(
        "bgrtu,bugd->btgrd",
        weights_soft.astype(low_type),
        values_low,
        preferred_element_type=wide_type,
    )
    mixed_heads = mixed_heads.reshape(rows_all, heads_here * HEAD_DIM).astype(low_type)
    hidden = token_float + jnp.dot(mixed_heads, out_full, preferred_element_type=wide_type)
    inv_second = lax.rsqrt(jnp.mean(hidden * hidden, axis=-1, keepdims=True) + EPSILON)
    unit_mlp = hidden * inv_second
    normed_mlp = (unit_mlp * gain_two).astype(low_type)
    gate_proj = jnp.dot(normed_mlp, gate_full, preferred_element_type=wide_type)
    upward = jnp.dot(normed_mlp, up_full, preferred_element_type=wide_type)
    gate_sigmoid = jax.nn.sigmoid(gate_proj)
    activation = (gate_proj * gate_sigmoid * upward).astype(low_type)
    down_terms = jnp.dot(activation, down_full, preferred_element_type=wide_type)
    layer_out = (hidden + down_terms).astype(low_type)
    feed_back = feed_weights(gain_mlp, w_gate, w_up, w_down)
    gate_back, up_back, down_back = (feed_back[1], feed_back[2], feed_back[3])
    grad_down = jnp.einsum(
        "tf,td->fd", activation, cotangent_rows, preferred_element_type=wide_type
    )
    grad_act = jnp.einsum("td,fd->tf", cotangent_rows, down_back, preferred_element_type=wide_type)
    grad_gate = (
        grad_act * upward * gate_sigmoid * (1.0 + gate_proj * (1.0 - gate_sigmoid))
    ).astype(low_type)
    grad_upward = (grad_act * gate_proj * gate_sigmoid).astype(low_type)
    grad_w_gate = jnp.einsum("tc,tf->cf", normed_mlp, grad_gate, preferred_element_type=wide_type)
    grad_w_up = jnp.einsum("tc,tf->cf", normed_mlp, grad_upward, preferred_element_type=wide_type)
    grad_normed_mlp = jnp.einsum(
        "tf,cf->tc", grad_gate, gate_back, preferred_element_type=wide_type
    )
    grad_normed_mlp = grad_normed_mlp + jnp.einsum(
        "tf,cf->tc", grad_upward, up_back, preferred_element_type=wide_type
    )
    grad_gain_mlp = jnp.sum(grad_normed_mlp * unit_mlp, axis=0)
    scaled_mlp = grad_normed_mlp * gain_two
    grad_hidden = cotangent_rows.astype(wide_type) + inv_second * (
        scaled_mlp - unit_mlp * jnp.mean(scaled_mlp * unit_mlp, axis=-1, keepdims=True)
    )
    feed_grads = reduce_feed(grad_gain_mlp, grad_w_gate, grad_w_up, grad_down)
    attn_back = attention_weights(gain_attn, w_query, w_key, w_value, w_out)
    query_back, key_back, value_back, out_back = (
        attn_back[1],
        attn_back[2],
        attn_back[3],
        attn_back[4],
    )
    grad_branch = grad_hidden.astype(low_type)
    grad_w_out = jnp.einsum("tc,td->cd", mixed_heads, grad_branch, preferred_element_type=wide_type)
    grad_mixed = jnp.einsum(
        "td,cd->tc", grad_branch, out_back, preferred_element_type=wide_type
    ).astype(low_type)
    grad_mixed = grad_mixed.reshape(blocks, block_rows, kv_here, group_size, HEAD_DIM)
    scores_again = (
        jnp.einsum("btgrd,bugd->bgrtu", query_rot, keys_rot, preferred_element_type=wide_type)
        * score_scale
    )
    weights_again = jnp.exp(jnp.where(allowed[:, None, None], scores_again, -1e30) - log_total)
    grad_weights = jnp.einsum(
        "btgrd,bugd->bgrtu", grad_mixed, values_low, preferred_element_type=wide_type
    )
    grad_values = jnp.einsum(
        "bgrtu,btgrd->bugd",
        weights_again.astype(low_type),
        grad_mixed,
        preferred_element_type=wide_type,
    )
    grad_values = grad_values.astype(low_type).reshape(rows_all, kv_here * HEAD_DIM)
    row_delta = jnp.sum(weights_again * grad_weights, axis=-1, keepdims=True)
    grad_scores = (weights_again * (grad_weights - row_delta)).astype(low_type)
    grad_query_rot = (
        jnp.einsum("bgrtu,bugd->btgrd", grad_scores, keys_rot, preferred_element_type=wide_type)
        * score_scale
    )
    grad_keys_rot = (
        jnp.einsum("bgrtu,btgrd->bugd", grad_scores, query_rot, preferred_element_type=wide_type)
        * score_scale
    )
    grad_query = (
        rotate(grad_query_rot.reshape(blocks, block_rows, heads_here, HEAD_DIM), cosine, -sine_part)
        .astype(low_type)
        .reshape(rows_all, heads_here * HEAD_DIM)
    )
    grad_keys = (
        rotate(grad_keys_rot, cosine, -sine_part)
        .astype(low_type)
        .reshape(rows_all, kv_here * HEAD_DIM)
    )
    grad_w_query = jnp.einsum("tc,te->ce", normed, grad_query, preferred_element_type=wide_type)
    grad_w_key = jnp.einsum("tc,te->ce", normed, grad_keys, preferred_element_type=wide_type)
    grad_w_value = jnp.einsum("tc,te->ce", normed, grad_values, preferred_element_type=wide_type)
    grad_normed = jnp.einsum("te,ce->tc", grad_query, query_back, preferred_element_type=wide_type)
    grad_normed = grad_normed + jnp.einsum(
        "te,ce->tc", grad_keys, key_back, preferred_element_type=wide_type
    )
    grad_normed = grad_normed + jnp.einsum(
        "te,ce->tc", grad_values, value_back, preferred_element_type=wide_type
    )
    grad_gain_attn = jnp.sum(grad_normed * unit_attn, axis=0)
    scaled_attn = grad_normed * gain_one
    grad_inputs = grad_hidden + inv_first * (
        scaled_attn - unit_attn * jnp.mean(scaled_attn * unit_attn, axis=-1, keepdims=True)
    )
    grad_tokens = grad_inputs.astype(low_type)
    attn_grads = reduce_attention(
        grad_gain_attn, grad_w_query, grad_w_key, grad_w_value, grad_w_out
    )
    return (
        layer_out,
        grad_tokens,
        attn_grads[0],
        attn_grads[1],
        attn_grads[2],
        attn_grads[3],
        attn_grads[4],
        feed_grads[0],
        feed_grads[1],
        feed_grads[2],
        feed_grads[3],
    )


def solution(mesh):
    placed = (
        P(("dp", "fsdp"), None),
        P(("dp", "fsdp")),
        P("dp"),
        P("dp", "fsdp"),
        P("dp", "fsdp"),
        P("dp", "fsdp"),
        P("fsdp", "dp"),
        P("dp"),
        P("dp", "fsdp"),
        P("dp", "fsdp"),
        P("fsdp", "dp"),
        P(("dp", "fsdp"), None),
    )
    return jax.shard_map(
        on_device,
        mesh=mesh,
        in_specs=placed,
        out_specs=(
            P(("dp", "fsdp"), None),
            P(("dp", "fsdp"), None),
            P("dp"),
            P("dp", "fsdp"),
            P("dp", "fsdp"),
            P("dp", "fsdp"),
            P("fsdp", "dp"),
            P("dp"),
            P("dp", "fsdp"),
            P("dp", "fsdp"),
            P("fsdp", "dp"),
        ),
        check_vma=False,
    )
```

profile of v0, /device:TPU:0, one launch (start us, length us, event | category | flops | bytes accessed | tf_op | source)
XLA Modules:
  0.0 2389.2 jit_solution(8841014630282834477)
XLA Ops:
  14.7 35.2 %all_gather.65 = bf16[2048,64]{0,1:T(8,128)(2,1)} all-gather(bf16[256,64]{0,1:T(8,128)(2,1)S(1)} %convert_element_type.225), channel_id=1, replica_groups=mesh['dp'=8,'fsdp'=4] {'dp'}, dimensions={0}, use_global_device_ids=true | all-gather | bytes 294912 | tf_op jit(solution)/shard_map/all_gather | solution.py:47
  50.0 33.1 %all_gather.63 = bf16[2048,64]{0,1:T(8,128)(2,1)} all-gather(bf16[256,64]{0,1:T(8,128)(2,1)S(1)} %convert_element_type.223), channel_id=1, replica_groups=mesh['dp'=8,'fsdp'=4] {'dp'}, dimensions={0}, use_global_device_ids=true | all-gather | bytes 294912 | tf_op jit(solution)/shard_map/all_gather | solution.py:48
  84.0 34.4 %all-gather.23.cloned.1.call-done = bf16[512,2048]{1,0:T(8,128)(2,1)} async-done(((bf16[512,256]{1,0:T(8,128)(2,1)}), bf16[512,2048]{1,0:T(8,128)(2,1)}) %all-gather.23.cloned.1.call-update) | async-done | bytes 2097168 | tf_op jit(solution)/shard_map/all_gather | solution.py:49
  118.4 93.6 %all-gather.27.cloned.1.call-done = bf16[2048,1408]{1,0:T(8,128)(2,1)} async-done(((bf16[256,1408]{1,0:T(8,128)(2,1)}), bf16[2048,1408]{1,0:T(8,128)(2,1)}) %all-gather.27.cloned.1.call-update) | async-done | bytes 5767184 | tf_op jit(solution)/shard_map/all_gather | solution.py:64
  212.1 93.4 %all-gather.31.cloned.1.call-done = bf16[2048,1408]{1,0:T(8,128)(2,1)} async-done(((bf16[256,1408]{1,0:T(8,128)(2,1)}), bf16[2048,1408]{1,0:T(8,128)(2,1)}) %all-gather.31.cloned.1.call-update) | async-done | bytes 5767184 | tf_op jit(solution)/shard_map/all_gather | solution.py:65
  305.5 94.2 %all-gather.35.cloned.1.call-done = bf16[1408,2048]{1,0:T(8,128)(2,1)} async-done(((bf16[1408,256]{1,0:T(8,128)(2,1)}), bf16[1408,2048]{1,0:T(8,128)(2,1)}) %all-gather.35.cloned.1.call-update) | async-done | bytes 5767184 | tf_op jit(solution)/shard_map/all_gather | solution.py:66
  400.4 17.7 all-gather
  418.2 16.8 all-gather.1
  440.3 54.0 %all-gather.21.cloned.1.call-done = bf16[2048,2048]{1,0:T(8,128)(2,1)} async-done(((bf16[2048,512]{1,0:T(8,128)(2,1)}), bf16[2048,2048]{1,0:T(8,128)(2,1)}) %all-gather.21.cloned.1.call-update) | async-done | bytes 8388624 | tf_op jit(solution)/shard_map/all_gather | solution.py:52
  510.3 43.9 %all-gather.25.cloned.1.call-done = bf16[2048,2048]{1,0:T(8,128)(2,1)} async-done(((bf16[512,2048]{1,0:T(8,128)(2,1)}), bf16[2048,2048]{1,0:T(8,128)(2,1)}) %all-gather.25.cloned.1.call-update) | async-done | bytes 8388624 | tf_op jit(solution)/shard_map/all_gather | solution.py:55
  562.0 136.7 %all-gather.29.cloned.1.call-done = bf16[2048,5632]{1,0:T(8,128)(2,1)} async-done(((bf16[2048,1408]{1,0:T(8,128)(2,1)}), bf16[2048,5632]{1,0:T(8,128)(2,1)}) %all-gather.29.cloned.1.call-update) | async-done | bytes 23068688 | tf_op jit(solution)/shard_map/all_gather | solution.py:69
  698.8 13.0 fusion.57
  711.8 131.7 %all-gather.33.cloned.1.call-done = bf16[2048,5632]{1,0:T(8,128)(2,1)} async-done(((bf16[2048,1408]{1,0:T(8,128)(2,1)}), bf16[2048,5632]{1,0:T(8,128)(2,1)}) %all-gather.33.cloned.1.call-update) | async-done | bytes 23068688 | tf_op jit(solution)/shard_map/all_gather | solution.py:70
  843.5 13.1 fusion.58
  856.6 131.6 %all-gather.37.cloned.1.call-done = bf16[5632,2048]{1,0:T(8,128)(2,1)} async-done(((bf16[1408,2048]{1,0:T(8,128)(2,1)}), bf16[5632,2048]{1,0:T(8,128)(2,1)}) %all-gather.37.cloned.1.call-update) | async-done | bytes 23068688 | tf_op jit(solution)/shard_map/all_gather | solution.py:71
  988.2 18.6 multiply_convert_fusion
  1019.4 13.7 multiply_reduce_fusion
  1083.0 13.0 convolution_convert_fusion.2
  1096.1 30.9 %copy.62 = bf16[2048,5632]{0,1:T(8,128)(2,1)} copy(bf16[2048,5632]{1,0:T(8,128)(2,1)} %convolution_convert_fusion.2) | data formatting | bytes 46137344
  1127.3 13.2 convolution_convert_fusion.1
  1140.5 29.0 %copy.64 = bf16[2048,5632]{0,1:T(8,128)(2,1)} copy(bf16[2048,5632]{1,0:T(8,128)(2,1)} %convolution_convert_fusion.1) | data formatting | bytes 46137344
  1185.1 74.3 %reduce-scatter.31.cloned.1.call-done = bf16[512,2048]{1,0:T(8,128)(2,1)} async-done(((bf16[2048,2048]{1,0:T(8,128)(2,1)}), bf16[512,2048]{1,0:T(8,128)(2,1)}) %reduce-scatter.31.cloned.1.call-update) | async-done | bytes 2097168 | tf_op jit(solution)/shard_map/reduce_scatter | solution.py:93
  1259.4 169.2 %reduce-scatter.43.cloned.1.call-done = bf16[1408,2048]{1,0:T(8,128)(2,1)} async-done(((bf16[5632,2048]{1,0:T(8,128)(2,1)}), bf16[1408,2048]{1,0:T(8,128)(2,1)}) %reduce-scatter.43.cloned.1.call-update) | async-done | bytes 5767184
  1436.9 161.1 %reduce-scatter.45.cloned.1.call-done = bf16[1408,2048]{1,0:T(8,128)(2,1)} async-done(((bf16[5632,2048]{1,0:T(8,128)(2,1)}), bf16[1408,2048]{1,0:T(8,128)(2,1)}) %reduce-scatter.45.cloned.1.call-update) | async-done | bytes 5767184
  1606.5 160.9 %reduce-scatter.39.cloned.1.call-done = bf16[1408,2048]{1,0:T(8,128)(2,1)} async-done(((bf16[5632,2048]{1,0:T(8,128)(2,1)}), bf16[1408,2048]{1,0:T(8,128)(2,1)}) %reduce-scatter.39.cloned.1.call-update) | async-done | bytes 5767184 | tf_op jit(solution)/shard_map/reduce_scatter | solution.py:130
  1791.0 21.9 all-reduce.4
  1834.0 63.0 %reduce-scatter.29.cloned.1.call-done = bf16[256,64]{0,1:T(8,128)(2,1)} async-done(((bf16[2048,64]{0,1:T(8,128)(2,1)}), bf16[256,64]{0,1:T(8,128)(2,1)}) %reduce-scatter.29.cloned.1.call-update) | async-done | bytes 32784 | tf_op jit(solution)/shard_map/reduce_scatter | solution.py:107
  1898.4 69.3 %reduce-scatter.21.cloned.1.call-done = bf16[256,512]{1,0:T(8,128)(2,1)} async-done(((bf16[2048,512]{1,0:T(8,128)(2,1)}), bf16[256,512]{1,0:T(8,128)(2,1)}) %reduce-scatter.21.cloned.1.call-update) | async-done | bytes 262160 | tf_op jit(solution)/shard_map/reduce_scatter | solution.py:101
  1969.5 69.5 %reduce-scatter.33.cloned.1.call-done = bf16[512,256]{1,0:T(8,128)(2,1)} async-done(((bf16[512,2048]{1,0:T(8,128)(2,1)}), bf16[512,256]{1,0:T(8,128)(2,1)}) %reduce-scatter.33.cloned.1.call-update) | async-done | bytes 262160 | tf_op jit(solution)/shard_map/reduce_scatter | solution.py:110
  2040.8 111.1 %reduce-scatter.35.cloned.1.call-done = bf16[256,1408]{1,0:T(8,128)(2,1)} async-done(((bf16[2048,1408]{1,0:T(8,128)(2,1)}), bf16[256,1408]{1,0:T(8,128)(2,1)}) %reduce-scatter.35.cloned.1.call-update) | async-done | bytes 720912 | tf_op jit(solution)/shard_map/reduce_scatter | solution.py:138
  2154.2 111.6 %reduce-scatter.37.cloned.1.call-done = bf16[256,1408]{1,0:T(8,128)(2,1)} async-done(((bf16[2048,1408]{1,0:T(8,128)(2,1)}), bf16[256,1408]{1,0:T(8,128)(2,1)}) %reduce-scatter.37.cloned.1.call-update) | async-done | bytes 720912 | tf_op jit(solution)/shard_map/reduce_scatter | solution.py:141
  2268.1 111.9 %reduce-scatter.41.cloned.1.call-done = bf16[1408,256]{1,0:T(8,128)(2,1)} async-done(((bf16[1408,2048]{1,0:T(8,128)(2,1)}), bf16[1408,256]{1,0:T(8,128)(2,1)}) %reduce-scatter.41.cloned.1.call-update) | async-done | bytes 720912 | tf_op jit(solution)/shard_map/reduce_scatter | solution.py:144
  (201 shorter events, 188.2 us)
Async XLA Ops:
  7.2 76.0 %all-gather.19.cloned.1.call-start = ((), (), s32[]{:S(2)}) async-start(), calls=%async_computation.16 | async-start | bytes 2359296 | tf_op jit(solution)/shard_map/all_gather | solution.py:46
  9.2 109.2 %all-gather.23.cloned.1.call-start = ((), (), s32[]{:S(2)}) async-start(), calls=%async_computation.18 | async-start | bytes 2359296 | tf_op jit(solution)/shard_map/all_gather | solution.py:49
  11.0 200.9 %all-gather.27.cloned.1.call-start = ((), (), s32[]{:S(2)}) async-start(), calls=%async_computation.20 | async-start | bytes 6488064 | tf_op jit(solution)/shard_map/all_gather | solution.py:64
  12.1 37.9 %copy-start.21 = (f32[256,64]{0,1:T(8,128)S(1)}, f32[256,64]{0,1:T(8,128)}, u32[]{:S(2)}) copy-start(f32[256,64]{0,1:T(8,128)} %param.17) | copy-start | bytes 196612
  12.1 293.4 %all-gather.31.cloned.1.call-start = ((), (), s32[]{:S(2)}) async-start(), calls=%async_computation.22 | async-start | bytes 6488064 | tf_op jit(solution)/shard_map/all_gather | solution.py:65
  13.1 386.6 %all-gather.35.cloned.1.call-start = ((), (), s32[]{:S(2)}) async-start(), calls=%async_computation.24 | async-start | bytes 6488064 | tf_op jit(solution)/shard_map/all_gather | solution.py:66
  14.6 422.0 %all-gather.17.cloned.1.call-start = ((), (), s32[]{:S(2)}) async-start(), calls=%async_computation.15 | async-start | bytes 1310720 | tf_op jit(solution)/shard_map/all_gather | solution.py:53
  49.9 388.5 %all-gather.15.cloned.1.call-start = ((), (), s32[]{:S(2)}) async-start(), calls=%async_computation.14 | async-start | bytes 1310720 | tf_op jit(solution)/shard_map/all_gather | solution.py:54
  83.2 411.2 %all-gather.21.cloned.1.call-start = ((), (), s32[]{:S(2)}) async-start(), calls=%async_computation.17 | async-start | bytes 10485760 | tf_op jit(solution)/shard_map/all_gather | solution.py:52
  83.9 470.3 %all-gather.25.cloned.1.call-start = ((), (), s32[]{:S(2)}) async-start(), calls=%async_computation.19 | async-start | bytes 10485760 | tf_op jit(solution)/shard_map/all_gather | solution.py:55
  118.4 580.4 %all-gather.29.cloned.1.call-start = ((), (), s32[]{:S(2)}) async-start(), calls=%async_computation.21 | async-start | bytes 28835840 | tf_op jit(solution)/shard_map/all_gather | solution.py:69
  212.0 631.5 %all-gather.33.cloned.1.call-start = ((), (), s32[]{:S(2)}) async-start(), calls=%async_computation.23 | async-start | bytes 28835840 | tf_op jit(solution)/shard_map/all_gather | solution.py:70
  305.5 682.7 %all-gather.37.cloned.1.call-start = ((), (), s32[]{:S(2)}) async-start(), calls=%async_computation.25 | async-start | bytes 28835840 | tf_op jit(solution)/shard_map/all_gather | solution.py:71
  399.7 35.3 %copy-start.22 = (s32[256]{0:T(256)S(1)}, s32[256]{0:T(256)}, u32[]{:S(2)}) copy-start(s32[256]{0:T(256)} %param.13) | copy-start | bytes 3076
  399.7 36.4 %copy-start.2 = (bf16[256,2048]{1,0:T(8,128)(2,1)S(1)}, bf16[256,2048]{1,0:T(8,128)(2,1)}, u32[]{:S(2)}) copy-start(bf16[256,2048]{1,0:T(8,128)(2,1)} %param.12) | copy-start | bytes 3145732
  399.8 782.4 %reduce-scatter.23.cloned.1.call-start = ((), (), s32[]{:S(2)}) async-start(), calls=%async_computation.28 | async-start | bytes 1310720 | tf_op jit(solution)/shard_map/reduce_scatter | solution.py:87
  435.5 620.0 %copy-start.14 = (f32[256,64]{0,1:T(8,128)}, f32[256,64]{0,1:T(8,128)S(1)}, u32[]{:S(2)}) copy-start(f32[256,64]{0,1:T(8,128)S(1)} %fusion.47) | copy-start | bytes 196612
  440.3 64.6 %copy-start.19 = (bf16[256,256]{0,1:T(8,128)(2,1)}, bf16[256,256]{0,1:T(8,128)(2,1)S(1)}, u32[]{:S(2)}) copy-start(bf16[256,256]{0,1:T(8,128)(2,1)S(1)} %convolution_convert_fusion.8) | copy-start | bytes 393220
  560.4 459.0 %copy-start.3 = (f32[256,2048]{1,0:T(8,128)}, f32[256,2048]{1,0:T(8,128)S(1)}, u32[]{:S(2)}) copy-start(f32[256,2048]{1,0:T(8,128)S(1)} %get-tuple-element.35) | copy-start | bytes 6291460
  1057.7 125.0 %reduce-scatter.27.cloned.1.call-start = ((), (), s32[]{:S(2)}) async-start(), calls=%async_computation.30 | async-start | bytes 1310720 | tf_op jit(solution)/shard_map/reduce_scatter | solution.py:90
  1064.5 120.5 %reduce-scatter.19.cloned.1.call-start = ((), (), s32[]{:S(2)}) async-start(), calls=%async_computation.26 | async-start | bytes 10485760 | tf_op jit(solution)/shard_map/reduce_scatter | solution.py:84
  1076.1 183.3 %reduce-scatter.31.cloned.1.call-start = ((), (), s32[]{:S(2)}) async-start(), calls=%async_computation.32 | async-start | bytes 10485760 | tf_op jit(solution)/shard_map/reduce_scatter | solution.py:93
  1083.0 345.6 %reduce-scatter.43.cloned.1.call-start = ((), (), s32[]{:S(2)}) async-start(), calls=%async_computation.38 | async-start | bytes 28835840
  1127.0 471.0 %reduce-scatter.45.cloned.1.call-start = ((), (), s32[]{:S(2)}) async-start(), calls=%async_computation.39 | async-start | bytes 28835840
  1169.4 598.0 %reduce-scatter.39.cloned.1.call-start = ((), (), s32[]{:S(2)}) async-start(), calls=%async_computation.36 | async-start | bytes 28835840 | tf_op jit(solution)/shard_map/reduce_scatter | solution.py:130
  1182.1 650.5 %reduce-scatter.25.cloned.1.call-start = ((), (), s32[]{:S(2)}) async-start(), calls=%async_computation.29 | async-start | bytes 294912 | tf_op jit(solution)/shard_map/reduce_scatter | solution.py:104
  1182.7 714.4 %reduce-scatter.29.cloned.1.call-start = ((), (), s32[]{:S(2)}) async-start(), calls=%async_computation.31 | async-start | bytes 294912 | tf_op jit(solution)/shard_map/reduce_scatter | solution.py:107
  1183.4 784.3 %reduce-scatter.21.cloned.1.call-start = ((), (), s32[]{:S(2)}) async-start(), calls=%async_computation.27 | async-start | bytes 2359296 | tf_op jit(solution)/shard_map/reduce_scatter | solution.py:101
  1185.0 854.0 %reduce-scatter.33.cloned.1.call-start = ((), (), s32[]{:S(2)}) async-start(), calls=%async_computation.33 | async-start | bytes 2359296 | tf_op jit(solution)/shard_map/reduce_scatter | solution.py:110
  1259.4 892.5 %reduce-scatter.35.cloned.1.call-start = ((), (), s32[]{:S(2)}) async-start(), calls=%async_computation.34 | async-start | bytes 6488064 | tf_op jit(solution)/shard_map/reduce_scatter | solution.py:138
  1436.9 828.9 %reduce-scatter.37.cloned.1.call-start = ((), (), s32[]{:S(2)}) async-start(), calls=%async_computation.35 | async-start | bytes 6488064 | tf_op jit(solution)/shard_map/reduce_scatter | solution.py:141
  1606.5 773.5 %reduce-scatter.41.cloned.1.call-start = ((), (), s32[]{:S(2)}) async-start(), calls=%async_computation.37 | async-start | bytes 6488064 | tf_op jit(solution)/shard_map/reduce_scatter | solution.py:144
  (23 other events, 80.7 us)
Sparse Core Ops, SparseCore 0:
  10.7 55.1 all-gather.18
  68.6 49.7 all-gather.22
  121.1 90.8 all-gather.26
  214.6 90.8 all-gather.30
  307.9 91.7 all-gather.34
  401.1 14.9 all-gather.16
  417.7 16.7 all-gather.14
  436.0 58.2 all-gather.20
  495.9 58.2 all-gather.24
  555.6 143.1 all-gather.28
  700.4 143.1 all-gather.32
  844.9 143.2 all-gather.36
  1057.9 24.8 reduce-scatter.22
  1085.9 24.8 reduce-scatter.26
  1113.2 71.7 reduce-scatter.18
  1187.6 71.6 reduce-scatter.30
  1261.8 166.7 reduce-scatter.42
  1431.2 166.7 reduce-scatter.44
  1600.6 166.7 reduce-scatter.38
  1771.0 61.6 reduce-scatter.24
  1836.3 60.6 reduce-scatter.28
  1901.0 66.6 reduce-scatter.20
  1971.7 67.2 reduce-scatter.32
  2043.0 108.9 reduce-scatter.34
  2156.0 109.7 reduce-scatter.36
  2269.8 110.1 reduce-scatter.40
where the time goes:
time: 2400 us; the launch traced here: 2390 us
  waiting for transfers between devices  1920 us (80%)
  matrix products  189 us (8%)
  blocking collectives  135 us (6%)
  local copies, waits for them, and re-layouts  88.9 us (4%)
  other arithmetic  35.7 us (1%)
    unnamed x28, waiting for transfers between devices  333 us
    reduce_scatter x1, waiting for transfers between devices, reduce_feed(): lax.psum_scatter(grad_down.astype(jnp.bfloat16), 'fsdp', scatter_dimensio...  161 us
    all_gather x1, waiting for transfers between devices, feed_weights(): lax.all_gather(rows_full[1], 'fsdp', axis=1, tiled=True)  137 us
    all_gather x1, waiting for transfers between devices, feed_weights(): lax.all_gather(rows_full[2], 'fsdp', axis=1, tiled=True)  132 us
    all_gather x1, waiting for transfers between devices, feed_weights(): lax.all_gather(rows_full[3], 'fsdp', axis=0, tiled=True)  132 us
    reduce_scatter x1, waiting for transfers between devices, reduce_feed(): lax.psum_scatter(terms[3].astype(jnp.bfloat16), 'dp', scatter_dimension=1...  112 us
    reduce_scatter x1, waiting for transfers between devices, reduce_feed(): lax.psum_scatter(terms[2].astype(jnp.bfloat16), 'dp', scatter_dimension=0...  112 us
    reduce_scatter x1, waiting for transfers between devices, reduce_feed(): lax.psum_scatter(terms[1].astype(jnp.bfloat16), 'dp', scatter_dimension=0...  111 us
  transfers between devices with their start and end apart: 26, of which 21 were waited for; matrix products, arithmetic and copies ran while one was open for 10% of the time, Pallas kernels for 0%

commit v1 on v0

v1 whole, which is shorter than its diff:
```python
import math

import jax
import jax.numpy as jnp
from jax import lax
from jax.experimental import pallas as pl
from jax.experimental.pallas import tpu as pltpu
from jax.sharding import PartitionSpec as P

HEAD_DIM = 64
EPSILON = 1e-05
ROPE_BASE = 10000.0
LOW = jnp.bfloat16
WIDE = jnp.float32
LANES = 128


def ring_order(n):
    return list(range(0, n, 2)) + list(range(n - 1, 0, -2))


def ring_perms(n):
    order = ring_order(n)
    forward = [(order[i], order[(i + 1) % n]) for i in range(n)]
    return forward, [(b, a) for a, b in forward]


def place_of(index, n):
    return jnp.where(index % 2 == 0, index // 2, n - (index + 1) // 2)


def index_at(place, n):
    return jnp.where(place < n // 2, 2 * place, 2 * (n - place) - 1)


def ring_gather(own, n):
    forward, backward = ring_perms(n)
    half = own.shape[0] // 2
    chunks = [None] * n
    chunks[0] = own
    ahead = behind = own
    for hop in range(1, n // 2):
        ahead = lax.ppermute(ahead, "dp", forward)
        behind = lax.ppermute(behind, "dp", backward)
        chunks[n - hop] = ahead
        chunks[hop] = behind
    top = lax.ppermute(ahead[:half], "dp", forward)
    bottom = lax.ppermute(behind[half:], "dp", backward)
    chunks[n // 2] = jnp.concatenate([top, bottom], axis=0)
    return chunks


def ring_reduce(parts, n):
    forward, backward = ring_perms(n)
    half = parts[0].shape[0] // 2
    far = parts[n // 2]
    ahead = lax.ppermute(far[:half], "dp", forward)
    behind = lax.ppermute(far[half:], "dp", backward)
    for hop in range(n // 2 - 1, 0, -1):
        mine_ahead, mine_behind = parts[hop], parts[n - hop]
        if hop == n // 2 - 1:
            ahead = jnp.concatenate([mine_ahead[:half] + ahead, mine_ahead[half:]], axis=0)
            behind = jnp.concatenate([mine_behind[:half], mine_behind[half:] + behind], axis=0)
        else:
            ahead = mine_ahead + ahead
            behind = mine_behind + behind
        ahead = lax.ppermute(ahead, "dp", forward)
        behind = lax.ppermute(behind, "dp", backward)
    return parts[0].astype(WIDE) + ahead.astype(WIDE) + behind.astype(WIDE)


def swap_core(value):
    return lax.ppermute(value, "fsdp", [(i, i ^ 1) for i in range(4)])


def swap_pair(value):
    return lax.ppermute(value, "fsdp", [(i, i ^ 2) for i in range(4)])


def group_gather(own):
    pair = swap_pair(own)
    core = swap_core(own)
    return [own, core, pair, swap_core(pair)]


def group_reduce(partial, rows):
    block = [partial[i * rows : (i + 1) * rows] for i in range(4)]
    far = swap_core(block[3])
    near = swap_core(block[1])
    sent = swap_pair(block[2] + far)
    return block[0].astype(WIDE) + near.astype(WIDE) + sent.astype(WIDE)


def turn(values, first_half):
    width = values.shape[-1]
    left = pltpu.roll(values, width - HEAD_DIM // 2, 1)
    right = pltpu.roll(values, HEAD_DIM // 2, 1)
    return jnp.where(first_half, -left, right)


def lane_ids(rows, width):
    return lax.broadcasted_iota(jnp.int32, (rows, width), 1)


def allowed_pairs(column, row):
    rows = column.shape[0]
    later = lax.broadcasted_iota(jnp.int32, (rows, rows), 0)
    earlier = lax.broadcasted_iota(jnp.int32, (rows, rows), 1)
    return (column == row) & (later >= earlier)


def dot_rows(a, b):
    return lax.dot_general(a, b, (((1,), (1,)), ((), ())), preferred_element_type=WIDE)


def dot_firsts(a, b):
    return lax.dot_general(a, b, (((0,), (0,)), ((), ())), preferred_element_type=WIDE)


def attention_forward(qkv_ref, cos_ref, sin_ref, col_ref, row_ref, q_ref, kv_ref, o_ref, lse_ref):
    rows, width = q_ref.shape
    pairs = width // LANES
    cosine, sine = cos_ref[...], sin_ref[...]
    lanes = lane_ids(rows, LANES)
    even = lanes < HEAD_DIM
    first = (lanes % HEAD_DIM) < HEAD_DIM // 2
    keyval = qkv_ref[:, width:]
    keyval_rot = keyval * cosine + turn(keyval, first) * sine
    keyval = jnp.where(even, keyval_rot, keyval)
    kv_ref[...] = keyval.astype(LOW)
    other = pltpu.roll(keyval, HEAD_DIM, 1)
    keys = jnp.where(even, keyval, other).astype(LOW)
    vals = jnp.where(even, other, keyval).astype(LOW)
    allowed = allowed_pairs(col_ref[...], row_ref[0])
    log_sums = jnp.zeros((rows, LANES), WIDE)
    for pair in range(pairs):
        piece = qkv_ref[:, pair * LANES : (pair + 1) * LANES]
        piece = (piece * cosine + turn(piece, first) * sine).astype(LOW)
        q_ref[:, pair * LANES : (pair + 1) * LANES] = piece
        mixed = []
        for side in range(2):
            chosen = jnp.where(even if side == 0 else ~even, piece, jnp.zeros_like(piece))
            scores = dot_rows(chosen, keys) * (HEAD_DIM ** -0.5)
            scores = jnp.where(allowed, scores, -1e30)
            peak = jnp.max(scores, axis=1, keepdims=True)
            powers = jnp.exp(scores - peak)
            total = jnp.sum(powers, axis=1, keepdims=True)
            soft = (powers / total).astype(LOW)
            mixed.append(jnp.dot(soft, vals, preferred_element_type=WIDE))
            log_sums = jnp.where(lanes == 2 * pair + side, peak + jnp.log(total), log_sums)
        o_ref[:, pair * LANES : (pair + 1) * LANES] = jnp.where(even, mixed[0], mixed[1]).astype(LOW)
    lse_ref[...] = log_sums


def attention_backward(q_ref, kv_ref, lse_ref, do_ref, cos_ref, sin_ref, col_ref, row_ref, out_ref):
    rows, width = q_ref.shape
    pairs = width // LANES
    scale = HEAD_DIM ** -0.5
    cosine, sine = cos_ref[...], sin_ref[...]
    lanes = lane_ids(rows, LANES)
    even = lanes < HEAD_DIM
    first = (lanes % HEAD_DIM) < HEAD_DIM // 2
    keyval = kv_ref[...].astype(WIDE)
    other = pltpu.roll(keyval, HEAD_DIM, 1)
    keys = jnp.where(even, keyval, other).astype(LOW)
    vals = jnp.where(even, other, keyval).astype(LOW)
    allowed = allowed_pairs(col_ref[...], row_ref[0])
    log_sums = lse_ref[...]
    grad_keys = jnp.zeros((rows, LANES), WIDE)
    grad_vals = jnp.zeros((rows, LANES), WIDE)
    for pair in range(pairs):
        piece = q_ref[:, pair * LANES : (pair + 1) * LANES]
        grads = do_ref[:, pair * LANES : (pair + 1) * LANES]
        turned = []
        for side in range(2):
            mine = even if side == 0 else ~even
            chosen = jnp.where(mine, piece, jnp.zeros_like(piece))
            chosen_grad = jnp.where(mine, grads, jnp.zeros_like(grads))
            head = 2 * pair + side
            log_sum = log_sums[:, head : head + 1]
            scores = jnp.where(allowed, dot_rows(chosen, keys) * scale, -1e30)
            soft = jnp.exp(scores - log_sum)
            grad_soft = dot_rows(chosen_grad, vals)
            delta = jnp.sum(soft * grad_soft, axis=1, keepdims=True)
            grad_scores = (soft * (grad_soft - delta)).astype(LOW)
            grad_vals = grad_vals + dot_firsts(soft.astype(LOW), chosen_grad)
            grad_keys = grad_keys + dot_firsts(grad_scores, chosen)
            turned.append(jnp.dot(grad_scores, keys, preferred_element_type=WIDE))
        grad_q = jnp.where(even, turned[0], turned[1]) * scale
        grad_q = grad_q * cosine - turn(grad_q, first) * sine
        out_ref[:, pair * LANES : (pair + 1) * LANES] = grad_q.astype(LOW)
    grad_keys = (grad_keys + pltpu.roll(grad_keys, HEAD_DIM, 1)) * scale
    grad_keys = grad_keys * cosine - turn(grad_keys, first) * sine
    grad_vals = grad_vals + pltpu.roll(grad_vals, HEAD_DIM, 1)
    out_ref[:, width:] = jnp.where(even, grad_keys, grad_vals).astype(LOW)


def by_rows(rows, width):
    return pl.BlockSpec((rows, width), lambda i: (i, 0))


def attend(qkv, cosine, sine, column, row, rows):
    total, wide = qkv.shape
    width = wide - LANES
    blocks = total // rows
    return pl.pallas_call(
        attention_forward,
        grid=(blocks,),
        in_specs=[
            by_rows(rows, wide),
            by_rows(rows, LANES),
            by_rows(rows, LANES),
            by_rows(rows, 1),
            pl.BlockSpec((1, 1, rows), lambda i: (i, 0, 0)),
        ],
        out_specs=[by_rows(rows, width), by_rows(rows, LANES), by_rows(rows, width), by_rows(rows, LANES)],
        out_shape=[
            jax.ShapeDtypeStruct((total, width), LOW),
            jax.ShapeDtypeStruct((total, LANES), LOW),
            jax.ShapeDtypeStruct((total, width), LOW),
            jax.ShapeDtypeStruct((total, LANES), WIDE),
        ],
        name="attend",
    )(qkv, cosine, sine, column, row)


def attend_back(query, keyval, log_sums, grads, cosine, sine, column, row, rows):
    total, width = query.shape
    blocks = total // rows
    return pl.pallas_call(
        attention_backward,
        grid=(blocks,),
        in_specs=[
            by_rows(rows, width),
            by_rows(rows, LANES),
            by_rows(rows, LANES),
            by_rows(rows, width),
            by_rows(rows, LANES),
            by_rows(rows, LANES),
            by_rows(rows, 1),
            pl.BlockSpec((1, 1, rows), lambda i: (i, 0, 0)),
        ],
        out_specs=by_rows(rows, width + LANES),
        out_shape=jax.ShapeDtypeStruct((total, width + LANES), LOW),
        name="attend_back",
    )(query, keyval, log_sums, grads, cosine, sine, column, row)


def tables(segment_block):
    rows = segment_block.shape[0]
    places = jnp.arange(rows, dtype=jnp.int32)
    same = segment_block[:, None] == segment_block[None, :]
    first_index = jnp.min(jnp.where(same, places[None, :], rows), axis=1)
    offsets = (places - first_index).astype(WIDE)
    half = HEAD_DIM // 2
    frequencies = jnp.exp(jnp.arange(half, dtype=WIDE) * (-2.0 * math.log(ROPE_BASE) / HEAD_DIM))
    angles = offsets[:, None] * frequencies[None, :]
    cosine, sine = jnp.cos(angles), jnp.sin(angles)
    return jnp.concatenate([cosine] * 4, axis=1), jnp.concatenate([sine] * 4, axis=1)


def mul(a, b):
    return jnp.dot(a, b, preferred_element_type=WIDE)


def on_device(
    tokens, segments, gain_attn, w_query, w_key, w_value, w_out, gain_mlp, w_gate, w_up, w_down, cotangent
):
    n = lax.axis_size("dp")
    rows, depth = tokens.shape
    part = depth // n
    me = lax.axis_index("dp")
    place = place_of(me, n)
    sources = [index_at((place + s) % n, n) for s in range(n)]
    offsets = [(place_of(jnp.int32(j), n) - place) % n for j in range(n)]

    def pick(value, starts):
        return jnp.concatenate(
            [lax.dynamic_slice(value, (0, at * part), (value.shape[0], part)) for at in starts], axis=1
        )

    attn_own = jnp.concatenate([w_query, w_key, w_value, w_out.T], axis=1).astype(LOW)
    gate_up_own = jnp.concatenate([w_gate, w_up], axis=1).astype(LOW)
    down_own = w_down.T.astype(LOW)
    heads_wide = w_query.shape[1]
    qkv_wide = heads_wide + w_key.shape[1] + w_value.shape[1]
    hidden_wide = w_gate.shape[1]

    attn_chunks = ring_gather(attn_own, n)
    gate_up_chunks = ring_gather(gate_up_own, n)
    down_chunks = ring_gather(down_own, n)
    gains = lax.all_gather(jnp.stack([gain_attn, gain_mlp]).astype(LOW), "dp", axis=1, tiled=True)
    gains = pick(gains, sources).astype(WIDE)
    gain_one, gain_two = gains[0:1], gains[1:2]

    own_tokens = pick(tokens, sources)
    own_grads = pick(cotangent, sources)
    token_all = jnp.concatenate(group_gather(own_tokens), axis=0)
    segment_blocks = jnp.stack(group_gather(segments))
    grads_all = jnp.concatenate(group_gather(own_grads), axis=0)
    cosine, sine = jax.vmap(tables)(segment_blocks)
    cosine, sine = cosine.reshape(-1, LANES), sine.reshape(-1, LANES)
    column, row = segment_blocks.reshape(-1, 1), segment_blocks[:, None, :]

    query_key_value = jnp.concatenate([c[:, :qkv_wide] for c in attn_chunks], axis=0)
    out_turned = jnp.concatenate([c[:, qkv_wide:] for c in attn_chunks], axis=0)
    gate = jnp.concatenate([c[:, :hidden_wide] for c in gate_up_chunks], axis=0)
    up = jnp.concatenate([c[:, hidden_wide:] for c in gate_up_chunks], axis=0)
    down_turned = jnp.concatenate(down_chunks, axis=0)

    wide_all = token_all.astype(WIDE)
    inv_all = lax.rsqrt(jnp.mean(wide_all * wide_all, axis=-1, keepdims=True) + EPSILON)
    normed = (wide_all * inv_all * gain_one).astype(LOW)
    qkv = mul(normed, query_key_value)
    query, keyval, mixed, log_sums = attend(qkv, cosine, sine, column, row, rows)
    own_wide = own_tokens.astype(WIDE)
    branch = dot_rows(mixed, out_turned).astype(LOW)
    hidden = own_wide + group_reduce(branch, rows)

    inv_second = lax.rsqrt(jnp.mean(hidden * hidden, axis=-1, keepdims=True) + EPSILON)
    unit_mlp = hidden * inv_second
    normed_mlp = jnp.concatenate(group_gather((unit_mlp * gain_two).astype(LOW)), axis=0)
    gate_proj = mul(normed_mlp, gate)
    upward = mul(normed_mlp, up)
    sigmoid = jax.nn.sigmoid(gate_proj)
    activation = (gate_proj * sigmoid * upward).astype(LOW)
    layer_own = hidden + group_reduce(dot_rows(activation, down_turned).astype(LOW), rows)

    def parts_of(value):
        return [value[s * part : (s + 1) * part] for s in range(n)]

    grad_down = ring_reduce(parts_of(dot_firsts(grads_all, activation).astype(LOW)), n)
    grad_act = mul(grads_all, down_turned)
    grad_gate = (grad_act * upward * sigmoid * (1.0 + gate_proj * (1.0 - sigmoid))).astype(LOW)
    grad_up = (grad_act * gate_proj * sigmoid).astype(LOW)
    grad_w_gate = ring_reduce(parts_of(dot_firsts(normed_mlp, grad_gate).astype(LOW)), n)
    grad_w_up = ring_reduce(parts_of(dot_firsts(normed_mlp, grad_up).astype(LOW)), n)
    grad_normed_mlp = group_reduce((dot_rows(grad_gate, gate) + dot_rows(grad_up, up)).astype(LOW), rows)
    gain_mlp_terms = jnp.sum(grad_normed_mlp * unit_mlp, axis=0, keepdims=True)
    scaled = grad_normed_mlp * gain_two
    grad_hidden = own_grads.astype(WIDE) + inv_second * (
        scaled - unit_mlp * jnp.mean(scaled * unit_mlp, axis=-1, keepdims=True)
    )

    grad_branch = jnp.concatenate(group_gather(grad_hidden.astype(LOW)), axis=0)
    grad_mixed = mul(grad_branch, out_turned).astype(LOW)
    grad_qkv = attend_back(query, keyval, log_sums, grad_mixed, cosine, sine, column, row, rows)
    attn_terms = jnp.concatenate(
        [dot_firsts(normed, grad_qkv).astype(LOW), dot_firsts(grad_branch, mixed).astype(LOW)], axis=1
    )
    grad_attn = ring_reduce(parts_of(attn_terms), n)
    grad_normed = group_reduce(dot_rows(grad_qkv, query_key_value).astype(LOW), rows)
    inv_first = lax.rsqrt(jnp.mean(own_wide * own_wide, axis=-1, keepdims=True) + EPSILON)
    unit_attn = own_wide * inv_first
    gain_attn_terms = jnp.sum(grad_normed * unit_attn, axis=0, keepdims=True)
    scaled = grad_normed * gain_one
    grad_inputs = grad_hidden + inv_first * (
        scaled - unit_attn * jnp.mean(scaled * unit_attn, axis=-1, keepdims=True)
    )

    gain_terms = pick(jnp.concatenate([gain_attn_terms, gain_mlp_terms], axis=0), offsets)
    bit = 1
    while bit < 4:
        gain_terms = gain_terms + lax.ppermute(gain_terms, "fsdp", [(i, i ^ bit) for i in range(4)])
        bit *= 2
    bit = 1
    while bit < n:
        gain_terms = gain_terms + lax.ppermute(gain_terms, "dp", [(i, i ^ bit) for i in range(n)])
        bit *= 2
    gain_own = lax.dynamic_slice(gain_terms, (0, me * part), (2, part))

    key_at, value_at = heads_wide, heads_wide + w_key.shape[1]
    return (
        pick(layer_own.astype(LOW), offsets),
        pick(grad_inputs.astype(LOW), offsets),
        gain_own[0],
        grad_attn[:, :key_at],
        grad_attn[:, key_at:value_at],
        grad_attn[:, value_at:qkv_wide],
        grad_attn[:, qkv_wide:].T,
        gain_own[1],
        grad_w_gate,
        grad_w_up,
        grad_down.T,
    )


def solution(mesh):
    placed = (
        P(("dp", "fsdp"), None),
        P(("dp", "fsdp")),
        P("dp"),
        P("dp", "fsdp"),
        P("dp", "fsdp"),
        P("dp", "fsdp"),
        P("fsdp", "dp"),
        P("dp"),
        P("dp", "fsdp"),
        P("dp", "fsdp"),
        P("fsdp", "dp"),
        P(("dp", "fsdp"), None),
    )
    return jax.shard_map(
        on_device,
        mesh=mesh,
        in_specs=placed,
        out_specs=(
            P(("dp", "fsdp"), None),
            P(("dp", "fsdp"), None),
            P("dp"),
            P("dp", "fsdp"),
            P("dp", "fsdp"),
            P("dp", "fsdp"),
            P("fsdp", "dp"),
            P("dp"),
            P("dp", "fsdp"),
            P("dp", "fsdp"),
            P("fsdp", "dp"),
        ),
        check_vma=False,
    )
```

time: 2400 us -> 700 us (0.29)
  waiting for transfers between devices: 1920 us -> 284 us
  blocking collectives: 135 us -> 49 us
  starting transfers between devices: 1.43 us -> 80 us
  matrix products: 189 us -> 129 us
  Pallas kernels: 0 us -> 29.4 us
  local copies, waits for them, and re-layouts: 88.9 us -> 64.9 us
    all_gather x12 -> x0, waiting for transfers between devices: 814 us -> none  [the longest x1 137 us: feed_weights(): lax.all_gather(rows_full[1], 'fsdp', axis=1, tiled=True)]
    reduce_scatter x12 -> x0, waiting for transfers between devices: 776 us -> none  [the longest x1 161 us: reduce_feed(): lax.psum_scatter(grad_down.astype(jnp.bfloat16), 'fsdp', scatter_dimensio...]
    unnamed x28 -> x0, waiting for transfers between devices: 333 us -> none
    ppermute x0 -> x88, waiting for transfers between devices: none -> 284 us  [the longest x12 65.4 us: ring_reduce(): ahead = lax.ppermute(ahead, 'dp', forward)]
    ppermute x0 -> x88, starting transfers between devices: none -> 80 us  [the longest x12 14.8 us: ring_reduce(): behind = lax.ppermute(behind, 'dp', backward)]
    dot_general x27 -> x15, matrix products: 189 us -> 129 us  [the longest x5 54 us: mul(): return jnp.dot(a, b, preferred_element_type=WIDE)]
    all_gather x4 -> x1, blocking collectives: 103 us -> 49 us  [on_device(): lax.all_gather(jnp.stack([gain_attn, gain_mlp]).astype(LOW), 'dp', axis=1...]
    unnamed x72 -> x181, local copies, waits for them, and re-layouts: 86.6 us -> 48.8 us
  transfers between devices with their start and end apart: 26 -> 88, of which waited for: 21 -> 34; matrix products, arithmetic and copies ran while one was open for 10% -> 28% of each run, Pallas kernels for 0% -> 4%
where the time goes in v1:
time: 700 us; the launch traced here: 693 us
  waiting for transfers between devices  284 us (41%)
  matrix products  129 us (18%)
  starting transfers between devices  80 us (11%)
  local copies, waits for them, and re-layouts  64.9 us (9%)
  other arithmetic  54.3 us (8%)
  blocking collectives  49 us (7%)
  Pallas kernels  29.4 us (4%)
    ppermute x12, waiting for transfers between devices, ring_reduce(): ahead = lax.ppermute(ahead, 'dp', forward)  65.4 us
    dot_general x5, matrix products, mul(): return jnp.dot(a, b, preferred_element_type=WIDE)  54 us
    ppermute x9, waiting for transfers between devices, swap_pair(): return lax.ppermute(value, 'fsdp', [(i, i ^ 2) for i in range(4)])  53.7 us
    all_gather x1, blocking collectives, on_device(): lax.all_gather(jnp.stack([gain_attn, gain_mlp]).astype(LOW), 'dp', axis=1...  49 us
    unnamed x181, local copies, waits for them, and re-layouts  48.8 us
    ppermute x9, waiting for transfers between devices, ring_gather(): behind = lax.ppermute(behind, 'dp', backward)  44.9 us
    dot_general x5, matrix products, dot_rows(): lax.dot_general(a, b, (((1,), (1,)), ((), ())), preferred_element_type=WIDE)  39.9 us
    dot_general x5, matrix products, dot_firsts(): lax.dot_general(a, b, (((0,), (0,)), ((), ())), preferred_element_type=WIDE)  35.6 us
  transfers between devices with their start and end apart: 88, of which 34 were waited for; matrix products, arithmetic and copies ran while one was open for 28% of the time, Pallas kernels for 4%

profile of v1, /device:TPU:0, one launch (start us, length us, event | category | flops | bytes accessed | tf_op | source)
XLA Modules:
  0.0 693.3 jit_solution(16359351354997345728)
XLA Ops:
  14.8 49.0 %all_gather.3 = bf16[2,2048]{1,0:T(2,128)(2,1)S(1)} all-gather(bf16[2,256]{1,0:T(2,128)(2,1)S(1)} %pad_maximum_fusion.21), channel_id=1, replica_groups=mesh['dp'=8,'fsdp'=4] {'dp'}, dimensions={1}, use_global_device_ids=true | all-gather | bytes 9216 | tf_op jit(solution)/shard_map/all_gather | solution.py:292
  107.2 9.7 %collective-permute-done.4 = bf16[256,1152]{0,1:T(8,128)(2,1)S(1)} collective-permute-done((bf16[256,1152]{0,1:T(8,128)(2,1)}, bf16[256,1152]{0,1:T(8,128)(2,1)S(1)}, u32[]{:S(2)}, u32[]{:S(2)}) %collective-permute-start.4) | collective-permute-done | bytes 589856 | tf_op jit(solution)/shard_map/ppermute | solution.py:44
  124.7 11.6 %collective-permute-done.29 = bf16[256,1408]{0,1:T(8,128)(2,1)} collective-permute-done((bf16[256,1408]{0,1:T(8,128)(2,1)}, bf16[256,1408]{0,1:T(8,128)(2,1)}, u32[]{:S(2)}, u32[]{:S(2)}) %collective-permute-start.29) | collective-permute-done | bytes 720928 | tf_op jit(solution)/shard_map/ppermute | solution.py:44
  139.7 7.5 %collective-permute-done.5 = bf16[256,1152]{0,1:T(8,128)(2,1)S(1)} collective-permute-done((bf16[256,1152]{0,1:T(8,128)(2,1)S(1)}, bf16[256,1152]{0,1:T(8,128)(2,1)S(1)}, u32[]{:S(2)}, u32[]{:S(2)}) %collective-permute-start.5) | collective-permute-done | bytes 589856 | tf_op jit(solution)/shard_map/ppermute | solution.py:44
  149.7 7.8 %collective-permute-done.9 = bf16[128,1152]{0,1:T(8,128)(2,1)S(1)} collective-permute-done((bf16[128,1152]{0,1:T(8,128)(2,1)S(1)}, bf16[128,1152]{0,1:T(8,128)(2,1)S(1)}, u32[]{:S(2)}, u32[]{:S(2)}) %collective-permute-start.9) | collective-permute-done | bytes 294944 | tf_op jit(solution)/shard_map/ppermute | solution.py:47
  165.3 17.9 %collective-permute-done.40 = bf16[256,2048]{1,0:T(8,128)(2,1)} collective-permute-done((bf16[256,2048]{1,0:T(8,128)(2,1)S(1)}, bf16[256,2048]{1,0:T(8,128)(2,1)}, u32[]{:S(2)}, u32[]{:S(2)}) %collective-permute-start.40) | collective-permute-done | bytes 1048608 | tf_op jit(solution)/shard_map/ppermute | solution.py:77
  186.6 8.2 %fusion.14.qkv_ref = f32[1024,640]{1,0:T(8,128)} fusion(bf16[2048,640]{0,1:T(8,128)(2,1)S(1)} %slice_dynamic-update-slice_fusion.14, f32[2048]{0:T(1024)S(1)} %bitcast.71, f32[1024]{0:T(1024)S(1)} %add_rsqrt_fusion, bf16[256,2048]{1,0:T(8,128)(2,1)S(1)} %collective-permute-done.2, bf16[256,2048]{1,0:T(8,128)(2,1)S(1)} %collective-permute-done.1, ...), kind=kOutput, calls=%fused_computation.68 | convolution fusion | flops 2707423232 | bytes 9449472 | tf_op jit(solution)/shard_map/dot_general | solution.py:263
  194.8 12.2 %attend.1 = (bf16[1024,512]{1,0:T(8,128)(2,1)}, bf16[1024,128]{1,0:T(8,128)(2,1)}, bf16[1024,512]{1,0:T(8,128)(2,1)}, f32[1024,128]{1,0:T(8,128)}) custom-call(f32[1024,640]{1,0:T(8,128)} %fusion.14.qkv_ref, f32[1024,128]{1,0:T(8,128)} %get-tuple-element.124.cos_ref, f32[1024,128]{1,0:T(8,128)} %get-tuple-element.125.sin_ref, s32[1024,1]{1,0:T(8,128)} %bitcast.48, ...), custom_call_target="tpu_custom_call" | custom-call | tf_op jit(solution)/shard_map/attend/pallas_call | solution.py:206
  231.0 12.6 %fusion.16 = f32[1024,1408]{1,0:T(8,128)} fusion(bf16[2048,1408]{0,1:T(8,128)(2,1)} %constant_dynamic-update-slice_fusion.23, bf16[256,2048]{1,0:T(8,128)(2,1)} %collective-permute-done.41, bf16[256,2048]{1,0:T(8,128)(2,1)} %collective-permute-done.40, bf16[256,2048]{1,0:T(8,128)(2,1)} %collective-permute-done.39, ...), kind=kOutput, calls=%fused_computation.110 | convolution fusion | flops 5922357248 | bytes 15728640 | tf_op jit(solution)/shard_map/dot_general | solution.py:263
  243.6 13.0 %collective-permute-done.21 = bf16[256,2816]{1,0:T(8,128)(2,1)S(1)} collective-permute-done((bf16[256,2816]{1,0:T(8,128)(2,1)}, bf16[256,2816]{1,0:T(8,128)(2,1)S(1)}, u32[]{:S(2)}, u32[]{:S(2)}) %collective-permute-start.21) | collective-permute-done | bytes 1441824 | tf_op jit(solution)/shard_map/ppermute | solution.py:44
  262.7 28.5 %collective-permute-done.25 = bf16[256,2816]{1,0:T(8,128)(2,1)S(1)} collective-permute-done((bf16[256,2816]{1,0:T(8,128)(2,1)S(1)}, bf16[256,2816]{1,0:T(8,128)(2,1)S(1)}, u32[]{:S(2)}, u32[]{:S(2)}) %collective-permute-start.25) | collective-permute-done | bytes 1441824 | tf_op jit(solution)/shard_map/ppermute | solution.py:43
  295.4 12.5 %collective-permute-done.26 = bf16[128,2816]{1,0:T(8,128)(2,1)S(1)} collective-permute-done((bf16[128,2816]{1,0:T(8,128)(2,1)S(1)}, bf16[128,2816]{1,0:T(8,128)(2,1)S(1)}, u32[]{:S(2)}, u32[]{:S(2)}) %collective-permute-start.26) | collective-permute-done | bytes 720928 | tf_op jit(solution)/shard_map/ppermute | solution.py:47
  314.6 11.4 %fusion.47 = f32[1024,1408]{1,0:T(8,128)} fusion(bf16[2048,1408]{1,0:T(8,128)(2,1)S(1)} %get-tuple-element.96, bf16[256,2048]{1,0:T(8,128)(2,1)S(1)} %collective-permute-done.19, bf16[256,2048]{1,0:T(8,128)(2,1)S(1)} %collective-permute-done.18, bf16[256,2048]{1,0:T(8,128)(2,1)S(1)} %collective-permute-done.17, ...), kind=kOutput, calls=%fused_computation.269 | convolution fusion | flops 5922357248 | bytes 15728640 | tf_op jit(solution)/shard_map/dot_general | solution.py:263
  326.0 15.7 %multiply_convert_fusion.1 = (bf16[1024,1408]{1,0:T(8,128)(2,1)}, bf16[1024,1408]{1,0:T(8,128)(2,1)}, bf16[1024,1408]{1,0:T(8,128)(2,1)}) fusion(f32[1024,1408]{1,0:T(8,128)} %fusion.16, f32[1024,1408]{1,0:T(8,128)} %fusion.47, bf16[2048,1408]{1,0:T(8,128)(2,1)S(1)} %copy-done.24, bf16[256,2048]{1,0:T(8,128)(2,1)S(1)} %collective-permute-done.19, ...), kind=kOutput, calls=%fused_computation.30 | convolution fusion | flops 5945425920 | bytes 30146560 | tf_op jit(solution)/shard_map/dot_general | solution.py:263
  341.7 9.7 %convolution_convert_fusion.4 = bf16[1024,2048]{1,0:T(8,128)(2,1)S(1)} fusion(bf16[1024,1408]{1,0:T(8,128)(2,1)} %get-tuple-element.58, bf16[2048,1408]{0,1:T(8,128)(2,1)} %constant_dynamic-update-slice_fusion.23), kind=kOutput, calls=%fused_computation.38 | convolution fusion | flops 5907677184 | bytes 12845056 | tf_op jit(solution)/shard_map/dot_general | solution.py:113
  351.5 8.7 %convolution_convert_fusion = bf16[2048,1408]{1,0:T(8,128)(2,1)S(1)} fusion(bf16[1024,1408]{1,0:T(8,128)(2,1)S(1)} %copy-done.54, bf16[256,2048]{1,0:T(8,128)(2,1)} %collective-permute-done.41, bf16[256,2048]{1,0:T(8,128)(2,1)} %collective-permute-done.40, bf16[256,2048]{1,0:T(8,128)(2,1)} %collective-permute-done.39, bf16[256,2048]{1,0:T(8,128)(2,1)S(1)} %copy-done.10), kind=kOutput, calls=%fused_computation.26 | convolution fusion | flops 5925240832 | bytes 12845056 | tf_op jit(solution)/shard_map/dot_general | solution.py:117
  360.8 11.6 %fusion.57 = f32[1024,2048]{1,0:T(8,128)} fusion(bf16[1024,1408]{1,0:T(8,128)(2,1)} %get-tuple-element.59, bf16[2048,1408]{1,0:T(8,128)(2,1)S(1)} %bitcast.70), kind=kOutput, calls=%fused_computation.279 | convolution fusion | flops 5905580032 | bytes 17039360 | tf_op jit(solution)/shard_map/dot_general | solution.py:113
  372.4 9.0 %convolution_convert_fusion.1 = bf16[2048,1408]{1,0:T(8,128)(2,1)S(1)} fusion(bf16[1024,1408]{1,0:T(8,128)(2,1)} %get-tuple-element.59, bf16[256,2048]{1,0:T(8,128)(2,1)} %copy-done.49, bf16[256,2048]{1,0:T(8,128)(2,1)S(1)} %copy-done.42, bf16[256,2048]{1,0:T(8,128)(2,1)S(1)} %copy-done.44, bf16[256,2048]{1,0:T(8,128)(2,1)S(1)} %multiply_convert_fusion.3), kind=kOutput, calls=%fused_computation.27 | convolution fusion | flops 5925240832 | bytes 12845056 | tf_op jit(solution)/shard_map/dot_general | solution.py:117
  383.0 9.5 %convolution_convert_fusion.2 = bf16[2048,1408]{1,0:T(8,128)(2,1)S(1)} fusion(bf16[1024,1408]{1,0:T(8,128)(2,1)} %get-tuple-element.57, bf16[256,2048]{1,0:T(8,128)(2,1)} %copy-done.49, bf16[256,2048]{1,0:T(8,128)(2,1)S(1)} %copy-done.42, bf16[256,2048]{1,0:T(8,128)(2,1)S(1)} %copy-done.44, bf16[256,2048]{1,0:T(8,128)(2,1)S(1)} %multiply_convert_fusion.3), kind=kOutput, calls=%fused_computation.28 | convolution fusion | flops 5925240832 | bytes 12845056 | tf_op jit(solution)/shard_map/dot_general | solution.py:117
  396.3 10.8 %add_convert_fusion = bf16[1024,2048]{1,0:T(8,128)(2,1)S(1)} fusion(f32[1024,2048]{1,0:T(8,128)} %fusion.57, bf16[1024,1408]{1,0:T(8,128)(2,1)} %get-tuple-element.57, bf16[2048,1408]{1,0:T(8,128)(2,1)} %get-tuple-element.95), kind=kOutput, calls=%fused_computation.25 | convolution fusion | flops 5909774336 | bytes 21233664 | tf_op jit(solution)/shard_map/dot_general | solution.py:113
  411.6 8.1 %collective-permute-done.84 = bf16[128,1408]{1,0:T(8,128)(2,1)S(1)} collective-permute-done((bf16[128,1408]{1,0:T(8,128)(2,1)S(1)}, bf16[128,1408]{1,0:T(8,128)(2,1)S(1)}, u32[]{:S(2)}, u32[]{:S(2)}) %collective-permute-start.84) | collective-permute-done | bytes 360480 | tf_op jit(solution)/shard_map/ppermute | solution.py:58
  422.3 7.2 %collective-permute-done.76 = bf16[128,1408]{1,0:T(8,128)(2,1)S(1)} collective-permute-done((bf16[128,1408]{1,0:T(8,128)(2,1)S(1)}, bf16[128,1408]{1,0:T(8,128)(2,1)S(1)}, u32[]{:S(2)}, u32[]{:S(2)}) %collective-permute-start.76) | collective-permute-done | bytes 360480 | tf_op jit(solution)/shard_map/ppermute | solution.py:58
  445.7 11.9 %collective-permute-done.73 = bf16[256,1408]{1,0:T(8,128)(2,1)S(1)} collective-permute-done((bf16[256,1408]{1,0:T(8,128)(2,1)S(1)}, bf16[256,1408]{1,0:T(8,128)(2,1)S(1)}, u32[]{:S(2)}, u32[]{:S(2)}) %collective-permute-start.73) | collective-permute-done | bytes 720928 | tf_op jit(solution)/shard_map/ppermute | solution.py:67
  459.1 14.0 %collective-permute-done.65 = bf16[256,1408]{1,0:T(8,128)(2,1)S(1)} collective-permute-done((bf16[256,1408]{1,0:T(8,128)(2,1)S(1)}, bf16[256,1408]{1,0:T(8,128)(2,1)S(1)}, u32[]{:S(2)}, u32[]{:S(2)}) %collective-permute-start.65) | collective-permute-done | bytes 720928 | tf_op jit(solution)/shard_map/ppermute | solution.py:67
  475.2 13.3 %collective-permute-done.82 = bf16[256,1408]{1,0:T(8,128)(2,1)S(1)} collective-permute-done((bf16[256,1408]{1,0:T(8,128)(2,1)S(1)}, bf16[256,1408]{1,0:T(8,128)(2,1)S(1)}, u32[]{:S(2)}, u32[]{:S(2)}) %collective-permute-start.82) | collective-permute-done | bytes 720928 | tf_op jit(solution)/shard_map/ppermute | solution.py:67
  492.5 11.4 %collective-permute-done.74 = bf16[256,1408]{1,0:T(8,128)(2,1)S(1)} collective-permute-done((bf16[256,1408]{1,0:T(8,128)(2,1)S(1)}, bf16[256,1408]{1,0:T(8,128)(2,1)S(1)}, u32[]{:S(2)}, u32[]{:S(2)}) %collective-permute-start.74) | collective-permute-done | bytes 720928 | tf_op jit(solution)/shard_map/ppermute | solution.py:67
  507.2 9.2 %collective-permute-done.66 = bf16[256,1408]{1,0:T(8,128)(2,1)S(1)} collective-permute-done((bf16[256,1408]{1,0:T(8,128)(2,1)S(1)}, bf16[256,1408]{1,0:T(8,128)(2,1)S(1)}, u32[]{:S(2)}, u32[]{:S(2)}) %collective-permute-start.66) | collective-permute-done | bytes 720928 | tf_op jit(solution)/shard_map/ppermute | solution.py:67
  519.8 10.2 %collective-permute-done.44 = bf16[256,2048]{1,0:T(8,128)(2,1)S(1)} collective-permute-done((bf16[256,2048]{1,0:T(8,128)(2,1)S(1)}, bf16[256,2048]{1,0:T(8,128)(2,1)S(1)}, u32[]{:S(2)}, u32[]{:S(2)}) %collective-permute-start.44) | collective-permute-done | bytes 1048608 | tf_op jit(solution)/shard_map/ppermute | solution.py:77
  533.0 12.8 %collective-permute-done.38 = bf16[256,2048]{1,0:T(8,128)(2,1)} collective-permute-done((bf16[256,2048]{1,0:T(8,128)(2,1)S(1)}, bf16[256,2048]{1,0:T(8,128)(2,1)}, u32[]{:S(2)}, u32[]{:S(2)}) %collective-permute-start.38) | collective-permute-done | bytes 1048608 | tf_op jit(solution)/shard_map/ppermute | solution.py:77
  556.4 12.7 %collective-permute-done.46 = bf16[256,2048]{1,0:T(8,128)(2,1)S(1)} collective-permute-done((bf16[256,2048]{1,0:T(8,128)(2,1)S(1)}, bf16[256,2048]{1,0:T(8,128)(2,1)S(1)}, u32[]{:S(2)}, u32[]{:S(2)}) %collective-permute-start.46) | collective-permute-done | bytes 1048608 | tf_op jit(solution)/shard_map/ppermute | solution.py:77
  582.2 17.2 %attend_back.1 = bf16[1024,640]{1,0:T(8,128)(2,1)} custom-call(bf16[1024,512]{1,0:T(8,128)(2,1)} %get-tuple-element.16.q_ref, bf16[1024,128]{1,0:T(8,128)(2,1)} %get-tuple-element.17.kv_ref, f32[1024,128]{1,0:T(8,128)} %get-tuple-element.18.lse_ref, bf16[1024,512]{1,0:T(8,128)(2,1)} %convolution_convert_fusion.8.do_ref, ...), custom_call_target="tpu_custom_call" | custom-call | tf_op jit(solution)/shard_map/attend_back/pallas_call | solution.py:230
  648.1 11.1 %collective-permute-done.71 = bf16[256,1408]{1,0:T(8,128)(2,1)S(1)} collective-permute-done((bf16[256,1408]{1,0:T(8,128)(2,1)S(1)}, bf16[256,1408]{1,0:T(8,128)(2,1)S(1)}, u32[]{:S(2)}, u32[]{:S(2)}) %collective-permute-start.71) | collective-permute-done | bytes 720928 | tf_op jit(solution)/shard_map/ppermute | solution.py:68
  (453 shorter events, 275.0 us)
Async XLA Ops:
  5.1 115.7 %collective-permute-start.20 = (bf16[256,2816]{1,0:T(8,128)(2,1)}, bf16[256,2816]{1,0:T(8,128)(2,1)}, u32[]{:S(2)}, u32[]{:S(2)}) collective-permute-start(bf16[256,2816]{1,0:T(8,128)(2,1)} %pad_maximum_fusion.4), channel_id=1, source_target_pairs={{8,0},{16,8},{24,16},{28,24},{20,28},{12,20},{4,12},{0,4},{9,1},{1... | collective-permute-start | bytes 4325384 | tf_op jit(solution)/shard_map/ppermute | solution.py:44
  8.0 214.4 %collective-permute-start.23 = (bf16[256,2816]{1,0:T(8,128)(2,1)}, bf16[256,2816]{1,0:T(8,128)(2,1)}, u32[]{:S(2)}, u32[]{:S(2)}) collective-permute-start(bf16[256,2816]{1,0:T(8,128)(2,1)} %pad_maximum_fusion.4), channel_id=1, source_target_pairs={{0,8},{8,16},{16,24},{24,28},{28,20},{20,12},{12,4},{4,0},{1,9},{9... | collective-permute-start | bytes 4325384 | tf_op jit(solution)/shard_map/ppermute | solution.py:43
  8.1 76.4 %collective-permute-start.12 = (s32[256]{0:T(256)}, s32[256]{0:T(256)}, u32[]{:S(2)}, u32[]{:S(2)}) collective-permute-start(s32[256]{0:T(256)} %param.13), channel_id=1, source_target_pairs={{0,2},{1,3},{2,0},{3,1},{4,6},{5,7},{6,4},{7,5},{8,10},{9,11},{10,... | collective-permute-start | bytes 3080 | tf_op jit(solution)/shard_map/ppermute | solution.py:77
  10.1 74.4 %collective-permute-start.11 = (s32[256]{0:T(256)}, s32[256]{0:T(256)}, u32[]{:S(2)}, u32[]{:S(2)}) collective-permute-start(s32[256]{0:T(256)} %param.13), channel_id=1, source_target_pairs={{0,1},{1,0},{2,3},{3,2},{4,5},{5,4},{6,7},{7,6},{8,9},{9,8},{10,11... | collective-permute-start | bytes 3080 | tf_op jit(solution)/shard_map/ppermute | solution.py:73
  11.9 82.7 %collective-permute-start.3 = (bf16[256,1152]{0,1:T(8,128)(2,1)}, bf16[256,1152]{0,1:T(8,128)(2,1)}, u32[]{:S(2)}, u32[]{:S(2)}) collective-permute-start(bf16[256,1152]{0,1:T(8,128)(2,1)} %pad_maximum_fusion.15), channel_id=1, source_target_pairs={{8,0},{16,8},{24,16},{28,24},{20,28},{12,20},{4,12},{0,4},{9,1},{1... | collective-permute-start | bytes 1769480 | tf_op jit(solution)/shard_map/ppermute | solution.py:44
  100.6 58.6 %collective-permute-start.1 = (bf16[256,2048]{1,0:T(8,128)(2,1)S(1)}, bf16[256,2048]{1,0:T(8,128)(2,1)S(1)}, u32[]{:S(2)}, u32[]{:S(2)}) collective-permute-start(bf16[256,2048]{1,0:T(8,128)(2,1)S(1)} %constant_dynamic-update-slice_fusion), channel_id=1, source_target_pairs={{0,2},{1,3},{2,0},{3,1},{4,6},{5,7},{6,4},{7,5},{8,10},{9,11},{10,... | collective-permute-start | bytes 3145736 | tf_op jit(solution)/shard_map/ppermute | solution.py:77
  164.8 64.6 %collective-permute-start.39 = (bf16[256,2048]{1,0:T(8,128)(2,1)S(1)}, bf16[256,2048]{1,0:T(8,128)(2,1)}, u32[]{:S(2)}, u32[]{:S(2)}) collective-permute-start(bf16[256,2048]{1,0:T(8,128)(2,1)S(1)} %constant_dynamic-update-slice_fusion.40), channel_id=1, source_target_pairs={{0,1},{1,0},{2,3},{3,2},{4,5},{5,4},{6,7},{7,6},{8,9},{9,8},{10,11... | collective-permute-start | bytes 3145736 | tf_op jit(solution)/shard_map/ppermute | solution.py:73
  183.3 47.7 %collective-permute-start.41 = (bf16[256,2048]{1,0:T(8,128)(2,1)}, bf16[256,2048]{1,0:T(8,128)(2,1)}, u32[]{:S(2)}, u32[]{:S(2)}) collective-permute-start(bf16[256,2048]{1,0:T(8,128)(2,1)} %collective-permute-done.40), channel_id=1, source_target_pairs={{0,1},{1,0},{2,3},{3,2},{4,5},{5,4},{6,7},{7,6},{8,9},{9,8},{10,11... | collective-permute-start | bytes 3145736 | tf_op jit(solution)/shard_map/ppermute | solution.py:73
  222.4 34.2 %collective-permute-start.21 = (bf16[256,2816]{1,0:T(8,128)(2,1)}, bf16[256,2816]{1,0:T(8,128)(2,1)S(1)}, u32[]{:S(2)}, u32[]{:S(2)}) collective-permute-start(bf16[256,2816]{1,0:T(8,128)(2,1)} %collective-permute-done.20), channel_id=1, source_target_pairs={{8,0},{16,8},{24,16},{28,24},{20,28},{12,20},{4,12},{0,4},{9,1},{1... | collective-permute-start | bytes 4325384 | tf_op jit(solution)/shard_map/ppermute | solution.py:44
  224.0 34.2 %collective-permute-start.24 = (bf16[256,2816]{1,0:T(8,128)(2,1)}, bf16[256,2816]{1,0:T(8,128)(2,1)S(1)}, u32[]{:S(2)}, u32[]{:S(2)}) collective-permute-start(bf16[256,2816]{1,0:T(8,128)(2,1)} %collective-permute-done.23), channel_id=1, source_target_pairs={{0,8},{8,16},{16,24},{24,28},{28,20},{20,12},{12,4},{4,0},{1,9},{9... | collective-permute-start | bytes 4325384 | tf_op jit(solution)/shard_map/ppermute | solution.py:43
  256.6 35.6 %collective-permute-start.22 = (bf16[256,2816]{1,0:T(8,128)(2,1)S(1)}, bf16[256,2816]{1,0:T(8,128)(2,1)S(1)}, u32[]{:S(2)}, u32[]{:S(2)}) collective-permute-start(bf16[256,2816]{1,0:T(8,128)(2,1)S(1)} %collective-permute-done.21), channel_id=1, source_target_pairs={{8,0},{16,8},{24,16},{28,24},{20,28},{12,20},{4,12},{0,4},{9,1},{1... | collective-permute-start | bytes 4325384 | tf_op jit(solution)/shard_map/ppermute | solution.py:44
  258.3 32.9 %collective-permute-start.25 = (bf16[256,2816]{1,0:T(8,128)(2,1)S(1)}, bf16[256,2816]{1,0:T(8,128)(2,1)S(1)}, u32[]{:S(2)}, u32[]{:S(2)}) collective-permute-start(bf16[256,2816]{1,0:T(8,128)(2,1)S(1)} %collective-permute-done.24), channel_id=1, source_target_pairs={{0,8},{8,16},{16,24},{24,28},{28,20},{20,12},{12,4},{4,0},{1,9},{9... | collective-permute-start | bytes 4325384 | tf_op jit(solution)/shard_map/ppermute | solution.py:43
  261.1 50.0 %collective-permute-start.18 = (bf16[256,2048]{1,0:T(8,128)(2,1)S(1)}, bf16[256,2048]{1,0:T(8,128)(2,1)S(1)}, u32[]{:S(2)}, u32[]{:S(2)}) collective-permute-start(bf16[256,2048]{1,0:T(8,128)(2,1)S(1)} %multiply_convert_fusion.3), channel_id=1, source_target_pairs={{0,2},{1,3},{2,0},{3,1},{4,6},{5,7},{6,4},{7,5},{8,10},{9,11},{10,... | collective-permute-start | bytes 3145736 | tf_op jit(solution)/shard_map/ppermute | solution.py:77
  262.7 51.8 %collective-permute-start.17 = (bf16[256,2048]{1,0:T(8,128)(2,1)S(1)}, bf16[256,2048]{1,0:T(8,128)(2,1)S(1)}, u32[]{:S(2)}, u32[]{:S(2)}) collective-permute-start(bf16[256,2048]{1,0:T(8,128)(2,1)S(1)} %multiply_convert_fusion.3), channel_id=1, source_target_pairs={{0,1},{1,0},{2,3},{3,2},{4,5},{5,4},{6,7},{7,6},{8,9},{9,8},{10,11... | collective-permute-start | bytes 3145736 | tf_op jit(solution)/shard_map/ppermute | solution.py:73
  360.2 47.0 %collective-permute-start.80 = (bf16[128,1408]{1,0:T(8,128)(2,1)S(1)}, bf16[128,1408]{1,0:T(8,128)(2,1)S(1)}, u32[]{:S(2)}, u32[]{:S(2)}) collective-permute-start(bf16[128,1408]{1,0:T(8,128)(2,1)S(1)} %slice.559), channel_id=1, source_target_pairs={{0,8},{8,16},{16,24},{24,28},{28,20},{20,12},{12,4},{4,0},{1,9},{9... | collective-permute-start | bytes 1081352 | tf_op jit(solution)/shard_map/ppermute | solution.py:57
  395.8 44.4 %collective-permute-start.37 = (bf16[256,2048]{1,0:T(8,128)(2,1)}, bf16[256,2048]{1,0:T(8,128)(2,1)}, u32[]{:S(2)}, u32[]{:S(2)}) collective-permute-start(bf16[256,2048]{1,0:T(8,128)(2,1)} %get-tuple-element.91), channel_id=1, source_target_pairs={{0,1},{1,0},{2,3},{3,2},{4,5},{5,4},{6,7},{7,6},{8,9},{9,8},{10,11... | collective-permute-start | bytes 3145736 | tf_op jit(solution)/shard_map/ppermute | solution.py:73
  396.0 136.9 %collective-permute-start.36 = (bf16[256,2048]{1,0:T(8,128)(2,1)}, bf16[256,2048]{1,0:T(8,128)(2,1)}, u32[]{:S(2)}, u32[]{:S(2)}) collective-permute-start(bf16[256,2048]{1,0:T(8,128)(2,1)} %get-tuple-element.90), channel_id=1, source_target_pairs={{0,1},{1,0},{2,3},{3,2},{4,5},{5,4},{6,7},{7,6},{8,9},{9,8},{10,11... | collective-permute-start | bytes 3145736 | tf_op jit(solution)/shard_map/ppermute | solution.py:73
  407.3 35.2 %collective-permute-start.43 = (bf16[256,2048]{1,0:T(8,128)(2,1)S(1)}, bf16[256,2048]{1,0:T(8,128)(2,1)S(1)}, u32[]{:S(2)}, u32[]{:S(2)}) collective-permute-start(bf16[256,2048]{1,0:T(8,128)(2,1)S(1)} %get-tuple-element.89), channel_id=1, source_target_pairs={{0,1},{1,0},{2,3},{3,2},{4,5},{5,4},{6,7},{7,6},{8,9},{9,8},{10,11... | collective-permute-start | bytes 3145736 | tf_op jit(solution)/shard_map/ppermute | solution.py:73
  410.7 33.1 %collective-permute-start.81 = (bf16[256,1408]{1,0:T(8,128)(2,1)S(1)}, bf16[256,1408]{1,0:T(8,128)(2,1)S(1)}, u32[]{:S(2)}, u32[]{:S(2)}) collective-permute-start(bf16[256,1408]{1,0:T(8,128)(2,1)S(1)} %pad_maximum_fusion.9), channel_id=1, source_target_pairs={{0,8},{8,16},{16,24},{24,28},{28,20},{20,12},{12,4},{4,0},{1,9},{9... | collective-permute-start | bytes 2162696 | tf_op jit(solution)/shard_map/ppermute | solution.py:67
  440.1 32.9 %collective-permute-start.65 = (bf16[256,1408]{1,0:T(8,128)(2,1)S(1)}, bf16[256,1408]{1,0:T(8,128)(2,1)S(1)}, u32[]{:S(2)}, u32[]{:S(2)}) collective-permute-start(bf16[256,1408]{1,0:T(8,128)(2,1)S(1)} %pad_maximum_fusion.5), channel_id=1, source_target_pairs={{0,8},{8,16},{16,24},{24,28},{28,20},{20,12},{12,4},{4,0},{1,9},{9... | collective-permute-start | bytes 2162696 | tf_op jit(solution)/shard_map/ppermute | solution.py:67
  442.5 32.0 %collective-permute-start.85 = (bf16[256,1408]{1,0:T(8,128)(2,1)S(1)}, bf16[256,1408]{1,0:T(8,128)(2,1)S(1)}, u32[]{:S(2)}, u32[]{:S(2)}) collective-permute-start(bf16[256,1408]{1,0:T(8,128)(2,1)S(1)} %pad_maximum_fusion.10), channel_id=1, source_target_pairs={{8,0},{16,8},{24,16},{28,24},{20,28},{12,20},{4,12},{0,4},{9,1},{1... | collective-permute-start | bytes 2162696 | tf_op jit(solution)/shard_map/ppermute | solution.py:68
  443.8 48.7 %collective-permute-start.77 = (bf16[256,1408]{1,0:T(8,128)(2,1)S(1)}, bf16[256,1408]{1,0:T(8,128)(2,1)S(1)}, u32[]{:S(2)}, u32[]{:S(2)}) collective-permute-start(bf16[256,1408]{1,0:T(8,128)(2,1)S(1)} %pad_maximum_fusion.8), channel_id=1, source_target_pairs={{8,0},{16,8},{24,16},{28,24},{20,28},{12,20},{4,12},{0,4},{9,1},{1... | collective-permute-start | bytes 2162696 | tf_op jit(solution)/shard_map/ppermute | solution.py:68
  473.0 30.9 %collective-permute-start.74 = (bf16[256,1408]{1,0:T(8,128)(2,1)S(1)}, bf16[256,1408]{1,0:T(8,128)(2,1)S(1)}, u32[]{:S(2)}, u32[]{:S(2)}) collective-permute-start(bf16[256,1408]{1,0:T(8,128)(2,1)S(1)} %slice_add_fusion.10), channel_id=1, source_target_pairs={{0,8},{8,16},{16,24},{24,28},{28,20},{20,12},{12,4},{4,0},{1,9},{9... | collective-permute-start | bytes 2162696 | tf_op jit(solution)/shard_map/ppermute | solution.py:67
  474.5 32.2 %collective-permute-start.69 = (bf16[256,1408]{1,0:T(8,128)(2,1)S(1)}, bf16[256,1408]{1,0:T(8,128)(2,1)S(1)}, u32[]{:S(2)}, u32[]{:S(2)}) collective-permute-start(bf16[256,1408]{1,0:T(8,128)(2,1)S(1)} %pad_maximum_fusion.6), channel_id=1, source_target_pairs={{8,0},{16,8},{24,16},{28,24},{20,28},{12,20},{4,12},{0,4},{9,1},{1... | collective-permute-start | bytes 2162696 | tf_op jit(solution)/shard_map/ppermute | solution.py:68
  506.7 39.1 %collective-permute-start.38 = (bf16[256,2048]{1,0:T(8,128)(2,1)S(1)}, bf16[256,2048]{1,0:T(8,128)(2,1)}, u32[]{:S(2)}, u32[]{:S(2)}) collective-permute-start(bf16[256,2048]{1,0:T(8,128)(2,1)S(1)} %slice_add_fusion.2), channel_id=1, source_target_pairs={{0,2},{1,3},{2,0},{3,1},{4,6},{5,7},{6,4},{7,5},{8,10},{9,11},{10,... | collective-permute-start | bytes 3145736 | tf_op jit(solution)/shard_map/ppermute | solution.py:77
  516.4 36.2 %collective-permute-start.86 = (bf16[256,1408]{1,0:T(8,128)(2,1)}, bf16[256,1408]{1,0:T(8,128)(2,1)}, u32[]{:S(2)}, u32[]{:S(2)}) collective-permute-start(bf16[256,1408]{1,0:T(8,128)(2,1)} %get-tuple-element.61), channel_id=1, source_target_pairs={{8,0},{16,8},{24,16},{28,24},{20,28},{12,20},{4,12},{0,4},{9,1},{1... | collective-permute-start | bytes 2162696 | tf_op jit(solution)/shard_map/ppermute | solution.py:68
  519.5 90.6 %collective-permute-start.83 = (bf16[256,1408]{1,0:T(8,128)(2,1)}, bf16[256,1408]{1,0:T(8,128)(2,1)}, u32[]{:S(2)}, u32[]{:S(2)}) collective-permute-start(bf16[256,1408]{1,0:T(8,128)(2,1)} %get-tuple-element.60), channel_id=1, source_target_pairs={{0,8},{8,16},{16,24},{24,28},{28,20},{20,12},{12,4},{4,0},{1,9},{9... | collective-permute-start | bytes 2162696 | tf_op jit(solution)/shard_map/ppermute | solution.py:67
  532.9 95.6 %collective-permute-start.75 = (bf16[256,1408]{1,0:T(8,128)(2,1)}, bf16[256,1408]{1,0:T(8,128)(2,1)S(1)}, u32[]{:S(2)}, u32[]{:S(2)}) collective-permute-start(bf16[256,1408]{1,0:T(8,128)(2,1)} %get-tuple-element.66), channel_id=1, source_target_pairs={{0,8},{8,16},{16,24},{24,28},{28,20},{20,12},{12,4},{4,0},{1,9},{9... | collective-permute-start | bytes 2162696 | tf_op jit(solution)/shard_map/ppermute | solution.py:67
  571.6 74.8 %collective-permute-start.67 = (bf16[256,1408]{1,0:T(8,128)(2,1)}, bf16[256,1408]{1,0:T(8,128)(2,1)}, u32[]{:S(2)}, u32[]{:S(2)}) collective-permute-start(bf16[256,1408]{1,0:T(8,128)(2,1)} %get-tuple-element.72), channel_id=1, source_target_pairs={{0,8},{8,16},{16,24},{24,28},{28,20},{20,12},{12,4},{4,0},{1,9},{9... | collective-permute-start | bytes 2162696 | tf_op jit(solution)/shard_map/ppermute | solution.py:67
  573.2 37.8 %collective-permute-start.87 = (bf16[256,1408]{1,0:T(8,128)(2,1)}, bf16[256,1408]{1,0:T(8,128)(2,1)}, u32[]{:S(2)}, u32[]{:S(2)}) collective-permute-start(bf16[256,1408]{1,0:T(8,128)(2,1)} %slice_add_fusion.5), channel_id=1, source_target_pairs={{8,0},{16,8},{24,16},{28,24},{20,28},{12,20},{4,12},{0,4},{9,1},{1... | collective-permute-start | bytes 2162696 | tf_op jit(solution)/shard_map/ppermute | solution.py:68
  574.7 54.9 %collective-permute-start.79 = (bf16[256,1408]{1,0:T(8,128)(2,1)}, bf16[256,1408]{1,0:T(8,128)(2,1)}, u32[]{:S(2)}, u32[]{:S(2)}) collective-permute-start(bf16[256,1408]{1,0:T(8,128)(2,1)} %slice_add_fusion.9), channel_id=1, source_target_pairs={{8,0},{16,8},{24,16},{28,24},{20,28},{12,20},{4,12},{0,4},{9,1},{1... | collective-permute-start | bytes 2162696 | tf_op jit(solution)/shard_map/ppermute | solution.py:68
  637.9 32.8 %collective-permute-start.48 = (bf16[256,2048]{1,0:T(8,128)(2,1)S(1)}, bf16[256,2048]{1,0:T(8,128)(2,1)S(1)}, u32[]{:S(2)}, u32[]{:S(2)}) collective-permute-start(bf16[256,2048]{1,0:T(8,128)(2,1)S(1)} %get-tuple-element.86), channel_id=1, source_target_pairs={{0,1},{1,0},{2,3},{3,2},{4,5},{5,4},{6,7},{7,6},{8,9},{9,8},{10,11... | collective-permute-start | bytes 3145736 | tf_op jit(solution)/shard_map/ppermute | solution.py:73
  (113 other events, 2568.1 us)

commit v2 on v1

v2 whole, which is shorter than its diff:
```python
import functools
import math

import jax
import jax.numpy as jnp
import numpy as np
from jax import lax
from jax.experimental import pallas as pl
from jax.experimental.pallas import tpu as pltpu
from jax.sharding import PartitionSpec as P

HEAD_DIM = 64
EPSILON = 1e-05
ROPE_BASE = 10000.0
LOW = jnp.bfloat16
WIDE = jnp.float32
LANES = 128


def ring_order(n):
    return list(range(0, n, 2)) + list(range(n - 1, 0, -2))


def ring_perms(n):
    order = ring_order(n)
    forward = [(order[i], order[(i + 1) % n]) for i in range(n)]
    return forward, [(b, a) for a, b in forward]


def ring_tables(n):
    order = ring_order(n)
    place = [order.index(j) for j in range(n)]
    sources = [[order[(place[i] + s) % n] for s in range(n)] for i in range(n)]
    offsets = [[(place[j] - place[i]) % n for j in range(n)] for i in range(n)]
    return np.array(sources, np.int32), np.array(offsets, np.int32)


class Line:
    def __init__(self, token):
        self.token = token

    def after(self, *values):
        out = lax.optimization_barrier((*values, self.token))
        return out[0] if len(values) == 1 else out[:-1]

    def passed(self, *values):
        out = lax.optimization_barrier((*values, self.token))
        self.token = out[-1]
        return out[0] if len(values) == 1 else out[:-1]

    def run(self, work, *values):
        result = work(*lax.optimization_barrier((*values, self.token))[:-1])
        if isinstance(result, (tuple, list)):
            return self.passed(*result)
        return self.passed(result)

    def send(self, value, axis, pairs):
        return lax.ppermute(self.after(value), axis, pairs)


class RingGather:
    def __init__(self, line, own, n, split):
        self.line, self.n, self.split = line, n, split
        self.chunks = {0: own}
        self.flying = None

    def start(self, hop):
        n, pairs = self.n, ring_perms(self.n)
        ahead, behind = self.chunks[(n - hop + 1) % n], self.chunks[hop - 1]
        if hop == n // 2:
            ahead, behind = ahead[:, : self.split], behind[:, self.split :]
        self.flying = (self.line.send(ahead, "dp", pairs[0]), self.line.send(behind, "dp", pairs[1]))

    def wait(self, hop):
        ahead, behind = self.line.passed(*self.flying)
        if hop == self.n // 2:
            self.far = (ahead, behind)
        else:
            self.chunks[self.n - hop], self.chunks[hop] = ahead, behind

    def panel(self):
        n = self.n
        near = [self.chunks[s] for s in range(n) if s != n // 2]
        if near[0].shape[0] % LANES == 0:
            return [*near, *self.far]
        far = jnp.concatenate(self.far, axis=1)
        return [jnp.concatenate([*near[: n // 2], far, *near[n // 2 :]], axis=0)]


class RingReduce:
    def __init__(self, line, product, n, split):
        self.line, self.product, self.n, self.split = line, product, n, split
        self.came = ()

    def start(self, hop):
        n, pairs = self.n, ring_perms(self.n)
        part = self.product.shape[0] // n
        if hop == 1:
            far = self.product[n // 2 * part : (n // 2 + 1) * part]
            ahead, behind = far[:, : self.split], far[:, self.split :]
        else:
            ahead, behind = self.line.run(
                lambda v, *c: grow(v, c, n, n // 2 - hop + 1, self.split), self.product, *self.came
            )
        self.came = (self.line.send(ahead, "dp", pairs[0]), self.line.send(behind, "dp", pairs[1]))

    def wait(self, hop):
        self.came = self.line.passed(*self.came)

    def total(self):
        return self.line.run(lambda v, *c: grow(v, c, self.n, 0, self.split), self.product, *self.came)


CORE = [(i, i ^ 1) for i in range(4)]
PAIR = [(i, i ^ 2) for i in range(4)]


class GroupGather:
    def __init__(self, line, own):
        self.line, self.own = line, own
        self.pair = line.send(own, "fsdp", PAIR)
        self.core = line.send(own, "fsdp", CORE)

    def relay(self):
        self.pair, self.core = self.line.passed(self.pair, self.core)
        self.diagonal = self.line.send(self.pair, "fsdp", CORE)

    def blocks(self):
        return [self.own, self.pair, self.core, self.line.passed(self.diagonal)]


class GroupReduce:
    def __init__(self, line, blocks):
        self.line, self.blocks = line, blocks
        self.far = line.send(blocks[3], "fsdp", CORE)
        self.near = line.send(blocks[2], "fsdp", CORE)

    def relay(self):
        far, self.near = self.line.passed(self.far, self.near)
        self.sent = self.line.send(self.line.run(plus, self.blocks[1], far), "fsdp", PAIR)

    def terms(self):
        return self.blocks[0], self.near, self.line.passed(self.sent)


def dot(a, b):
    return jnp.dot(a, b, preferred_element_type=WIDE)


def dot_rows(a, b):
    return lax.dot_general(a, b, (((1,), (1,)), ((), ())), preferred_element_type=WIDE)


def dot_firsts(a, b):
    return lax.dot_general(a, b, (((0,), (0,)), ((), ())), preferred_element_type=WIDE)


def by_rows(rows, width):
    return pl.BlockSpec((rows, width), lambda i: (i, 0))


def whole(value):
    zeros = (0,) * value.ndim
    return pl.BlockSpec(value.shape, lambda i: zeros, pipeline_mode=pl.Buffered(1))


def shaped(shape, kind):
    return jax.ShapeDtypeStruct(shape, kind)


def times_chunks(value, chunks):
    total, at = None, 0
    for chunk in chunks:
        size = chunk.shape[0]
        term = dot(value[:, at : at + size], chunk[...])
        total = term if total is None else total + term
        at += size
    return total


def into_chunks(out_ref, values, chunk_sets):
    at = 0
    for row in zip(*chunk_sets):
        size = row[0].shape[0]
        total = None
        for value, chunk in zip(values, row):
            term = dot_rows(value, chunk[...])
            total = term if total is None else total + term
        out_ref[:, at : at + size] = total.astype(out_ref.dtype)
        at += size


def pieces_of(panel, split):
    if len(panel) == 1:
        chunk = panel[0]
        return [chunk.at[:, :split]], [chunk.at[:, split:]]
    near, far = panel[:-2], panel[-2:]
    left = [chunk.at[:, :split] for chunk in near]
    right = [chunk.at[:, split:] for chunk in near]
    at = (len(near) + 1) // 2
    return left[:at] + [far[0]] + left[at:], right[:at] + [far[1]] + right[at:]


def turn(values, first_half):
    width = values.shape[-1]
    left = pltpu.roll(values, width - HEAD_DIM // 2, 1)
    right = pltpu.roll(values, HEAD_DIM // 2, 1)
    return jnp.where(first_half, -left, right)


def lane_ids(rows, width):
    return lax.broadcasted_iota(jnp.int32, (rows, width), 1)


def allowed_pairs(column, row):
    rows = column.shape[0]
    later = lax.broadcasted_iota(jnp.int32, (rows, rows), 0)
    earlier = lax.broadcasted_iota(jnp.int32, (rows, rows), 1)
    return (column == row) & (later >= earlier)


def normalize(hidden, gain):
    inverse = lax.rsqrt(jnp.mean(hidden * hidden, axis=-1, keepdims=True) + EPSILON)
    return (hidden * inverse * gain).astype(LOW)


def attention_forward(count, *refs):
    x_ref, gain_ref, cos_ref, sin_ref, col_ref, row_ref = refs[:6]
    turned_ref, q_ref, kv_ref, o_ref, lse_ref = refs[6 + count : 11 + count]
    branch_refs, qkv_ref = refs[11 + count : 15 + count], refs[15 + count]
    q_chunks, o_chunks = pieces_of(refs[6 : 6 + count], qkv_ref.shape[1])
    depth = gain_ref.shape[1]
    rows, width = q_ref.shape
    pairs = width // LANES
    normed = normalize(x_ref[:, :depth].astype(WIDE), gain_ref[...])
    turned_ref[...] = normed.T
    qkv_ref[...] = times_chunks(normed, q_chunks)
    cosine, sine = cos_ref[...], sin_ref[...]
    lanes = lane_ids(rows, LANES)
    even = lanes < HEAD_DIM
    first = (lanes % HEAD_DIM) < HEAD_DIM // 2
    keyval = qkv_ref[:, width:]
    keyval_rot = keyval * cosine + turn(keyval, first) * sine
    keyval = jnp.where(even, keyval_rot, keyval)
    kv_ref[...] = keyval.astype(LOW)
    other = pltpu.roll(keyval, HEAD_DIM, 1)
    keys = jnp.where(even, keyval, other).astype(LOW)
    vals = jnp.where(even, other, keyval).astype(LOW)
    allowed = allowed_pairs(col_ref[...], row_ref[0])
    log_sums = jnp.zeros((rows, LANES), WIDE)
    for pair in range(pairs):
        piece = qkv_ref[:, pair * LANES : (pair + 1) * LANES]
        piece = (piece * cosine + turn(piece, first) * sine).astype(LOW)
        q_ref[:, pair * LANES : (pair + 1) * LANES] = piece
        mixed = []
        for side in range(2):
            chosen = jnp.where(even if side == 0 else ~even, piece, jnp.zeros_like(piece))
            scores = dot_rows(chosen, keys) * (HEAD_DIM ** -0.5)
            scores = jnp.where(allowed, scores, -1e30)
            peak = jnp.max(scores, axis=1, keepdims=True)
            powers = jnp.exp(scores - peak)
            total = jnp.sum(powers, axis=1, keepdims=True)
            soft = (powers / total).astype(LOW)
            mixed.append(dot(soft, vals))
            log_sums = jnp.where(lanes == 2 * pair + side, peak + jnp.log(total), log_sums)
        o_ref[:, pair * LANES : (pair + 1) * LANES] = jnp.where(even, mixed[0], mixed[1]).astype(LOW)
    lse_ref[...] = log_sums
    for block, branch_ref in enumerate(branch_refs):

        @pl.when(pl.program_id(0) == block)
        def _(branch_ref=branch_ref):
            into_chunks(branch_ref, [o_ref[...]], [o_chunks])


def fixed(rows, width):
    return pl.BlockSpec((rows, width), lambda i: (0, 0))


def attend(x, gain, cosine, sine, column, row, panel, width, rows):
    total, depth = x.shape[0], gain.shape[1]
    return pl.pallas_call(
        functools.partial(attention_forward, len(panel)),
        grid=(total // rows,),
        in_specs=[
            by_rows(rows, x.shape[1]),
            whole(gain),
            by_rows(rows, LANES),
            by_rows(rows, LANES),
            by_rows(rows, 1),
            pl.BlockSpec((1, 1, rows), lambda i: (i, 0, 0)),
        ]
        + [whole(v) for v in panel],
        out_specs=[
            pl.BlockSpec((depth, rows), lambda i: (0, i)),
            by_rows(rows, width),
            by_rows(rows, LANES),
            by_rows(rows, width),
            by_rows(rows, LANES),
        ]
        + [fixed(rows, depth)] * 4,
        out_shape=[
            shaped((depth, total), LOW),
            shaped((total, width), LOW),
            shaped((total, LANES), LOW),
            shaped((total, width), LOW),
            shaped((total, LANES), WIDE),
        ]
        + [shaped((rows, depth), LOW)] * 4,
        scratch_shapes=[pltpu.VMEM((rows, width + LANES), WIDE)],
        name="attend",
    )(x, gain, cosine, sine, column, row, *panel)


def attention_backward(count, *refs):
    dh_ref, q_ref, kv_ref, lse_ref, cos_ref, sin_ref, col_ref, row_ref = refs[:8]
    grad_ref, part_refs, do_ref = refs[8 + count], refs[9 + count : 13 + count], refs[13 + count]
    q_chunks, o_chunks = pieces_of(refs[8 : 8 + count], grad_ref.shape[1])
    rows, width = q_ref.shape
    pairs = width // LANES
    scale = HEAD_DIM ** -0.5
    do_ref[...] = times_chunks(dh_ref, o_chunks).astype(LOW)
    cosine, sine = cos_ref[...], sin_ref[...]
    lanes = lane_ids(rows, LANES)
    even = lanes < HEAD_DIM
    first = (lanes % HEAD_DIM) < HEAD_DIM // 2
    keyval = kv_ref[...].astype(WIDE)
    other = pltpu.roll(keyval, HEAD_DIM, 1)
    keys = jnp.where(even, keyval, other).astype(LOW)
    vals = jnp.where(even, other, keyval).astype(LOW)
    allowed = allowed_pairs(col_ref[...], row_ref[0])
    log_sums = lse_ref[...]
    grad_keys = jnp.zeros((rows, LANES), WIDE)
    grad_vals = jnp.zeros((rows, LANES), WIDE)
    for pair in range(pairs):
        piece = q_ref[:, pair * LANES : (pair + 1) * LANES]
        grads = do_ref[:, pair * LANES : (pair + 1) * LANES]
        turned = []
        for side in range(2):
            mine = even if side == 0 else ~even
            chosen = jnp.where(mine, piece, jnp.zeros_like(piece))
            chosen_grad = jnp.where(mine, grads, jnp.zeros_like(grads))
            head = 2 * pair + side
            log_sum = log_sums[:, head : head + 1]
            scores = jnp.where(allowed, dot_rows(chosen, keys) * scale, -1e30)
            soft = jnp.exp(scores - log_sum)
            grad_soft = dot_rows(chosen_grad, vals)
            delta = jnp.sum(soft * grad_soft, axis=1, keepdims=True)
            grad_scores = (soft * (grad_soft - delta)).astype(LOW)
            grad_vals = grad_vals + dot_firsts(soft.astype(LOW), chosen_grad)
            grad_keys = grad_keys + dot_firsts(grad_scores, chosen)
            turned.append(dot(grad_scores, keys))
        grad_q = jnp.where(even, turned[0], turned[1]) * scale
        grad_q = grad_q * cosine - turn(grad_q, first) * sine
        grad_ref[:, pair * LANES : (pair + 1) * LANES] = grad_q.astype(LOW)
    grad_keys = (grad_keys + pltpu.roll(grad_keys, HEAD_DIM, 1)) * scale
    grad_keys = grad_keys * cosine - turn(grad_keys, first) * sine
    grad_vals = grad_vals + pltpu.roll(grad_vals, HEAD_DIM, 1)
    grad_ref[:, width:] = jnp.where(even, grad_keys, grad_vals).astype(LOW)
    for block, part_ref in enumerate(part_refs):

        @pl.when(pl.program_id(0) == block)
        def _(part_ref=part_ref):
            into_chunks(part_ref, [grad_ref[...]], [q_chunks])


def attend_back(grads, query, keyval, log_sums, cosine, sine, column, row, panel, rows):
    total, depth = grads.shape
    width = query.shape[1]
    return pl.pallas_call(
        functools.partial(attention_backward, len(panel)),
        grid=(total // rows,),
        in_specs=[
            by_rows(rows, depth),
            by_rows(rows, width),
            by_rows(rows, LANES),
            by_rows(rows, LANES),
            by_rows(rows, LANES),
            by_rows(rows, LANES),
            by_rows(rows, 1),
            pl.BlockSpec((1, 1, rows), lambda i: (i, 0, 0)),
        ]
        + [whole(v) for v in panel],
        out_specs=[by_rows(rows, width + LANES)] + [fixed(rows, depth)] * 4,
        out_shape=[shaped((total, width + LANES), LOW)] + [shaped((rows, depth), LOW)] * 4,
        scratch_shapes=[pltpu.VMEM((rows, width), LOW)],
        name="attend_back",
    )(grads, query, keyval, log_sums, cosine, sine, column, row, *panel)


def plus_kernel(a_ref, b_ref, out_ref):
    out_ref[...] = a_ref[...] + b_ref[...]


def plus(a, b):
    rows, depth = a.shape
    step = rows // 2
    return pl.pallas_call(
        plus_kernel,
        grid=(2,),
        in_specs=[by_rows(step, depth)] * 2,
        out_specs=by_rows(step, depth),
        out_shape=shaped(a.shape, a.dtype),
        name="plus",
    )(a, b)


def gathered_kernel(own_ref, pair_ref, core_ref, diagonal_ref, all_ref, turned_ref=None):
    for block, ref in enumerate((own_ref, pair_ref, core_ref, diagonal_ref)):

        @pl.when(pl.program_id(0) == block)
        def _(ref=ref):
            value = ref[...]
            all_ref[...] = value
            if turned_ref is not None:
                turned_ref[...] = value.T


def gathered(blocks, with_turned):
    rows, depth = blocks[0].shape
    out_specs, out_shape = [by_rows(rows, depth)], [shaped((4 * rows, depth), LOW)]
    if with_turned:
        out_specs.append(pl.BlockSpec((depth, rows), lambda i: (0, i)))
        out_shape.append(shaped((depth, 4 * rows), LOW))
    out = pl.pallas_call(
        gathered_kernel,
        grid=(4,),
        in_specs=[whole(v) for v in blocks],
        out_specs=out_specs,
        out_shape=out_shape,
        name="gathered",
    )(*blocks)
    return tuple(out) if with_turned else out[0]


def added(refs):
    total = refs[0][...].astype(WIDE)
    for ref in refs[1:]:
        total = total + ref[...].astype(WIDE)
    return total


def join_kernel(x_ref, own_ref, near_ref, sent_ref, gain_ref, hidden_ref, normed_ref):
    hidden = added((x_ref, own_ref, near_ref, sent_ref))
    hidden_ref[...] = hidden
    normed_ref[...] = normalize(hidden, gain_ref[...])


def join(x, gain, *parts):
    rows, depth = x.shape
    step = rows // 2
    return pl.pallas_call(
        join_kernel,
        grid=(2,),
        in_specs=[by_rows(step, depth)] * 4 + [whole(gain)],
        out_specs=[by_rows(step, depth)] * 2,
        out_shape=[shaped((rows, depth), WIDE), shaped((rows, depth), LOW)],
        name="join",
    )(x, *parts, gain)


def feed_kernel(count, *refs):
    x_ref = refs[0]
    act_ref, slope_ref, silu_ref = refs[1 + count :]
    g_chunks, u_chunks = pieces_of(refs[1 : 1 + count], act_ref.shape[1])
    gate = times_chunks(x_ref, g_chunks)
    up = times_chunks(x_ref, u_chunks)
    sigmoid = 1.0 / (1.0 + jnp.exp(-gate))
    silu = gate * sigmoid
    act_ref[...] = (silu * up).astype(LOW)
    silu_ref[...] = silu.astype(LOW)
    slope_ref[...] = (up * sigmoid * (1.0 + gate * (1.0 - sigmoid))).astype(LOW)


def feed(x, panel, wide):
    total, depth = x.shape
    step = total // 4
    return pl.pallas_call(
        functools.partial(feed_kernel, len(panel)),
        grid=(4,),
        in_specs=[by_rows(step, depth)] + [whole(v) for v in panel],
        out_specs=[by_rows(step, wide)] * 3,
        out_shape=[shaped((total, wide), LOW)] * 3,
        name="feed",
    )(x, *panel)


def feed_back_kernel(count, split, *refs):
    dy_ref, slope_ref, silu_ref = refs[:3]
    (out_ref,) = refs[3 + count :]
    wide = slope_ref.shape[1]
    at = 0
    for chunks in pieces_of(refs[3 : 3 + count], split):
        end = at + chunks[0].shape[1]
        grads = times_chunks(dy_ref, chunks)
        out_ref[:, at:end] = (grads * slope_ref[:, at:end].astype(WIDE)).astype(LOW)
        out_ref[:, wide + at : wide + end] = (grads * silu_ref[:, at:end].astype(WIDE)).astype(LOW)
        at = end


def feed_back(grads, slope, silu, panel, split):
    total, depth = grads.shape
    wide = slope.shape[1]
    step = total // 4
    return pl.pallas_call(
        functools.partial(feed_back_kernel, len(panel), split),
        grid=(4,),
        in_specs=[by_rows(step, depth), by_rows(step, wide), by_rows(step, wide)]
        + [whole(v) for v in panel],
        out_specs=by_rows(step, 2 * wide),
        out_shape=shaped((total, 2 * wide), LOW),
        name="feed_back",
    )(grads, slope, silu, *panel)


def spread_kernel(count, split, *refs):
    value, out_refs = refs[0], refs[1 + count :]
    left, right = pieces_of(refs[1 : 1 + count], split)
    rows = out_refs[0].shape[0]
    each = value.shape[0] // rows
    for block, out_ref in enumerate(out_refs):
        inside = block % each

        @pl.when(pl.program_id(0) == block // each)
        def _(out_ref=out_ref, at=inside * rows):
            pieces = [value[at : at + rows, :split], value[at : at + rows, split:]]
            into_chunks(out_ref, pieces, [left, right])


def spread(value, panel, split, rows):
    total, wide = value.shape
    n = len(panel)
    depth = panel[0].shape[0] * max(1, n - 1)
    return pl.pallas_call(
        functools.partial(spread_kernel, n, split),
        grid=(4,),
        in_specs=[by_rows(total // 4, wide)] + [whole(c) for c in panel],
        out_specs=[fixed(rows, depth)] * 4,
        out_shape=[shaped((rows, depth), LOW)] * 4,
        name="spread",
    )(value, *panel)


def product_kernel(count, *refs):
    out_ref = refs[-1]
    at = 0
    for left, right in zip(refs[:count], refs[count : 2 * count]):
        end = at + right.shape[1]
        out_ref[:, at:end] = dot(left[...], right[...]).astype(LOW)
        at = end


def product(lefts, rights):
    depth, total = lefts[0].shape
    wide = sum(v.shape[1] for v in rights)
    step = depth // 8
    return pl.pallas_call(
        functools.partial(product_kernel, len(lefts)),
        grid=(8,),
        in_specs=[by_rows(step, total) for _ in lefts] + [whole(v) for v in rights],
        out_specs=by_rows(step, wide),
        out_shape=shaped((depth, wide), LOW),
        name="product",
    )(*lefts, *rights)


def grow_kernel(split, narrow, *refs):
    ahead_term, behind_term, ahead, behind, ahead_out, behind_out = refs
    if narrow:
        ahead_out[:, :split] = ahead_term[:, :split] + ahead[...]
        ahead_out[:, split:] = ahead_term[:, split:]
        behind_out[:, :split] = behind_term[:, :split]
        behind_out[:, split:] = behind_term[:, split:] + behind[...]
    else:
        ahead_out[...] = ahead_term[...] + ahead[...]
        behind_out[...] = behind_term[...] + behind[...]


def last_kernel(term, ahead, behind, out):
    out[...] = term[...].astype(WIDE) + ahead[...].astype(WIDE) + behind[...].astype(WIDE)


def grow(product, came, n, away, split):
    part, wide = product.shape[0] // n, product.shape[1]
    narrow = away == n // 2 - 1
    step = part // 2
    sizes = [v.shape[1] for v in came]
    came_specs = [by_rows(step, size) for size in sizes]

    def rows_at(offset):
        return pl.BlockSpec((step, wide), lambda i: (2 * offset + i, 0))

    if away == 0:
        return pl.pallas_call(
            last_kernel,
            grid=(2,),
            in_specs=[rows_at(0)] + came_specs,
            out_specs=by_rows(step, wide),
            out_shape=shaped((part, wide), WIDE),
            name="last",
        )(product, *came)
    return tuple(
        pl.pallas_call(
            functools.partial(grow_kernel, split, narrow),
            grid=(2,),
            in_specs=[rows_at(away), rows_at(n - away)] + came_specs,
            out_specs=[by_rows(step, wide)] * 2,
            out_shape=[shaped((part, wide), LOW)] * 2,
            name="grow",
        )(product, product, *came)
    )


def norm_back_kernel(hidden_ref, gain_ref, rest_ref, own_ref, near_ref, sent_ref, grads_ref, low_ref, terms_ref):
    hidden = hidden_ref[...].astype(WIDE)
    grad_normed = added((own_ref, near_ref, sent_ref))
    inverse = lax.rsqrt(jnp.mean(hidden * hidden, axis=-1, keepdims=True) + EPSILON)
    unit = hidden * inverse
    scaled = grad_normed * gain_ref[...]
    grads = rest_ref[...].astype(WIDE) + inverse * (
        scaled - unit * jnp.mean(scaled * unit, axis=-1, keepdims=True)
    )
    grads_ref[...] = grads
    low_ref[...] = grads.astype(LOW)

    @pl.when(pl.program_id(0) == 0)
    def _():
        terms_ref[...] = jnp.zeros_like(terms_ref)

    terms_ref[...] += jnp.sum(grad_normed * unit, axis=0, keepdims=True)


def norm_back(hidden, gain, rest, *parts):
    rows, depth = hidden.shape
    step = rows // 2
    return pl.pallas_call(
        norm_back_kernel,
        grid=(2,),
        in_specs=[by_rows(step, depth), whole(gain)] + [by_rows(step, depth)] * 4,
        out_specs=[by_rows(step, depth), by_rows(step, depth), pl.BlockSpec((1, depth), lambda i: (0, 0))],
        out_shape=[shaped((rows, depth), WIDE), shaped((rows, depth), LOW), shaped((1, depth), WIDE)],
        name="norm_back",
    )(hidden, gain, rest, *parts)


def shuffle_kernel(n, order_ref, *refs):
    out_ref = refs[-1]
    part = out_ref.shape[1] // n
    for s in range(n):
        at = pl.multiple_of(order_ref[s] * part, part)
        if len(refs) == 2:
            piece = refs[0][:, pl.ds(at, part)]
        else:
            piece = refs[0][:, pl.ds(at, part)]
            for ref in refs[1:-1]:
                piece = piece + ref[:, pl.ds(at, part)].astype(WIDE)
        out_ref[:, s * part : (s + 1) * part] = piece.astype(out_ref.dtype)


def shuffle(order, n, *values):
    rows, depth = values[0].shape
    part = depth // n
    if part % LANES:
        total = values[0]
        for v in values[1:]:
            total = total + v.astype(WIDE)
        pieces = [lax.dynamic_slice(total, (0, order[s] * part), (rows, part)) for s in range(n)]
        return jnp.concatenate(pieces, axis=1).astype(LOW)
    step = rows // 2
    return pl.pallas_call(
        functools.partial(shuffle_kernel, n),
        grid_spec=pltpu.PrefetchScalarGridSpec(
            num_scalar_prefetch=1,
            grid=(2,),
            in_specs=[pl.BlockSpec((step, depth), lambda i, order: (i, 0))] * len(values),
            out_specs=pl.BlockSpec((step, depth), lambda i, order: (i, 0)),
        ),
        out_shape=shaped((rows, depth), LOW),
        name="shuffle",
    )(order, *values)


def tables(segment_block):
    rows = segment_block.shape[0]
    places = jnp.arange(rows, dtype=jnp.int32)
    same = segment_block[:, None] == segment_block[None, :]
    first_index = jnp.min(jnp.where(same, places[None, :], rows), axis=1)
    offsets = (places - first_index).astype(WIDE)
    half = HEAD_DIM // 2
    frequencies = jnp.exp(jnp.arange(half, dtype=WIDE) * (-2.0 * math.log(ROPE_BASE) / HEAD_DIM))
    angles = offsets[:, None] * frequencies[None, :]
    cosine, sine = jnp.cos(angles), jnp.sin(angles)
    return jnp.concatenate([cosine] * 4, axis=1), jnp.concatenate([sine] * 4, axis=1)


def on_device(
    tokens, segments, gain_attn, w_query, w_key, w_value, w_out, gain_mlp, w_gate, w_up, w_down, cotangent
):
    n = lax.axis_size("dp")
    rows, depth = tokens.shape
    part = depth // n
    hops = n // 2
    me = lax.axis_index("dp")
    sources, offsets = [lax.dynamic_index_in_dim(jnp.asarray(t), me, keepdims=False) for t in ring_tables(n)]
    line = Line(jnp.zeros((8, LANES), WIDE))

    heads_wide, hidden_wide = w_query.shape[1], w_gate.shape[1]
    qkv_wide = heads_wide + w_key.shape[1] + w_value.shape[1]
    split = -(-hidden_wide // (2 * LANES)) * LANES
    attn = RingGather(line, jnp.concatenate([w_query, w_key, w_value, w_out.T], axis=1).astype(LOW), n, qkv_wide)
    feedw = RingGather(line, jnp.concatenate([w_gate, w_up], axis=1).astype(LOW), n, hidden_wide)
    down = RingGather(line, w_down.T.astype(LOW), n, split)

    attn.start(1)
    own_tokens = shuffle(sources, n, tokens)
    marks = jnp.broadcast_to(segments.astype(LOW)[:, None], (rows, LANES))
    x = GroupGather(line, jnp.concatenate([own_tokens, marks], axis=1))
    gains = jnp.stack([gain_attn, gain_mlp]).astype(LOW)
    bits = [1 << i for i in range((n - 1).bit_length())]

    def gains_from(value, bit):
        other = lax.ppermute(value, "dp", [(i, i ^ bit) for i in range(n)])
        return jnp.concatenate([value, other], axis=1)

    gains = gains_from(gains, bits[0])
    attn.wait(1)
    attn.start(2)
    for bit in bits[1:-1]:
        gains = gains_from(line.passed(gains), bit)
    own_grads = line.run(lambda *v: shuffle(v[0], n, v[1]), sources, cotangent)
    for hop in range(2, hops - 1):
        attn.wait(hop)
        attn.start(hop + 1)
    gains = gains_from(line.passed(gains), bits[-1])
    x.relay()
    attn.wait(hops - 1)
    attn.start(hops)
    token_rows = line.run(lambda *v: gathered(v, False), *x.blocks())
    gains = jnp.take(gains.reshape(2, n, part), sources ^ me, axis=1).reshape(2, depth).astype(WIDE)
    gains = line.passed(gains)
    gain_one, gain_two = gains[0:1], gains[1:2]
    attn.wait(hops)
    feedw.start(1)
    y = GroupGather(line, own_grads)
    segment_blocks = token_rows[:, depth].astype(jnp.int32).reshape(-1, rows)
    column, row = segment_blocks.reshape(-1, 1), segment_blocks[:, None, :]
    cosine, sine = line.run(lambda v: jax.vmap(tables)(v), segment_blocks)
    cosine, sine = cosine.reshape(-1, LANES), sine.reshape(-1, LANES)

    attn_panel = attn.panel()
    normed_turned, query, keyval, mixed, log_sums, *branch = line.run(
        lambda *v: attend(*v[:6], v[6:], heads_wide, rows),
        token_rows, gain_one, cosine, sine, column, row, *attn_panel,
    )
    y.relay()
    feedw.wait(1)
    feedw.start(2)
    branch = GroupReduce(line, branch)
    grads_all, grads_turned = line.run(lambda *v: gathered(v, True), *y.blocks())
    branch.relay()
    for hop in range(2, hops - 1):
        feedw.wait(hop)
        feedw.start(hop + 1)
    hidden, normed_own = line.run(join, own_tokens, gain_two, *branch.terms())
    z = GroupGather(line, normed_own)
    feedw.wait(hops - 1)
    feedw.start(hops)
    z.relay()
    normed_mlp, mlp_turned = line.run(lambda *v: gathered(v, True), *z.blocks())

    feedw.wait(hops)
    down.start(1)
    feed_panel = feedw.panel()
    activation, slope, silu = line.run(lambda a, *v: feed(a, v, hidden_wide), normed_mlp, *feed_panel)
    for hop in range(1, hops):
        down.wait(hop)
        down.start(hop + 1)
        if hop == 1:
            down_terms = line.run(lambda a, b: product([a], [b]), grads_turned, activation)
            r_down = RingReduce(line, down_terms, n, split)
    r_down.start(1)
    down.wait(hops)
    down_panel = down.panel()

    grad_feed = line.run(
        lambda a, b, c, *v: feed_back(a, b, c, v, split), grads_all, slope, silu, *down_panel
    )
    for hop in range(1, hops - 2):
        r_down.wait(hop)
        r_down.start(hop + 1)
    grad_normed = line.run(lambda a, *v: spread(a, v, hidden_wide, rows), grad_feed, *feed_panel)
    r_down.wait(hops - 2)
    r_down.start(hops - 1)
    grad_normed = GroupReduce(line, grad_normed)
    feed_terms = line.run(lambda a, b: product([a], [b]), mlp_turned, grad_feed)
    r_down.wait(hops - 1)
    r_down.start(hops)
    grad_normed.relay()
    layer_part = line.run(lambda a, *v: spread(a, v, split, rows), activation, *down_panel)
    r_down.wait(hops)
    r_feed = RingReduce(line, feed_terms, n, hidden_wide)
    r_feed.start(1)
    grad_down = r_down.total()
    grad_hidden, grad_branch, gain_mlp_terms = line.run(
        norm_back, hidden, gain_two, own_grads, *grad_normed.terms()
    )
    b = GroupGather(line, grad_branch)
    r_feed.wait(1)
    r_feed.start(2)
    b.relay()
    branch_grads, branch_turned = line.run(lambda *v: gathered(v, True), *b.blocks())
    for hop in range(2, hops - 1):
        r_feed.wait(hop)
        r_feed.start(hop + 1)

    grad_qkv, *grad_input_part = line.run(
        lambda *v: attend_back(*v[:8], v[8:], rows),
        branch_grads, query, keyval, log_sums, cosine, sine, column, row, *attn_panel,
    )
    attn_terms = line.run(
        lambda *v: product(v[:2], v[2:]), normed_turned, branch_turned, grad_qkv, mixed
    )
    r_feed.wait(hops - 1)
    r_feed.start(hops)
    grad_input_sum = GroupReduce(line, grad_input_part)
    grad_input_sum.relay()
    r_attn = RingReduce(line, attn_terms, n, qkv_wide)
    r_feed.wait(hops)
    r_attn.start(1)
    layer_sum = GroupReduce(line, layer_part)
    grad_w_feed = r_feed.total()
    r_attn.wait(1)
    r_attn.start(2)
    _, grad_tokens, gain_attn_terms = line.run(
        norm_back, own_tokens, gain_one, grad_hidden, *grad_input_sum.terms()
    )
    layer_sum.relay()
    gain_terms = jnp.concatenate([gain_attn_terms, gain_mlp_terms], axis=0).reshape(2, n, part)
    gain_terms = jnp.take(gain_terms, offsets, axis=1).reshape(2, depth)
    gain_steps = [("fsdp", 4, 1), ("fsdp", 4, 2)] + [("dp", n, bit) for bit in bits]

    def gain_step(value, step):
        axis, size, bit = step
        other = line.passed(line.send(value, axis, [(i, i ^ bit) for i in range(size)]))
        return line.run(jnp.add, value, other)

    for step in gain_steps[:2]:
        gain_terms = gain_step(gain_terms, step)
    grad_tokens = line.run(lambda at, v: shuffle(at, n, v), offsets, grad_tokens)
    for hop in range(2, hops):
        r_attn.wait(hop)
        r_attn.start(hop + 1)
        for step in gain_steps[2 * hop - 2 : 2 * hop]:
            gain_terms = gain_step(gain_terms, step)
    for step in gain_steps[2 * hops - 2 :]:
        gain_terms = gain_step(gain_terms, step)
    layer_own = line.run(lambda at, *v: shuffle(at, n, *v), offsets, hidden, *layer_sum.terms())
    gain_own = lax.dynamic_slice(gain_terms, (0, me * part), (2, part))
    r_attn.wait(hops)
    grad_attn = r_attn.total()

    value_at = heads_wide + w_key.shape[1]
    return (
        layer_own,
        grad_tokens,
        gain_own[0],
        grad_attn[:, :heads_wide],
        grad_attn[:, heads_wide:value_at],
        grad_attn[:, value_at:qkv_wide],
        grad_attn[:, qkv_wide:].T,
        gain_own[1],
        grad_w_feed[:, :hidden_wide],
        grad_w_feed[:, hidden_wide:],
        grad_down.T,
    )


def solution(mesh):
    placed = (
        P(("dp", "fsdp"), None),
        P(("dp", "fsdp")),
        P("dp"),
        P("dp", "fsdp"),
        P("dp", "fsdp"),
        P("dp", "fsdp"),
        P("fsdp", "dp"),
        P("dp"),
        P("dp", "fsdp"),
        P("dp", "fsdp"),
        P("fsdp", "dp"),
        P(("dp", "fsdp"), None),
    )
    return jax.shard_map(
        on_device,
        mesh=mesh,
        in_specs=placed,
        out_specs=(
            P(("dp", "fsdp"), None),
            P(("dp", "fsdp"), None),
            P("dp"),
            P("dp", "fsdp"),
            P("dp", "fsdp"),
            P("dp", "fsdp"),
            P("fsdp", "dp"),
            P("dp"),
            P("dp", "fsdp"),
            P("dp", "fsdp"),
            P("fsdp", "dp"),
        ),
        check_vma=False,
    )
```

time: 700 us -> 591 us (0.84)
  Pallas kernels: 29.4 us -> 250 us
  matrix products: 129 us -> 0 us
  waiting for transfers between devices: 284 us -> 194 us
  blocking collectives: 49 us -> 0 us
  other arithmetic: 54.3 us -> 18.9 us
  local copies, waits for them, and re-layouts: 64.9 us -> 49.3 us
  starting transfers between devices: 80 us -> 71.8 us
    pallas_call x2 -> x36, Pallas kernels: 29.4 us -> 250 us  [the longest x3 40.8 us: product(): pl.pallas_call(functools.partial(product_kernel, len(lefts)), grid=(8,),...]
    dot_general x15 -> x0, matrix products: 129 us -> none  [the longest x5 54 us: mul(): return jnp.dot(a, b, preferred_element_type=WIDE)]
    ppermute x88 -> x80, waiting for transfers between devices: 284 us -> 194 us  [the longest x77 171 us: send(): return lax.ppermute(self.after(value), axis, pairs)]
    all_gather x1 -> x0, blocking collectives: 49 us -> none  [on_device(): lax.all_gather(jnp.stack([gain_attn, gain_mlp]).astype(LOW), 'dp', axis=1...]
    add x31 -> x5, other arithmetic: 24.7 us -> 0.05 us  [run(): result = work(*lax.optimization_barrier((*values, self.token))[:-1])]
    unnamed x181 -> x122, local copies, waits for them, and re-layouts: 48.8 us -> 26.1 us
    slice x13 -> x12, local copies, waits for them, and re-layouts: 3.96 us -> 13.2 us  [the longest x5 7.75 us: start(): ahead, behind = (far[:, :self.split], far[:, self.split:])]
    concatenate x11 -> x1, local copies, waits for them, and re-layouts: 8.61 us -> 0.28 us  [on_device(): jnp.concatenate([w_query, w_key, w_value, w_out.T], axis=1).astype(LOW)]
  transfers between devices with their start and end apart: 88 -> 80, of which waited for: 34 -> 39; matrix products, arithmetic and copies ran while one was open for 28% -> 7% of each run, Pallas kernels for 4% -> 39%
where the time goes in v2:
time: 591 us; the launch traced here: 586 us
  Pallas kernels  250 us (42%)
  waiting for transfers between devices  194 us (33%)
  starting transfers between devices  71.8 us (12%)
  local copies, waits for them, and re-layouts  49.3 us (8%)
  other arithmetic  18.9 us (3%)
    ppermute x77, waiting for transfers between devices, send(): return lax.ppermute(self.after(value), axis, pairs)  171 us
    ppermute x77, starting transfers between devices, send(): return lax.ppermute(self.after(value), axis, pairs)  66.6 us
    pallas_call x3, Pallas kernels, product(): pl.pallas_call(functools.partial(product_kernel, len(lefts)), grid=(8,),...  40.8 us
    pallas_call x2, Pallas kernels, spread(): pl.pallas_call(functools.partial(spread_kernel, n, split), grid=(4,), in_...  32.8 us
    pallas_call x1, Pallas kernels, attend_back(): pl.pallas_call(functools.partial(attention_backward, len(panel)), grid=(t...  26.9 us
    pallas_call x9, Pallas kernels, grow(): pl.pallas_call(functools.partial(grow_kernel, split, narrow), grid=(2,),...  26.6 us
    unnamed x122, local copies, waits for them, and re-layouts  26.1 us
    pallas_call x4, Pallas kernels, gathered(): pl.pallas_call(gathered_kernel, grid=(4,), in_specs=[whole(v) for v in bl...  24 us
  transfers between devices with their start and end apart: 80, of which 39 were waited for; matrix products, arithmetic and copies ran while one was open for 7% of the time, Pallas kernels for 39%

profile of v2, /device:TPU:0, one launch (start us, length us, event | category | flops | bytes accessed | tf_op | source)
XLA Modules:
  0.0 585.8 jit_solution(6978941763292732415)
XLA Ops:
  14.9 5.6 collective-permute-done.1.refs_12_.refs_14_
  25.2 10.9 %collective-permute-done = bf16[2,256]{1,0:T(2,128)(2,1)S(1)} collective-permute-done((bf16[2,256]{1,0:T(2,128)(2,1)S(1)}, bf16[2,256]{1,0:T(2,128)(2,1)S(1)}, u32[]{:S(2)}, u32[]{:S(2)}) %collective-permute-start) | collective-permute-done | bytes 1056 | tf_op jit(solution)/shard_map/ppermute | solution.py:721
  45.3 4.7 collective-permute-start.6
  50.6 11.9 %collective-permute-done.6 = bf16[2,1024]{1,0:T(2,128)(2,1)S(1)} collective-permute-done((bf16[2,1024]{1,0:T(2,128)(2,1)S(1)}, bf16[2,1024]{1,0:T(2,128)(2,1)S(1)}, u32[]{:S(2)}, u32[]{:S(2)}) %collective-permute-start.6) | collective-permute-done | bytes 4128 | tf_op jit(solution)/shard_map/ppermute | solution.py:721
  66.8 4.9 gathered.4.refs_0_
  87.8 21.1 %attend.1 = (bf16[2048,1024]{1,0:T(8,128)(2,1)}, bf16[1024,512]{1,0:T(8,128)(2,1)}, bf16[1024,128]{1,0:T(8,128)(2,1)}, bf16[1024,512]{1,0:T(8,128)(2,1)}, f32[10...) custom-call(bf16[1024,2176]{1,0:T(8,128)(2,1)} %gathered.4.refs_0_, ...), custom_call_target="tpu_custom_call" | custom-call | tf_op jit(solution)/shard_map/attend/pallas_call | solution.py:281
  113.1 6.4 %gathered.5 = (bf16[1024,2048]{1,0:T(8,128)(2,1)}, bf16[2048,1024]{1,0:T(8,128)(2,1)}) custom-call(bf16[256,2048]{1,0:T(8,128)(2,1)} %shuffle.5.own_ref.rest_ref, bf16[256,2048]{1,0:T(8,128)(2,1)} %collective-permute-done.16.pair_ref, bf16[256,2048]{1,0:T(8,128)(2,1)} %collective-permute-done.17.core_ref, bf16[256,2048]{1,0:T(8,128)(2,1)} %copy-done.33), custom_call_target="tpu_custom_call" | custom-call | tf_op jit(solution)/shard_map/gathered/pallas_call | solution.py:424
  123.7 20.3 %collective-permute-done.22.refs_6_ = bf16[256,2816]{1,0:T(8,128)(2,1)} collective-permute-done((bf16[256,2816]{1,0:T(8,128)(2,1)}, bf16[256,2816]{1,0:T(8,128)(2,1)}, u32[]{:S(2)}, u32[]{:S(2)}) %collective-permute-start.22) | collective-permute-done | bytes 1441824 | tf_op jit(solution)/shard_map/ppermute | solution.py:58
  153.2 23.7 %collective-permute-done.26.refs_5_ = bf16[256,2816]{1,0:T(8,128)(2,1)S(1)} collective-permute-done((bf16[256,2816]{1,0:T(8,128)(2,1)}, bf16[256,2816]{1,0:T(8,128)(2,1)S(1)}, u32[]{:S(2)}, u32[]{:S(2)}) %collective-permute-start.26) | collective-permute-done | bytes 1441824 | tf_op jit(solution)/shard_map/ppermute | solution.py:58
  184.7 6.4 %gathered.6 = (bf16[1024,2048]{1,0:T(8,128)(2,1)}, bf16[2048,1024]{1,0:T(8,128)(2,1)}) custom-call(bf16[256,2048]{1,0:T(8,128)(2,1)} %get-tuple-element.691.own_ref, bf16[256,2048]{1,0:T(8,128)(2,1)} %collective-permute-done.24.pair_ref, bf16[256,2048]{1,0:T(8,128)(2,1)} %collective-permute-done.25.core_ref, ...), custom_call_target="tpu_custom_call" | custom-call | tf_op jit(solution)/shard_map/gathered/pallas_call | solution.py:424
  191.1 6.6 %collective-permute-done.29.refs_8_ = bf16[256,1408]{1,0:T(8,128)(2,1)} collective-permute-done((bf16[256,1408]{1,0:T(8,128)(2,1)}, bf16[256,1408]{1,0:T(8,128)(2,1)}, u32[]{:S(2)}, u32[]{:S(2)}) %collective-permute-start.29) | collective-permute-done | bytes 720928 | tf_op jit(solution)/shard_map/ppermute | solution.py:58
  201.5 20.2 %feed.1 = (bf16[1024,1408]{1,0:T(8,128)(2,1)}, bf16[1024,1408]{1,0:T(8,128)(2,1)}, bf16[1024,1408]{1,0:T(8,128)(2,1)}) custom-call(bf16[1024,2048]{1,0:T(8,128)(2,1)} %get-tuple-element.706.refs_0_, bf16[256,2816]{1,0:T(8,128)(2,1)} %copy-done, bf16[256,2816]{1,0:T(8,128)(2,1)} %collective-permute-done.15.refs_2_, ...), custom_call_target="tpu_custom_call" | custom-call | tf_op jit(solution)/shard_map/feed/pallas_call | solution.py:477
  223.9 11.8 %product.3.refs_0_.refs_1_.term = bf16[2048,1408]{1,0:T(8,128)(2,1)} custom-call(bf16[2048,1024]{1,0:T(8,128)(2,1)} %get-tuple-element.728.refs_0_, bf16[1024,1408]{1,0:T(8,128)(2,1)} %get-tuple-element.828.refs_1_.refs_0_), custom_call_target="tpu_custom_call" | custom-call | tf_op jit(solution)/shard_map/product/pallas_call | solution.py:556
  240.9 14.0 %collective-permute-done.35.refs_7_.refs_5_ = bf16[256,1408]{1,0:T(8,128)(2,1)S(1)} collective-permute-done((bf16[256,1408]{1,0:T(8,128)(2,1)}, bf16[256,1408]{1,0:T(8,128)(2,1)S(1)}, u32[]{:S(2)}, u32[]{:S(2)}) %collective-permute-start.35) | collective-permute-done | bytes 720928 | tf_op jit(solution)/shard_map/ppermute | solution.py:58
  262.4 6.1 %collective-permute-done.38.refs_11_.refs_9_ = bf16[256,640]{1,0:T(8,128)(2,1)S(1)} collective-permute-done((bf16[256,640]{1,0:T(8,128)(2,1)S(1)}, bf16[256,640]{1,0:T(8,128)(2,1)S(1)}, u32[]{:S(2)}, u32[]{:S(2)}) %collective-permute-start.38) | collective-permute-done | bytes 327712 | tf_op jit(solution)/shard_map/ppermute | solution.py:58
  269.9 12.4 %feed_back.1.refs_0_.refs_1_ = bf16[1024,2816]{1,0:T(8,128)(2,1)} custom-call(bf16[1024,2048]{1,0:T(8,128)(2,1)} %get-tuple-element.747.refs_0_, bf16[1024,1408]{1,0:T(8,128)(2,1)} %get-tuple-element.748.refs_1_, bf16[1024,1408]{1,0:T(8,128)(2,1)} %get-tuple-element.749.refs_2_, bf16[256,1408]{1,0:T(8,128)(2,1)} %bitcast.37, bf16[256,1408]{1,0:T(8,128)(2,1)} %copy-done.14, ...), custom_call_target="tpu_custom_call" | custom-call | tf_op jit(solution)/shard_map/feed_back/pallas_call | solution.py:504
  288.7 20.5 %spread.2 = (bf16[256,2048]{1,0:T(8,128)(2,1)}, bf16[256,2048]{1,0:T(8,128)(2,1)}, bf16[256,2048]{1,0:T(8,128)(2,1)}, bf16[256,2048]{1,0:T(8,128)(2,1)}) custom-call(bf16[1024,2816]{1,0:T(8,128)(2,1)} %feed_back.1.refs_0_.refs_1_, bf16[256,2816]{1,0:T(8,128)(2,1)} %copy-done, bf16[256,2816]{1,0:T(8,128)(2,1)} %collective-permute-done.15.refs_2_, ...), custom_call_target="tpu_custom_call" | custom-call | tf_op jit(solution)/shard_map/spread/pallas_call | solution.py:533
  316.3 17.4 %product.4.refs_0_.refs_1_.term = bf16[2048,2816]{1,0:T(8,128)(2,1)} custom-call(bf16[2048,1024]{1,0:T(8,128)(2,1)} %get-tuple-element.811.refs_0_, bf16[1024,2816]{1,0:T(8,128)(2,1)} %feed_back.1.refs_0_.refs_1_), custom_call_target="tpu_custom_call" | custom-call | tf_op jit(solution)/shard_map/product/pallas_call | solution.py:556
  346.8 12.3 %spread.3 = (bf16[256,2048]{1,0:T(8,128)(2,1)}, bf16[256,2048]{1,0:T(8,128)(2,1)}, bf16[256,2048]{1,0:T(8,128)(2,1)}, bf16[256,2048]{1,0:T(8,128)(2,1)}) custom-call(bf16[1024,1408]{1,0:T(8,128)(2,1)} %get-tuple-element.828.refs_1_.refs_0_, bf16[256,1408]{1,0:T(8,128)(2,1)} %bitcast.38, bf16[256,1408]{1,0:T(8,128)(2,1)} %copy-done.14, ...), custom_call_target="tpu_custom_call" | custom-call | tf_op jit(solution)/shard_map/spread/pallas_call | solution.py:533
  367.6 5.0 norm_back.2
  373.1 4.1 collective-permute-done.49.refs_2_
  384.4 12.2 %collective-permute-done.54.pair_ref = bf16[256,2048]{1,0:T(8,128)(2,1)} collective-permute-done((bf16[256,2048]{1,0:T(8,128)(2,1)}, bf16[256,2048]{1,0:T(8,128)(2,1)}, u32[]{:S(2)}, u32[]{:S(2)}) %collective-permute-start.54) | collective-permute-done | bytes 1048608 | tf_op jit(solution)/shard_map/ppermute | solution.py:58
  399.6 6.4 %gathered.7 = (bf16[1024,2048]{1,0:T(8,128)(2,1)}, bf16[2048,1024]{1,0:T(8,128)(2,1)}) custom-call(bf16[256,2048]{1,0:T(8,128)(2,1)} %get-tuple-element.895.own_ref, bf16[256,2048]{1,0:T(8,128)(2,1)} %collective-permute-done.54.pair_ref, bf16[256,2048]{1,0:T(8,128)(2,1)} %collective-permute-done.55.core_ref, ...), custom_call_target="tpu_custom_call" | custom-call | tf_op jit(solution)/shard_map/gathered/pallas_call | solution.py:424
  405.9 7.5 %collective-permute-done.52.refs_2_ = bf16[256,2816]{1,0:T(8,128)(2,1)S(1)} collective-permute-done((bf16[256,2816]{1,0:T(8,128)(2,1)}, bf16[256,2816]{1,0:T(8,128)(2,1)S(1)}, u32[]{:S(2)}, u32[]{:S(2)}) %collective-permute-start.52) | collective-permute-done | bytes 1441824 | tf_op jit(solution)/shard_map/ppermute | solution.py:58
  415.6 3.9 grow.13
  422.4 26.9 %attend_back.1 = (bf16[1024,640]{1,0:T(8,128)(2,1)}, bf16[256,2048]{1,0:T(8,128)(2,1)}, bf16[256,2048]{1,0:T(8,128)(2,1)}, bf16[256,2048]{1,0:T(8,128)(2,1)}, bf16[256,2048]{1,0:T(8,128)(2,1)}) custom-call(bf16[1024,2048]{1,0:T(8,128)(2,1)} %get-tuple-element.921.refs_0_, bf16[1024,512]{1,0:T(8,128)(2,1)} %get-tuple-element.922.refs_1_, ...), custom_call_target="tpu_custom_call" | custom-call | tf_op jit(solution)/shard_map/attend_back/pallas_call | solution.py:369
  449.2 11.6 %product.5.refs_0_.refs_1_.term = bf16[2048,1152]{1,0:T(8,128)(2,1)} custom-call(bf16[2048,1024]{1,0:T(8,128)(2,1)} %get-tuple-element.946.refs_0_, bf16[2048,1024]{1,0:T(8,128)(2,1)} %get-tuple-element.947.refs_1_, bf16[1024,640]{1,0:T(8,128)(2,1)} %get-tuple-element.948.refs_2_, bf16[1024,512]{1,0:T(8,128)(2,1)} %get-tuple-element.949.refs_3_), custom_call_target="tpu_custom_call" | custom-call | tf_op jit(solution)/shard_map/product/pallas_call | solution.py:556
  475.3 25.9 %collective-permute-done.59.ahead = bf16[256,2816]{1,0:T(8,128)(2,1)S(1)} collective-permute-done((bf16[256,2816]{1,0:T(8,128)(2,1)}, bf16[256,2816]{1,0:T(8,128)(2,1)S(1)}, u32[]{:S(2)}, u32[]{:S(2)}) %collective-permute-start.59) | collective-permute-done | bytes 1441824 | tf_op jit(solution)/shard_map/ppermute | solution.py:58
  518.8 5.2 norm_back.3
  544.8 10.0 %collective-permute-done.73 = f32[2,2048]{1,0:T(2,128)S(1)} collective-permute-done((f32[2,2048]{1,0:T(2,128)S(1)}, f32[2,2048]{1,0:T(2,128)S(1)}, u32[]{:S(2)}, u32[]{:S(2)}) %collective-permute-start.73) | collective-permute-done | bytes 16416 | tf_op jit(solution)/shard_map/ppermute | solution.py:58
  567.6 4.2 shuffle.7
  571.8 4.1 collective-permute-done.78.ahead
  (354 shorter events, 220.1 us)
Async XLA Ops:
  12.8 28.4 %collective-permute-start.7 = (bf16[256,2176]{1,0:T(8,128)(2,1)S(1)}, bf16[256,2176]{1,0:T(8,128)(2,1)}, u32[]{:S(2)}, u32[]{:S(2)}) collective-permute-start(bf16[256,2176]{1,0:T(8,128)(2,1)S(1)} %pad_maximum_fusion.1.own_ref), channel_id=1, source_target_pairs={{0,2},{1,3},{2,0},{3,1},{4,6},{5,7},{6,4},{7,5},{8,10},{9,11},{10,... | collective-permute-start | bytes 3342344 | tf_op jit(solution)/shard_map/ppermute | solution.py:58
  14.8 26.4 %collective-permute-start.8 = (bf16[256,2176]{1,0:T(8,128)(2,1)S(1)}, bf16[256,2176]{1,0:T(8,128)(2,1)}, u32[]{:S(2)}, u32[]{:S(2)}) collective-permute-start(bf16[256,2176]{1,0:T(8,128)(2,1)S(1)} %pad_maximum_fusion.1.own_ref), channel_id=1, source_target_pairs={{0,1},{1,0},{2,3},{3,2},{4,5},{5,4},{6,7},{7,6},{8,9},{9,8},{10,11... | collective-permute-start | bytes 3342344 | tf_op jit(solution)/shard_map/ppermute | solution.py:58
  42.1 24.8 %collective-permute-start.9 = (bf16[256,2176]{1,0:T(8,128)(2,1)}, bf16[256,2176]{1,0:T(8,128)(2,1)}, u32[]{:S(2)}, u32[]{:S(2)}) collective-permute-start(bf16[256,2176]{1,0:T(8,128)(2,1)} %collective-permute-done.7.pair_ref), channel_id=1, source_target_pairs={{0,1},{1,0},{2,3},{3,2},{4,5},{5,4},{6,7},{7,6},{8,9},{9,8},{10,11... | collective-permute-start | bytes 3342344 | tf_op jit(solution)/shard_map/ppermute | solution.py:58
  72.9 36.6 %collective-permute-start.14 = (bf16[256,2816]{1,0:T(8,128)(2,1)S(1)}, bf16[256,2816]{1,0:T(8,128)(2,1)}, u32[]{:S(2)}, u32[]{:S(2)}) collective-permute-start(bf16[256,2816]{1,0:T(8,128)(2,1)S(1)} %pad_maximum_fusion.refs_1_), channel_id=1, source_target_pairs={{0,8},{8,16},{16,24},{24,28},{28,20},{20,12},{12,4},{4,0},{1,9},{9... | collective-permute-start | bytes 4325384 | tf_op jit(solution)/shard_map/ppermute | solution.py:58
  73.5 36.1 %collective-permute-start.15 = (bf16[256,2816]{1,0:T(8,128)(2,1)S(1)}, bf16[256,2816]{1,0:T(8,128)(2,1)}, u32[]{:S(2)}, u32[]{:S(2)}) collective-permute-start(bf16[256,2816]{1,0:T(8,128)(2,1)S(1)} %pad_maximum_fusion.refs_1_), channel_id=1, source_target_pairs={{8,0},{16,8},{24,16},{28,24},{20,28},{12,20},{4,12},{0,4},{9,1},{1... | collective-permute-start | bytes 4325384 | tf_op jit(solution)/shard_map/ppermute | solution.py:58
  75.1 33.8 %collective-permute-start.16 = (bf16[256,2048]{1,0:T(8,128)(2,1)S(1)}, bf16[256,2048]{1,0:T(8,128)(2,1)}, u32[]{:S(2)}, u32[]{:S(2)}) collective-permute-start(bf16[256,2048]{1,0:T(8,128)(2,1)S(1)} %copy-done.2), channel_id=1, source_target_pairs={{0,2},{1,3},{2,0},{3,1},{4,6},{5,7},{6,4},{7,5},{8,10},{9,11},{10,... | collective-permute-start | bytes 3145736 | tf_op jit(solution)/shard_map/ppermute | solution.py:58
  76.6 32.3 %collective-permute-start.17 = (bf16[256,2048]{1,0:T(8,128)(2,1)S(1)}, bf16[256,2048]{1,0:T(8,128)(2,1)}, u32[]{:S(2)}, u32[]{:S(2)}) collective-permute-start(bf16[256,2048]{1,0:T(8,128)(2,1)S(1)} %copy-done.2), channel_id=1, source_target_pairs={{0,1},{1,0},{2,3},{3,2},{4,5},{5,4},{6,7},{7,6},{8,9},{9,8},{10,11... | collective-permute-start | bytes 3145736 | tf_op jit(solution)/shard_map/ppermute | solution.py:58
  110.0 33.9 %collective-permute-start.22 = (bf16[256,2816]{1,0:T(8,128)(2,1)}, bf16[256,2816]{1,0:T(8,128)(2,1)}, u32[]{:S(2)}, u32[]{:S(2)}) collective-permute-start(bf16[256,2816]{1,0:T(8,128)(2,1)} %collective-permute-done.14.refs_7_), channel_id=1, source_target_pairs={{0,8},{8,16},{16,24},{24,28},{28,20},{20,12},{12,4},{4,0},{1,9},{9... | collective-permute-start | bytes 4325384 | tf_op jit(solution)/shard_map/ppermute | solution.py:58
  110.5 33.6 %collective-permute-start.23 = (bf16[256,2816]{1,0:T(8,128)(2,1)}, bf16[256,2816]{1,0:T(8,128)(2,1)}, u32[]{:S(2)}, u32[]{:S(2)}) collective-permute-start(bf16[256,2816]{1,0:T(8,128)(2,1)} %collective-permute-done.15.refs_2_), channel_id=1, source_target_pairs={{8,0},{16,8},{24,16},{28,24},{20,28},{12,20},{4,12},{0,4},{9,1},{1... | collective-permute-start | bytes 4325384 | tf_op jit(solution)/shard_map/ppermute | solution.py:58
  123.2 25.7 %collective-permute-start.21 = (bf16[256,2048]{1,0:T(8,128)(2,1)}, bf16[256,2048]{1,0:T(8,128)(2,1)}, u32[]{:S(2)}, u32[]{:S(2)}) collective-permute-start(bf16[256,2048]{1,0:T(8,128)(2,1)} %plus.4), channel_id=1, source_target_pairs={{0,2},{1,3},{2,0},{3,1},{4,6},{5,7},{6,4},{7,5},{8,10},{9,11},{10,... | collective-permute-start | bytes 3145736 | tf_op jit(solution)/shard_map/ppermute | solution.py:58
  144.2 32.7 %collective-permute-start.26 = (bf16[256,2816]{1,0:T(8,128)(2,1)}, bf16[256,2816]{1,0:T(8,128)(2,1)S(1)}, u32[]{:S(2)}, u32[]{:S(2)}) collective-permute-start(bf16[256,2816]{1,0:T(8,128)(2,1)} %collective-permute-done.22.refs_6_), channel_id=1, source_target_pairs={{0,8},{8,16},{16,24},{24,28},{28,20},{20,12},{12,4},{4,0},{1,9},{9... | collective-permute-start | bytes 4325384 | tf_op jit(solution)/shard_map/ppermute | solution.py:58
  145.4 32.4 %collective-permute-start.27 = (bf16[256,2816]{1,0:T(8,128)(2,1)}, bf16[256,2816]{1,0:T(8,128)(2,1)S(1)}, u32[]{:S(2)}, u32[]{:S(2)}) collective-permute-start(bf16[256,2816]{1,0:T(8,128)(2,1)} %collective-permute-done.23.refs_3_), channel_id=1, source_target_pairs={{8,0},{16,8},{24,16},{28,24},{20,28},{12,20},{4,12},{0,4},{9,1},{1... | collective-permute-start | bytes 4325384 | tf_op jit(solution)/shard_map/ppermute | solution.py:58
  152.7 25.1 %collective-permute-start.24 = (bf16[256,2048]{1,0:T(8,128)(2,1)}, bf16[256,2048]{1,0:T(8,128)(2,1)}, u32[]{:S(2)}, u32[]{:S(2)}) collective-permute-start(bf16[256,2048]{1,0:T(8,128)(2,1)} %get-tuple-element.691.own_ref), channel_id=1, source_target_pairs={{0,2},{1,3},{2,0},{3,1},{4,6},{5,7},{6,4},{7,5},{8,10},{9,11},{10,... | collective-permute-start | bytes 3145736 | tf_op jit(solution)/shard_map/ppermute | solution.py:58
  153.2 24.6 %collective-permute-start.25 = (bf16[256,2048]{1,0:T(8,128)(2,1)}, bf16[256,2048]{1,0:T(8,128)(2,1)}, u32[]{:S(2)}, u32[]{:S(2)}) collective-permute-start(bf16[256,2048]{1,0:T(8,128)(2,1)} %get-tuple-element.691.own_ref), channel_id=1, source_target_pairs={{0,1},{1,0},{2,3},{3,2},{4,5},{5,4},{6,7},{7,6},{8,9},{9,8},{10,11... | collective-permute-start | bytes 3145736 | tf_op jit(solution)/shard_map/ppermute | solution.py:58
  199.5 22.3 %collective-permute-start.31 = (bf16[256,1408]{1,0:T(8,128)(2,1)S(1)}, bf16[256,1408]{1,0:T(8,128)(2,1)S(1)}, u32[]{:S(2)}, u32[]{:S(2)}) collective-permute-start(bf16[256,1408]{1,0:T(8,128)(2,1)S(1)} %bitcast.39), channel_id=1, source_target_pairs={{0,8},{8,16},{16,24},{24,28},{28,20},{20,12},{12,4},{4,0},{1,9},{9... | collective-permute-start | bytes 2162696 | tf_op jit(solution)/shard_map/ppermute | solution.py:58
  257.8 24.6 %collective-permute-start.39 = (bf16[256,768]{1,0:T(8,128)(2,1)S(1)}, bf16[256,768]{1,0:T(8,128)(2,1)S(1)}, u32[]{:S(2)}, u32[]{:S(2)}) collective-permute-start(bf16[256,768]{1,0:T(8,128)(2,1)S(1)} %slice.87), channel_id=1, source_target_pairs={{0,8},{8,16},{16,24},{24,28},{28,20},{20,12},{12,4},{4,0},{1,9},{9... | collective-permute-start | bytes 1179656 | tf_op jit(solution)/shard_map/ppermute | solution.py:58
  286.3 23.0 %collective-permute-start.41 = (bf16[256,1408]{1,0:T(8,128)(2,1)}, bf16[256,1408]{1,0:T(8,128)(2,1)S(1)}, u32[]{:S(2)}, u32[]{:S(2)}) collective-permute-start(bf16[256,1408]{1,0:T(8,128)(2,1)} %get-tuple-element.790), channel_id=1, source_target_pairs={{0,8},{8,16},{16,24},{24,28},{28,20},{20,12},{12,4},{4,0},{1,9},{9... | collective-permute-start | bytes 2162696 | tf_op jit(solution)/shard_map/ppermute | solution.py:58
  313.7 24.4 %collective-permute-start.43 = (bf16[256,2048]{1,0:T(8,128)(2,1)}, bf16[256,2048]{1,0:T(8,128)(2,1)S(1)}, u32[]{:S(2)}, u32[]{:S(2)}) collective-permute-start(bf16[256,2048]{1,0:T(8,128)(2,1)} %get-tuple-element.803), channel_id=1, source_target_pairs={{0,1},{1,0},{2,3},{3,2},{4,5},{5,4},{6,7},{7,6},{8,9},{9,8},{10,11... | collective-permute-start | bytes 3145736 | tf_op jit(solution)/shard_map/ppermute | solution.py:58
  313.7 24.4 %collective-permute-start.44 = (bf16[256,2048]{1,0:T(8,128)(2,1)}, bf16[256,2048]{1,0:T(8,128)(2,1)S(1)}, u32[]{:S(2)}, u32[]{:S(2)}) collective-permute-start(bf16[256,2048]{1,0:T(8,128)(2,1)} %get-tuple-element.805), channel_id=1, source_target_pairs={{0,1},{1,0},{2,3},{3,2},{4,5},{5,4},{6,7},{7,6},{8,9},{9,8},{10,11... | collective-permute-start | bytes 3145736 | tf_op jit(solution)/shard_map/ppermute | solution.py:58
  341.8 24.8 %collective-permute-start.51 = (bf16[256,2048]{1,0:T(8,128)(2,1)}, bf16[256,2048]{1,0:T(8,128)(2,1)S(1)}, u32[]{:S(2)}, u32[]{:S(2)}) collective-permute-start(bf16[256,2048]{1,0:T(8,128)(2,1)} %plus.5), channel_id=1, source_target_pairs={{0,2},{1,3},{2,0},{3,1},{4,6},{5,7},{6,4},{7,5},{8,10},{9,11},{10,... | collective-permute-start | bytes 3145736 | tf_op jit(solution)/shard_map/ppermute | solution.py:58
  372.6 24.0 %collective-permute-start.54 = (bf16[256,2048]{1,0:T(8,128)(2,1)}, bf16[256,2048]{1,0:T(8,128)(2,1)}, u32[]{:S(2)}, u32[]{:S(2)}) collective-permute-start(bf16[256,2048]{1,0:T(8,128)(2,1)} %get-tuple-element.895.own_ref), channel_id=1, source_target_pairs={{0,2},{1,3},{2,0},{3,1},{4,6},{5,7},{6,4},{7,5},{8,10},{9,11},{10,... | collective-permute-start | bytes 3145736 | tf_op jit(solution)/shard_map/ppermute | solution.py:58
  373.1 23.4 %collective-permute-start.55 = (bf16[256,2048]{1,0:T(8,128)(2,1)}, bf16[256,2048]{1,0:T(8,128)(2,1)}, u32[]{:S(2)}, u32[]{:S(2)}) collective-permute-start(bf16[256,2048]{1,0:T(8,128)(2,1)} %get-tuple-element.895.own_ref), channel_id=1, source_target_pairs={{0,1},{1,0},{2,3},{3,2},{4,5},{5,4},{6,7},{7,6},{8,9},{9,8},{10,11... | collective-permute-start | bytes 3145736 | tf_op jit(solution)/shard_map/ppermute | solution.py:58
  382.4 31.1 %collective-permute-start.52 = (bf16[256,2816]{1,0:T(8,128)(2,1)}, bf16[256,2816]{1,0:T(8,128)(2,1)S(1)}, u32[]{:S(2)}, u32[]{:S(2)}) collective-permute-start(bf16[256,2816]{1,0:T(8,128)(2,1)} %get-tuple-element.884), channel_id=1, source_target_pairs={{0,8},{8,16},{16,24},{24,28},{28,20},{20,12},{12,4},{4,0},{1,9},{9... | collective-permute-start | bytes 4325384 | tf_op jit(solution)/shard_map/ppermute | solution.py:58
  383.3 30.8 %collective-permute-start.53 = (bf16[256,2816]{1,0:T(8,128)(2,1)}, bf16[256,2816]{1,0:T(8,128)(2,1)S(1)}, u32[]{:S(2)}, u32[]{:S(2)}) collective-permute-start(bf16[256,2816]{1,0:T(8,128)(2,1)} %get-tuple-element.886), channel_id=1, source_target_pairs={{8,0},{16,8},{24,16},{28,24},{20,28},{12,20},{4,12},{0,4},{9,1},{1... | collective-permute-start | bytes 4325384 | tf_op jit(solution)/shard_map/ppermute | solution.py:58
  419.5 41.3 %collective-permute-start.57 = (bf16[256,2816]{1,0:T(8,128)(2,1)}, bf16[256,2816]{1,0:T(8,128)(2,1)S(1)}, u32[]{:S(2)}, u32[]{:S(2)}) collective-permute-start(bf16[256,2816]{1,0:T(8,128)(2,1)} %get-tuple-element.912), channel_id=1, source_target_pairs={{0,8},{8,16},{16,24},{24,28},{28,20},{20,12},{12,4},{4,0},{1,9},{9... | collective-permute-start | bytes 4325384 | tf_op jit(solution)/shard_map/ppermute | solution.py:58
  420.4 40.5 %collective-permute-start.58 = (bf16[256,2816]{1,0:T(8,128)(2,1)}, bf16[256,2816]{1,0:T(8,128)(2,1)S(1)}, u32[]{:S(2)}, u32[]{:S(2)}) collective-permute-start(bf16[256,2816]{1,0:T(8,128)(2,1)} %get-tuple-element.914), channel_id=1, source_target_pairs={{8,0},{16,8},{24,16},{28,24},{20,28},{12,20},{4,12},{0,4},{9,1},{1... | collective-permute-start | bytes 4325384 | tf_op jit(solution)/shard_map/ppermute | solution.py:58
  467.5 33.8 %collective-permute-start.59 = (bf16[256,2816]{1,0:T(8,128)(2,1)}, bf16[256,2816]{1,0:T(8,128)(2,1)S(1)}, u32[]{:S(2)}, u32[]{:S(2)}) collective-permute-start(bf16[256,2816]{1,0:T(8,128)(2,1)} %get-tuple-element.961), channel_id=1, source_target_pairs={{0,8},{8,16},{16,24},{24,28},{28,20},{20,12},{12,4},{4,0},{1,9},{9... | collective-permute-start | bytes 4325384 | tf_op jit(solution)/shard_map/ppermute | solution.py:58
  468.4 33.5 %collective-permute-start.60 = (bf16[256,2816]{1,0:T(8,128)(2,1)}, bf16[256,2816]{1,0:T(8,128)(2,1)S(1)}, u32[]{:S(2)}, u32[]{:S(2)}) collective-permute-start(bf16[256,2816]{1,0:T(8,128)(2,1)} %get-tuple-element.963), channel_id=1, source_target_pairs={{8,0},{16,8},{24,16},{28,24},{20,28},{12,20},{4,12},{0,4},{9,1},{1... | collective-permute-start | bytes 4325384 | tf_op jit(solution)/shard_map/ppermute | solution.py:58
  473.8 45.0 %collective-permute-start.65 = (bf16[256,2048]{1,0:T(8,128)(2,1)}, bf16[256,2048]{1,0:T(8,128)(2,1)}, u32[]{:S(2)}, u32[]{:S(2)}) collective-permute-start(bf16[256,2048]{1,0:T(8,128)(2,1)} %plus.6), channel_id=1, source_target_pairs={{0,2},{1,3},{2,0},{3,1},{4,6},{5,7},{6,4},{7,5},{8,10},{9,11},{10,... | collective-permute-start | bytes 3145736 | tf_op jit(solution)/shard_map/ppermute | solution.py:58
  501.9 23.5 %collective-permute-start.63 = (bf16[256,2048]{1,0:T(8,128)(2,1)}, bf16[256,2048]{1,0:T(8,128)(2,1)}, u32[]{:S(2)}, u32[]{:S(2)}) collective-permute-start(bf16[256,2048]{1,0:T(8,128)(2,1)} %get-tuple-element.975), channel_id=1, source_target_pairs={{0,1},{1,0},{2,3},{3,2},{4,5},{5,4},{6,7},{7,6},{8,9},{9,8},{10,11... | collective-permute-start | bytes 3145736 | tf_op jit(solution)/shard_map/ppermute | solution.py:58
  501.9 23.5 %collective-permute-start.64 = (bf16[256,2048]{1,0:T(8,128)(2,1)}, bf16[256,2048]{1,0:T(8,128)(2,1)}, u32[]{:S(2)}, u32[]{:S(2)}) collective-permute-start(bf16[256,2048]{1,0:T(8,128)(2,1)} %get-tuple-element.977), channel_id=1, source_target_pairs={{0,1},{1,0},{2,3},{3,2},{4,5},{5,4},{6,7},{7,6},{8,9},{9,8},{10,11... | collective-permute-start | bytes 3145736 | tf_op jit(solution)/shard_map/ppermute | solution.py:58
  541.7 25.9 %collective-permute-start.68 = (bf16[256,2048]{1,0:T(8,128)(2,1)}, bf16[256,2048]{1,0:T(8,128)(2,1)}, u32[]{:S(2)}, u32[]{:S(2)}) collective-permute-start(bf16[256,2048]{1,0:T(8,128)(2,1)} %plus.7), channel_id=1, source_target_pairs={{0,2},{1,3},{2,0},{3,1},{4,6},{5,7},{6,4},{7,5},{8,10},{9,11},{10,... | collective-permute-start | bytes 3145736 | tf_op jit(solution)/shard_map/ppermute | solution.py:58
  (106 other events, 1015.1 us)

commit v3 on v2

--- a/solution.py
+++ b/solution.py
@@ -59,8 +59,8 @@
 
 
 class RingGather:
-    def __init__(self, line, own, n, split):
-        self.line, self.n, self.split = line, n, split
+    def __init__(self, line, own, n, split, part):
+        self.line, self.n, self.split, self.part = line, n, split, part
         self.chunks = {0: own}
         self.flying = None
 
@@ -79,36 +79,47 @@
             self.chunks[self.n - hop], self.chunks[hop] = ahead, behind
 
     def panel(self):
-        n = self.n
+        n, part = self.n, self.part
         near = [self.chunks[s] for s in range(n) if s != n // 2]
-        if near[0].shape[0] % LANES == 0:
+        if part % LANES == 0:
             return [*near, *self.far]
         far = jnp.concatenate(self.far, axis=1)
-        return [jnp.concatenate([*near[: n // 2], far, *near[n // 2 :]], axis=0)]
+        return [jnp.concatenate([v[:part] for v in (*near[: n // 2], far, *near[n // 2 :])], axis=0)]
+
+    def extra(self, count):
+        n, part = self.n, self.part
+        chunks = [self.far[0] if s == n // 2 else self.chunks[s] for s in range(n)]
+        return jnp.concatenate([c[part : part + count, :part] for c in chunks], axis=1)
 
 
 class RingReduce:
-    def __init__(self, line, product, n, split):
-        self.line, self.product, self.n, self.split = line, product, n, split
+    def __init__(self, line, products, n, split):
+        self.line, self.products, self.n, self.split = line, products, n, split
         self.came = ()
+
+    def grown(self, away):
+        k = len(self.products)
+        return self.line.run(
+            lambda *v: grow(v[:k], v[k:], self.n, away, self.split), *self.products, *self.came
+        )
 
     def start(self, hop):
         n, pairs = self.n, ring_perms(self.n)
-        part = self.product.shape[0] // n
         if hop == 1:
-            far = self.product[n // 2 * part : (n // 2 + 1) * part]
-            ahead, behind = far[:, : self.split], far[:, self.split :]
+            part = self.products[0].shape[0] // n
+            far = [v[n // 2 * part : (n // 2 + 1) * part] for v in self.products]
+            if len(far) == 1:
+                far = [far[0][:, : self.split], far[0][:, self.split :]]
+            ahead, behind = far
         else:
-            ahead, behind = self.line.run(
-                lambda v, *c: grow(v, c, n, n // 2 - hop + 1, self.split), self.product, *self.came
-            )
+            ahead, behind = self.grown(n // 2 - hop + 1)
         self.came = (self.line.send(ahead, "dp", pairs[0]), self.line.send(behind, "dp", pairs[1]))
 
     def wait(self, hop):
         self.came = self.line.passed(*self.came)
 
     def total(self):
-        return self.line.run(lambda v, *c: grow(v, c, self.n, 0, self.split), self.product, *self.came)
+        return self.grown(0)
 
 
 CORE = [(i, i ^ 1) for i in range(4)]
@@ -119,28 +130,35 @@
     def __init__(self, line, own):
         self.line, self.own = line, own
         self.pair = line.send(own, "fsdp", PAIR)
-        self.core = line.send(own, "fsdp", CORE)
 
     def relay(self):
-        self.pair, self.core = self.line.passed(self.pair, self.core)
-        self.diagonal = self.line.send(self.pair, "fsdp", CORE)
+        self.pair = self.line.passed(self.pair)
+        half = self.pair.shape[0] // 2
+        upper = self.line.send(self.pair[:half], "fsdp", CORE)
+        lower = self.line.send(self.pair[half:], "fsdp", CORE)
+        return self.line.passed(upper, lower)
 
     def blocks(self):
-        return [self.own, self.pair, self.core, self.line.passed(self.diagonal)]
+        core = self.line.send(self.own, "fsdp", CORE)
+        upper, lower = self.relay()
+        return [self.own, self.pair, self.line.passed(core), upper, lower]
 
 
 class GroupReduce:
     def __init__(self, line, blocks):
         self.line, self.blocks = line, blocks
-        self.far = line.send(blocks[3], "fsdp", CORE)
-        self.near = line.send(blocks[2], "fsdp", CORE)
+        half = blocks[3].shape[0] // 2
+        self.upper = line.send(blocks[3][:half], "fsdp", CORE)
+        self.lower = line.send(blocks[3][half:], "fsdp", CORE)
 
     def relay(self):
-        far, self.near = self.line.passed(self.far, self.near)
-        self.sent = self.line.send(self.line.run(plus, self.blocks[1], far), "fsdp", PAIR)
+        far = self.line.passed(self.upper, self.lower)
+        self.sent = self.line.send(self.line.run(plus, self.blocks[1], *far), "fsdp", PAIR)
+        self.near = self.line.send(self.blocks[2], "fsdp", CORE)
 
     def terms(self):
-        return self.blocks[0], self.near, self.line.passed(self.sent)
+        self.near, self.sent = self.line.passed(self.near, self.sent)
+        return self.blocks[0], self.near, self.sent
 
 
 def dot(a, b):
@@ -190,13 +208,14 @@
         at += size
 
 
-def pieces_of(panel, split):
+def pieces_of(panel, split, depth):
     if len(panel) == 1:
         chunk = panel[0]
         return [chunk.at[:, :split]], [chunk.at[:, split:]]
-    near, far = panel[:-2], panel[-2:]
-    left = [chunk.at[:, :split] for chunk in near]
-    right = [chunk.at[:, split:] for chunk in near]
+    part = depth // (len(panel) - 1)
+    near, far = panel[:-2], [chunk.at[:part, :] for chunk in panel[-2:]]
+    left = [chunk.at[:part, :split] for chunk in near]
+    right = [chunk.at[:part, split:] for chunk in near]
     at = (len(near) + 1) // 2
     return left[:at] + [far[0]] + left[at:], right[:at] + [far[1]] + right[at:]
 
@@ -228,7 +247,7 @@
     x_ref, gain_ref, cos_ref, sin_ref, col_ref, row_ref = refs[:6]
     turned_ref, q_ref, kv_ref, o_ref, lse_ref = refs[6 + count : 11 + count]
     branch_refs, qkv_ref = refs[11 + count : 15 + count], refs[15 + count]
-    q_chunks, o_chunks = pieces_of(refs[6 : 6 + count], qkv_ref.shape[1])
+    q_chunks, o_chunks = pieces_of(refs[6 : 6 + count], qkv_ref.shape[1], gain_ref.shape[1])
     depth = gain_ref.shape[1]
     rows, width = q_ref.shape
     pairs = width // LANES
@@ -311,14 +330,25 @@
     )(x, gain, cosine, sine, column, row, *panel)
 
 
-def attention_backward(count, *refs):
-    dh_ref, q_ref, kv_ref, lse_ref, cos_ref, sin_ref, col_ref, row_ref = refs[:8]
-    grad_ref, part_refs, do_ref = refs[8 + count], refs[9 + count : 13 + count], refs[13 + count]
-    q_chunks, o_chunks = pieces_of(refs[8 : 8 + count], grad_ref.shape[1])
+def attention_backward(sizes, count, *refs):
+    dh_refs, refs = refs[: sum(sizes)], refs[sum(sizes) :]
+    q_ref, kv_ref, lse_ref, cos_ref, sin_ref, col_ref, row_ref = refs[:7]
+    panel, refs = refs[7 : 7 + count], refs[-len(sizes) - 2 :]
+    grad_ref, part_refs, do_ref = refs[0], refs[1:-1], refs[-1]
+    q_chunks, o_chunks = pieces_of(panel, grad_ref.shape[1], dh_refs[0].shape[1])
     rows, width = q_ref.shape
     pairs = width // LANES
     scale = HEAD_DIM ** -0.5
-    do_ref[...] = times_chunks(dh_ref, o_chunks).astype(LOW)
+    for block, size in enumerate(sizes):
+
+        @pl.when(pl.program_id(0) == block)
+        def _(mine=dh_refs[sum(sizes[:block]) : sum(sizes[: block + 1])]):
+            at = 0
+            for ref in mine:
+                end = at + ref.shape[0]
+                do_ref[at:end, :] = times_chunks(ref, o_chunks).astype(LOW)
+                at = end
+
     cosine, sine = cos_ref[...], sin_ref[...]
     lanes = lane_ids(rows, LANES)
     even = lanes < HEAD_DIM
@@ -363,73 +393,96 @@
             into_chunks(part_ref, [grad_ref[...]], [q_chunks])
 
 
-def attend_back(grads, query, keyval, log_sums, cosine, sine, column, row, panel, rows):
-    total, depth = grads.shape
-    width = query.shape[1]
+def attend_back(blocks, groups, query, keyval, log_sums, cosine, sine, column, row, panel, rows, before=None):
+    total, width = query.shape
+    depth = groups[0][0].shape[1]
+    first, step = blocks[0], blocks[1] - blocks[0]
+    flat = [v for group in groups for v in group]
+
+    def chosen(wide):
+        return pl.BlockSpec((rows, wide), lambda i: (first + step * i, 0))
+
+    operands = [*flat, query, keyval, log_sums, cosine, sine, column, row, *panel]
+    in_specs = [whole(v) for v in flat]
+    in_specs += [chosen(width), chosen(LANES), chosen(LANES), chosen(LANES), chosen(LANES), chosen(1)]
+    in_specs += [pl.BlockSpec((1, 1, rows), lambda i: (first + step * i, 0, 0))]
+    in_specs += [whole(v) for v in panel]
+    aliases = {}
+    if before is not None:
+        aliases = {len(operands): 0}
+        operands.append(before)
+        in_specs.append(pl.BlockSpec(memory_space=pl.ANY))
     return pl.pallas_call(
-        functools.partial(attention_backward, len(panel)),
-        grid=(total // rows,),
-        in_specs=[
-            by_rows(rows, depth),
-            by_rows(rows, width),
-            by_rows(rows, LANES),
-            by_rows(rows, LANES),
-            by_rows(rows, LANES),
-            by_rows(rows, LANES),
-            by_rows(rows, 1),
-            pl.BlockSpec((1, 1, rows), lambda i: (i, 0, 0)),
-        ]
-        + [whole(v) for v in panel],
-        out_specs=[by_rows(rows, width + LANES)] + [fixed(rows, depth)] * 4,
-        out_shape=[shaped((total, width + LANES), LOW)] + [shaped((rows, depth), LOW)] * 4,
+        functools.partial(attention_backward, [len(group) for group in groups], len(panel)),
+        grid=(len(groups),),
+        in_specs=in_specs,
+        out_specs=[chosen(width + LANES)] + [fixed(rows, depth)] * len(groups),
+        out_shape=[shaped((total, width + LANES), LOW)] + [shaped((rows, depth), LOW)] * len(groups),
         scratch_shapes=[pltpu.VMEM((rows, width), LOW)],
+        input_output_aliases=aliases,
         name="attend_back",
-    )(grads, query, keyval, log_sums, cosine, sine, column, row, *panel)
-
-
-def plus_kernel(a_ref, b_ref, out_ref):
-    out_ref[...] = a_ref[...] + b_ref[...]
-
-
-def plus(a, b):
-    rows, depth = a.shape
-    step = rows // 2
+    )(*operands)
+
+
+def plus_kernel(value_ref, upper_ref, lower_ref, out_ref):
+    rows = upper_ref.shape[0]
+    out_ref[:rows, :] = value_ref[:rows, :] + upper_ref[...]
+    out_ref[rows:, :] = value_ref[rows:, :] + lower_ref[...]
+
+
+def plus(value, upper, lower):
+    rows, depth = value.shape
+    step = depth // 2
+
+    def columns(size):
+        return pl.BlockSpec((size, step), lambda i: (0, i))
+
     return pl.pallas_call(
         plus_kernel,
         grid=(2,),
-        in_specs=[by_rows(step, depth)] * 2,
-        out_specs=by_rows(step, depth),
-        out_shape=shaped(a.shape, a.dtype),
+        in_specs=[columns(rows), columns(rows // 2), columns(rows // 2)],
+        out_specs=columns(rows),
+        out_shape=shaped(value.shape, value.dtype),
         name="plus",
-    )(a, b)
-
-
-def gathered_kernel(own_ref, pair_ref, core_ref, diagonal_ref, all_ref, turned_ref=None):
-    for block, ref in enumerate((own_ref, pair_ref, core_ref, diagonal_ref)):
+    )(value, upper, lower)
+
+
+def gathered_kernel(with_all, own, pair, core, upper, lower, *outs):
+    all_ref = outs[0] if with_all else None
+    turned_ref = outs[-1] if len(outs) == 2 or not with_all else None
+    for block, refs in enumerate(((own,), (pair,), (core,), (upper, lower))):
 
         @pl.when(pl.program_id(0) == block)
-        def _(ref=ref):
-            value = ref[...]
-            all_ref[...] = value
-            if turned_ref is not None:
-                turned_ref[...] = value.T
-
-
-def gathered(blocks, with_turned):
+        def _(refs=refs):
+            at = 0
+            for ref in refs:
+                value = ref[...]
+                end = at + value.shape[0]
+                if all_ref is not None:
+                    all_ref[at:end, :] = value
+                if turned_ref is not None:
+                    turned_ref[:, at:end] = value.T
+                at = end
+
+
+def gathered(blocks, with_all=True, with_turned=True):
     rows, depth = blocks[0].shape
-    out_specs, out_shape = [by_rows(rows, depth)], [shaped((4 * rows, depth), LOW)]
+    out_specs, out_shape = [], []
+    if with_all:
+        out_specs.append(by_rows(rows, depth))
+        out_shape.append(shaped((4 * rows, depth), LOW))
     if with_turned:
         out_specs.append(pl.BlockSpec((depth, rows), lambda i: (0, i)))
         out_shape.append(shaped((depth, 4 * rows), LOW))
     out = pl.pallas_call(
-        gathered_kernel,
+        functools.partial(gathered_kernel, with_all),
         grid=(4,),
         in_specs=[whole(v) for v in blocks],
         out_specs=out_specs,
         out_shape=out_shape,
         name="gathered",
     )(*blocks)
-    return tuple(out) if with_turned else out[0]
+    return tuple(out) if len(out) == 2 else out[0]
 
 
 def added(refs):
@@ -461,7 +514,7 @@
 def feed_kernel(count, *refs):
     x_ref = refs[0]
     act_ref, slope_ref, silu_ref = refs[1 + count :]
-    g_chunks, u_chunks = pieces_of(refs[1 : 1 + count], act_ref.shape[1])
+    g_chunks, u_chunks = pieces_of(refs[1 : 1 + count], act_ref.shape[1], x_ref.shape[1])
     gate = times_chunks(x_ref, g_chunks)
     up = times_chunks(x_ref, u_chunks)
     sigmoid = 1.0 / (1.0 + jnp.exp(-gate))
@@ -489,7 +542,7 @@
     (out_ref,) = refs[3 + count :]
     wide = slope_ref.shape[1]
     at = 0
-    for chunks in pieces_of(refs[3 : 3 + count], split):
+    for chunks in pieces_of(refs[3 : 3 + count], split, dy_ref.shape[1]):
         end = at + chunks[0].shape[1]
         grads = times_chunks(dy_ref, chunks)
         out_ref[:, at:end] = (grads * slope_ref[:, at:end].astype(WIDE)).astype(LOW)
@@ -514,7 +567,7 @@
 
 def spread_kernel(count, split, *refs):
     value, out_refs = refs[0], refs[1 + count :]
-    left, right = pieces_of(refs[1 : 1 + count], split)
+    left, right = pieces_of(refs[1 : 1 + count], split, out_refs[0].shape[1])
     rows = out_refs[0].shape[0]
     each = value.shape[0] // rows
     for block, out_ref in enumerate(out_refs):
@@ -540,73 +593,82 @@
     )(value, *panel)
 
 
-def product_kernel(count, *refs):
-    out_ref = refs[-1]
-    at = 0
-    for left, right in zip(refs[:count], refs[count : 2 * count]):
-        end = at + right.shape[1]
-        out_ref[:, at:end] = dot(left[...], right[...]).astype(LOW)
-        at = end
-
-
-def product(lefts, rights):
-    depth, total = lefts[0].shape
-    wide = sum(v.shape[1] for v in rights)
+def product_kernel(left, right, out):
+    out[...] = dot(left[...], right[...]).astype(LOW)
+
+
+def product(left, right):
+    depth, total = left.shape
+    wide = right.shape[1]
     step = depth // 8
     return pl.pallas_call(
-        functools.partial(product_kernel, len(lefts)),
+        product_kernel,
         grid=(8,),
-        in_specs=[by_rows(step, total) for _ in lefts] + [whole(v) for v in rights],
+        in_specs=[by_rows(step, total), whole(right)],
         out_specs=by_rows(step, wide),
         out_shape=shaped((depth, wide), LOW),
         name="product",
-    )(*lefts, *rights)
-
-
-def grow_kernel(split, narrow, *refs):
-    ahead_term, behind_term, ahead, behind, ahead_out, behind_out = refs
-    if narrow:
-        ahead_out[:, :split] = ahead_term[:, :split] + ahead[...]
-        ahead_out[:, split:] = ahead_term[:, split:]
-        behind_out[:, :split] = behind_term[:, :split]
-        behind_out[:, split:] = behind_term[:, split:] + behind[...]
-    else:
-        ahead_out[...] = ahead_term[...] + ahead[...]
-        behind_out[...] = behind_term[...] + behind[...]
-
-
-def last_kernel(term, ahead, behind, out):
-    out[...] = term[...].astype(WIDE) + ahead[...].astype(WIDE) + behind[...].astype(WIDE)
-
-
-def grow(product, came, n, away, split):
-    part, wide = product.shape[0] // n, product.shape[1]
+    )(left, right)
+
+
+def grow_kernel(split, narrow, count, *refs):
+    ahead_terms, behind_terms = refs[:count], refs[count : 2 * count]
+    ahead, behind, ahead_out, behind_out = refs[2 * count :]
+    at = 0
+    for ahead_term, behind_term in zip(ahead_terms, behind_terms):
+        width = ahead_term.shape[1]
+        cuts = [0, split - at, width] if at < split < at + width else [0, width]
+        for low, high in zip(cuts[:-1], cuts[1:]):
+            start, end = at + low, at + high
+            first, second = ahead_term[:, low:high], behind_term[:, low:high]
+            if not narrow or end <= split:
+                first = first + ahead[:, start:end]
+            if not narrow:
+                second = second + behind[:, start:end]
+            elif start >= split:
+                second = second + behind[:, start - split : end - split]
+            ahead_out[:, start:end] = first
+            behind_out[:, start:end] = second
+        at += width
+
+
+def last_kernel(count, *refs):
+    ahead, behind, out = refs[count:]
+    at = 0
+    for term in refs[:count]:
+        end = at + term.shape[1]
+        out[:, at:end] = term[...].astype(WIDE) + ahead[:, at:end].astype(WIDE) + behind[:, at:end].astype(WIDE)
+        at = end
+
+
+def grow(products, came, n, away, split):
+    part = products[0].shape[0] // n
+    wide = sum(v.shape[1] for v in products)
     narrow = away == n // 2 - 1
     step = part // 2
-    sizes = [v.shape[1] for v in came]
-    came_specs = [by_rows(step, size) for size in sizes]
+    came_specs = [by_rows(step, v.shape[1]) for v in came]
 
     def rows_at(offset):
-        return pl.BlockSpec((step, wide), lambda i: (2 * offset + i, 0))
+        return [pl.BlockSpec((step, v.shape[1]), lambda i: (2 * offset + i, 0)) for v in products]
 
     if away == 0:
         return pl.pallas_call(
-            last_kernel,
+            functools.partial(last_kernel, len(products)),
             grid=(2,),
-            in_specs=[rows_at(0)] + came_specs,
+            in_specs=rows_at(0) + came_specs,
             out_specs=by_rows(step, wide),
             out_shape=shaped((part, wide), WIDE),
             name="last",
-        )(product, *came)
+        )(*products, *came)
     return tuple(
         pl.pallas_call(
-            functools.partial(grow_kernel, split, narrow),
+            functools.partial(grow_kernel, split, narrow, len(products)),
             grid=(2,),
-            in_specs=[rows_at(away), rows_at(n - away)] + came_specs,
+            in_specs=rows_at(away) + rows_at(n - away) + came_specs,
             out_specs=[by_rows(step, wide)] * 2,
             out_shape=[shaped((part, wide), LOW)] * 2,
             name="grow",
-        )(product, product, *came)
+        )(*products, *products, *came)
     )
 
 
@@ -706,38 +768,26 @@
     heads_wide, hidden_wide = w_query.shape[1], w_gate.shape[1]
     qkv_wide = heads_wide + w_key.shape[1] + w_value.shape[1]
     split = -(-hidden_wide // (2 * LANES)) * LANES
-    attn = RingGather(line, jnp.concatenate([w_query, w_key, w_value, w_out.T], axis=1).astype(LOW), n, qkv_wide)
-    feedw = RingGather(line, jnp.concatenate([w_gate, w_up], axis=1).astype(LOW), n, hidden_wide)
-    down = RingGather(line, w_down.T.astype(LOW), n, split)
+    attn_own = jnp.concatenate([w_query, w_key, w_value, w_out.T], axis=1).astype(LOW)
+    gains = jnp.stack([gain_attn, gain_mlp]).astype(LOW)
+    gains = jnp.pad(gains, ((0, 14), (0, attn_own.shape[1] - part)))
+    attn = RingGather(line, jnp.concatenate([attn_own, gains], axis=0), n, qkv_wide, part)
+    feedw = RingGather(line, jnp.concatenate([w_gate, w_up], axis=1).astype(LOW), n, hidden_wide, part)
+    down = RingGather(line, w_down.T.astype(LOW), n, split, part)
 
     attn.start(1)
     own_tokens = shuffle(sources, n, tokens)
     marks = jnp.broadcast_to(segments.astype(LOW)[:, None], (rows, LANES))
     x = GroupGather(line, jnp.concatenate([own_tokens, marks], axis=1))
-    gains = jnp.stack([gain_attn, gain_mlp]).astype(LOW)
-    bits = [1 << i for i in range((n - 1).bit_length())]
-
-    def gains_from(value, bit):
-        other = lax.ppermute(value, "dp", [(i, i ^ bit) for i in range(n)])
-        return jnp.concatenate([value, other], axis=1)
-
-    gains = gains_from(gains, bits[0])
     attn.wait(1)
     attn.start(2)
-    for bit in bits[1:-1]:
-        gains = gains_from(line.passed(gains), bit)
     own_grads = line.run(lambda *v: shuffle(v[0], n, v[1]), sources, cotangent)
     for hop in range(2, hops - 1):
         attn.wait(hop)
         attn.start(hop + 1)
-    gains = gains_from(line.passed(gains), bits[-1])
-    x.relay()
     attn.wait(hops - 1)
     attn.start(hops)
-    token_rows = line.run(lambda *v: gathered(v, False), *x.blocks())
-    gains = jnp.take(gains.reshape(2, n, part), sources ^ me, axis=1).reshape(2, depth).astype(WIDE)
-    gains = line.passed(gains)
-    gain_one, gain_two = gains[0:1], gains[1:2]
+    token_rows = line.run(lambda *v: gathered(v, with_turned=False), *x.blocks())
     attn.wait(hops)
     feedw.start(1)
     y = GroupGather(line, own_grads)
@@ -745,17 +795,18 @@
     column, row = segment_blocks.reshape(-1, 1), segment_blocks[:, None, :]
     cosine, sine = line.run(lambda v: jax.vmap(tables)(v), segment_blocks)
     cosine, sine = cosine.reshape(-1, LANES), sine.reshape(-1, LANES)
+    gains = attn.extra(2).astype(WIDE)
+    gain_one, gain_two = gains[0:1], gains[1:2]
 
     attn_panel = attn.panel()
     normed_turned, query, keyval, mixed, log_sums, *branch = line.run(
         lambda *v: attend(*v[:6], v[6:], heads_wide, rows),
         token_rows, gain_one, cosine, sine, column, row, *attn_panel,
     )
-    y.relay()
     feedw.wait(1)
     feedw.start(2)
     branch = GroupReduce(line, branch)
-    grads_all, grads_turned = line.run(lambda *v: gathered(v, True), *y.blocks())
+    grads_all, grads_turned = line.run(lambda *v: gathered(v), *y.blocks())
     branch.relay()
     for hop in range(2, hops - 1):
         feedw.wait(hop)
@@ -764,8 +815,7 @@
     z = GroupGather(line, normed_own)
     feedw.wait(hops - 1)
     feedw.start(hops)
-    z.relay()
-    normed_mlp, mlp_turned = line.run(lambda *v: gathered(v, True), *z.blocks())
+    normed_mlp, mlp_turned = line.run(lambda *v: gathered(v), *z.blocks())
 
     feedw.wait(hops)
     down.start(1)
@@ -775,88 +825,113 @@
         down.wait(hop)
         down.start(hop + 1)
         if hop == 1:
-            down_terms = line.run(lambda a, b: product([a], [b]), grads_turned, activation)
-            r_down = RingReduce(line, down_terms, n, split)
+            down_terms = line.run(lambda a, b: product(a, b), grads_turned, activation)
+            r_down = RingReduce(line, [down_terms], n, split)
     r_down.start(1)
     down.wait(hops)
     down_panel = down.panel()
+    r_down.wait(1)
+    r_down.start(2)
 
     grad_feed = line.run(
         lambda a, b, c, *v: feed_back(a, b, c, v, split), grads_all, slope, silu, *down_panel
     )
-    for hop in range(1, hops - 2):
+    for hop in range(2, hops - 1):
         r_down.wait(hop)
         r_down.start(hop + 1)
-    grad_normed = line.run(lambda a, *v: spread(a, v, hidden_wide, rows), grad_feed, *feed_panel)
-    r_down.wait(hops - 2)
-    r_down.start(hops - 1)
-    grad_normed = GroupReduce(line, grad_normed)
-    feed_terms = line.run(lambda a, b: product([a], [b]), mlp_turned, grad_feed)
+    feed_terms = line.run(lambda a, b: product(a, b), mlp_turned, grad_feed)
+    r_feed = RingReduce(line, [feed_terms], n, hidden_wide)
     r_down.wait(hops - 1)
     r_down.start(hops)
+    r_feed.start(1)
+    grad_normed = line.run(lambda a, *v: spread(a, v, hidden_wide, rows), grad_feed, *feed_panel)
+    r_down.wait(hops)
+    r_feed.wait(1)
+    r_feed.start(2)
+    grad_normed = GroupReduce(line, grad_normed)
     grad_normed.relay()
+    grad_down = r_down.total()
     layer_part = line.run(lambda a, *v: spread(a, v, split, rows), activation, *down_panel)
-    r_down.wait(hops)
-    r_feed = RingReduce(line, feed_terms, n, hidden_wide)
-    r_feed.start(1)
-    grad_down = r_down.total()
+    for hop in range(2, hops - 1):
+        r_feed.wait(hop)
+        r_feed.start(hop + 1)
     grad_hidden, grad_branch, gain_mlp_terms = line.run(
         norm_back, hidden, gain_two, own_grads, *grad_normed.terms()
     )
     b = GroupGather(line, grad_branch)
-    r_feed.wait(1)
-    r_feed.start(2)
-    b.relay()
-    branch_grads, branch_turned = line.run(lambda *v: gathered(v, True), *b.blocks())
-    for hop in range(2, hops - 1):
-        r_feed.wait(hop)
-        r_feed.start(hop + 1)
-
-    grad_qkv, *grad_input_part = line.run(
-        lambda *v: attend_back(*v[:8], v[8:], rows),
-        branch_grads, query, keyval, log_sums, cosine, sine, column, row, *attn_panel,
-    )
-    attn_terms = line.run(
-        lambda *v: product(v[:2], v[2:]), normed_turned, branch_turned, grad_qkv, mixed
-    )
+    b_core = line.passed(line.send(b.own, "fsdp", CORE))
+    extras = (query, keyval, log_sums, cosine, sine, column, row)
+
+    def backward(blocks, groups, before=None):
+        sizes = [len(group) for group in groups]
+        flat = [v for group in groups for v in group]
+        k = len(flat)
+
+        def work(*v):
+            split_groups = [v[sum(sizes[:i]) : sum(sizes[: i + 1])] for i in range(len(sizes))]
+            last = len(v) if before is None else len(v) - 1
+            return attend_back(
+                blocks, split_groups, *v[k : k + 7], v[k + 7 : last], rows, None if before is None else v[-1]
+            )
+
+        return line.run(work, *flat, *extras, *attn_panel, *([] if before is None else [before]))
+
+    grad_qkv, own, core = backward((0, 2), [[b.own], [b_core]])
     r_feed.wait(hops - 1)
     r_feed.start(hops)
-    grad_input_sum = GroupReduce(line, grad_input_part)
+    upper, lower = b.relay()
+    grad_qkv, pair, diagonal = backward((1, 3), [[b.pair], [upper, lower]], grad_qkv)
+    grad_input_sum = GroupReduce(line, [own, pair, core, diagonal])
     grad_input_sum.relay()
-    r_attn = RingReduce(line, attn_terms, n, qkv_wide)
+    branch_turned = line.run(
+        lambda *v: gathered(v, with_all=False), b.own, b.pair, b_core, upper, lower
+    )
+    out_terms = line.run(product, branch_turned, mixed)
+    attn_terms = line.run(product, normed_turned, grad_qkv)
+    r_attn = RingReduce(line, [attn_terms, out_terms], n, qkv_wide)
     r_feed.wait(hops)
     r_attn.start(1)
-    layer_sum = GroupReduce(line, layer_part)
     grad_w_feed = r_feed.total()
     r_attn.wait(1)
     r_attn.start(2)
     _, grad_tokens, gain_attn_terms = line.run(
         norm_back, own_tokens, gain_one, grad_hidden, *grad_input_sum.terms()
     )
-    layer_sum.relay()
     gain_terms = jnp.concatenate([gain_attn_terms, gain_mlp_terms], axis=0).reshape(2, n, part)
     gain_terms = jnp.take(gain_terms, offsets, axis=1).reshape(2, depth)
-    gain_steps = [("fsdp", 4, 1), ("fsdp", 4, 2)] + [("dp", n, bit) for bit in bits]
-
-    def gain_step(value, step):
-        axis, size, bit = step
-        other = line.passed(line.send(value, axis, [(i, i ^ bit) for i in range(size)]))
-        return line.run(jnp.add, value, other)
-
-    for step in gain_steps[:2]:
-        gain_terms = gain_step(gain_terms, step)
-    grad_tokens = line.run(lambda at, v: shuffle(at, n, v), offsets, grad_tokens)
-    for hop in range(2, hops):
+    gain_steps = [("fsdp", 4, 1), ("fsdp", 4, 2)] + [("dp", n, 1 << i) for i in range((n - 1).bit_length())]
+    flying = []
+
+    def gain_send():
+        if gain_steps:
+            axis, size, bit = gain_steps.pop(0)
+            flying.append(line.send(gain_terms, axis, [(i, i ^ bit) for i in range(size)]))
+
+    def gain_take(value):
+        return line.run(jnp.add, value, line.passed(flying.pop())) if flying else value
+
+    for _ in range(2):
+        gain_send()
+        gain_terms = gain_take(gain_terms)
+    for hop in range(2, hops - 1):
         r_attn.wait(hop)
         r_attn.start(hop + 1)
-        for step in gain_steps[2 * hop - 2 : 2 * hop]:
-            gain_terms = gain_step(gain_terms, step)
-    for step in gain_steps[2 * hops - 2 :]:
-        gain_terms = gain_step(gain_terms, step)
+    gain_send()
+    layer_sum = GroupReduce(line, layer_part)
+    layer_sum.relay()
+    grad_tokens = line.run(lambda at, v: shuffle(at, n, v), offsets, grad_tokens)
+    r_attn.wait(hops - 1)
+    r_attn.start(hops)
+    while len(gain_steps) > 1:
+        gain_terms = gain_take(gain_terms)
+        gain_send()
     layer_own = line.run(lambda at, *v: shuffle(at, n, *v), offsets, hidden, *layer_sum.terms())
+    r_attn.wait(hops)
+    while flying:
+        gain_terms = gain_take(gain_terms)
+        gain_send()
+    grad_attn = r_attn.total()
     gain_own = lax.dynamic_slice(gain_terms, (0, me * part), (2, part))
-    r_attn.wait(hops)
-    grad_attn = r_attn.total()
 
     value_at = heads_wide + w_key.shape[1]
     return (

time: 591 us -> 568 us (0.961)
  waiting for transfers between devices: 194 us -> 157 us
  Pallas kernels: 250 us -> 259 us
  local copies, waits for them, and re-layouts: 49.3 us -> 56.2 us
    ppermute x3 -> x0, waiting for transfers between devices: 22.8 us -> none  [gains_from(): other = lax.ppermute(value, 'dp', [(i, i ^ bit) for i in range(n)])]
    ppermute x77 -> x85, waiting for transfers between devices: 171 us -> 157 us  [send(): return lax.ppermute(self.after(value), axis, pairs)]
    pallas_call x24 -> x26, Pallas kernels: 137 us -> 145 us  [the longest x4 46 us: product(): pl.pallas_call(product_kernel, grid=(8,), in_specs=[by_rows(step, total),...]
    slice x5 -> x13, local copies, waits for them, and re-layouts: 7.75 us -> 14 us  [the longest x3 4.56 us: start(): far = [far[0][:, :self.split], far[0][:, self.split:]]]
    ppermute x77 -> x85, starting transfers between devices: 66.6 us -> 71 us  [send(): return lax.ppermute(self.after(value), axis, pairs)]
    unnamed x122 -> x140, local copies, waits for them, and re-layouts: 26.1 us -> 27.5 us
  transfers between devices with their start and end apart: 80 -> 85, of which waited for: 39 -> 40; matrix products, arithmetic and copies ran while one was open for 7% -> 8% of each run, Pallas kernels for 39% -> 43%
where the time goes in v3:
time: 568 us; the launch traced here: 563 us
  Pallas kernels  259 us (46%)
  waiting for transfers between devices  157 us (28%)
  starting transfers between devices  71 us (12%)
  local copies, waits for them, and re-layouts  56.2 us (10%)
  other arithmetic  18.1 us (3%)
    ppermute x85, waiting for transfers between devices, send(): return lax.ppermute(self.after(value), axis, pairs)  157 us
    ppermute x85, starting transfers between devices, send(): return lax.ppermute(self.after(value), axis, pairs)  71 us
    pallas_call x4, Pallas kernels, product(): pl.pallas_call(product_kernel, grid=(8,), in_specs=[by_rows(step, total),...  46 us
    pallas_call x2, Pallas kernels, spread(): pl.pallas_call(functools.partial(spread_kernel, n, split), grid=(4,), in_...  33 us
    pallas_call x2, Pallas kernels, attend_back(): pl.pallas_call(functools.partial(attention_backward, [len(group) for grou...  31.9 us
    unnamed x140, local copies, waits for them, and re-layouts  27.5 us
    pallas_call x9, Pallas kernels, grow(): pl.pallas_call(functools.partial(grow_kernel, split, narrow, len(products...  26.7 us
    pallas_call x4, Pallas kernels, gathered(): pl.pallas_call(functools.partial(gathered_kernel, with_all), grid=(4,), i...  22.8 us
  transfers between devices with their start and end apart: 85, of which 40 were waited for; matrix products, arithmetic and copies ran while one was open for 8% of the time, Pallas kernels for 43%

profile of v3, /device:TPU:0, one launch (start us, length us, event | category | flops | bytes accessed | tf_op | source)
XLA Modules:
  0.0 562.7 jit_solution(5365108491275821295)
XLA Ops:
  12.7 10.0 %collective-permute-done.refs_12_.refs_15_.refs_16_ = bf16[272,1152]{1,0:T(8,128)(2,1)S(1)} collective-permute-done((bf16[272,1152]{1,0:T(8,128)(2,1)S(1)}, bf16[272,1152]{1,0:T(8,128)(2,1)S(1)}, u32[]{:S(2)}, u32[]{:S(2)}) %collective-permute-start) | collective-permute-done | bytes 626720 | tf_op jit(solution)/shard_map/ppermute | solution.py:58
  33.1 6.0 %collective-permute-done.2.refs_11_.refs_14_.refs_15_ = bf16[272,1152]{1,0:T(8,128)(2,1)} collective-permute-done((bf16[272,1152]{1,0:T(8,128)(2,1)S(1)}, bf16[272,1152]{1,0:T(8,128)(2,1)}, u32[]{:S(2)}, u32[]{:S(2)}) %collective-permute-start.2) | collective-permute-done | bytes 626720 | tf_op jit(solution)/shard_map/ppermute | solution.py:58
  44.1 10.0 %collective-permute-done.4.refs_10_.refs_13_.refs_14_ = bf16[272,1152]{1,0:T(8,128)(2,1)S(1)} collective-permute-done((bf16[272,1152]{1,0:T(8,128)(2,1)}, bf16[272,1152]{1,0:T(8,128)(2,1)S(1)}, u32[]{:S(2)}, u32[]{:S(2)}) %collective-permute-start.4) | collective-permute-done | bytes 626720 | tf_op jit(solution)/shard_map/ppermute | solution.py:58
  61.7 4.8 gathered.4.refs_0_
  83.2 21.2 %attend.1 = (bf16[2048,1024]{1,0:T(8,128)(2,1)}, bf16[1024,512]{1,0:T(8,128)(2,1)}, bf16[1024,128]{1,0:T(8,128)(2,1)}, bf16[1024,512]{1,0:T(8,128)(2,1)}, f32[10...) custom-call(bf16[1024,2176]{1,0:T(8,128)(2,1)} %gathered.4.refs_0_, ...), custom_call_target="tpu_custom_call" | custom-call | tf_op jit(solution)/shard_map/attend/pallas_call | solution.py:300
  112.1 6.4 %gathered.5 = (bf16[1024,2048]{1,0:T(8,128)(2,1)}, bf16[2048,1024]{1,0:T(8,128)(2,1)}) custom-call(bf16[256,2048]{1,0:T(8,128)(2,1)} %shuffle.5.own.rest_ref, bf16[256,2048]{1,0:T(8,128)(2,1)} %collective-permute-done.16.pair, bf16[256,2048]{1,0:T(8,128)(2,1)} %copy-done.35, bf16[128,2048]{1,0:T(8,128)(2,1)} %copy-done.54, bf16[128,2048]{1,0:T(8,128)(2,1)} %copy-done.55), custom_call_target="tpu_custom_call" | custom-call | tf_op jit(solution)/shard_map/gathered/pallas_call | solution.py:477
  122.1 18.5 %collective-permute-done.22.refs_6_ = bf16[256,2816]{1,0:T(8,128)(2,1)S(1)} collective-permute-done((bf16[256,2816]{1,0:T(8,128)(2,1)}, bf16[256,2816]{1,0:T(8,128)(2,1)S(1)}, u32[]{:S(2)}, u32[]{:S(2)}) %collective-permute-start.22) | collective-permute-done | bytes 1441824 | tf_op jit(solution)/shard_map/ppermute | solution.py:58
  146.9 3.9 join.1
  151.9 23.3 %collective-permute-done.25.refs_5_ = bf16[256,2816]{1,0:T(8,128)(2,1)S(1)} collective-permute-done((bf16[256,2816]{1,0:T(8,128)(2,1)}, bf16[256,2816]{1,0:T(8,128)(2,1)S(1)}, u32[]{:S(2)}, u32[]{:S(2)}) %collective-permute-start.25) | collective-permute-done | bytes 1441824 | tf_op jit(solution)/shard_map/ppermute | solution.py:58
  183.8 6.3 %gathered.6 = (bf16[1024,2048]{1,0:T(8,128)(2,1)}, bf16[2048,1024]{1,0:T(8,128)(2,1)}) custom-call(bf16[256,2048]{1,0:T(8,128)(2,1)} %get-tuple-element.754.own, bf16[256,2048]{1,0:T(8,128)(2,1)} %copy-done.16, bf16[256,2048]{1,0:T(8,128)(2,1)} %collective-permute-done.27.core, bf16[128,2048]{1,0:T(8,128)(2,1)} %copy-done.56, bf16[128,2048]{1,0:T(8,128)(2,1)} %copy-done.57), custom_call_target="tpu_custom_call" | custom-call | tf_op jit(solution)/shard_map/gathered/pallas_call | solution.py:477
  190.2 5.5 collective-permute-done.30.refs_8_
  199.4 20.2 %feed.1 = (bf16[1024,1408]{1,0:T(8,128)(2,1)}, bf16[1024,1408]{1,0:T(8,128)(2,1)}, bf16[1024,1408]{1,0:T(8,128)(2,1)}) custom-call(bf16[1024,2048]{1,0:T(8,128)(2,1)} %get-tuple-element.770.refs_0_, bf16[256,2816]{1,0:T(8,128)(2,1)} %copy-done, bf16[256,2816]{1,0:T(8,128)(2,1)} %collective-permute-done.13.refs_2_, ...), custom_call_target="tpu_custom_call" | custom-call | tf_op jit(solution)/shard_map/feed/pallas_call | solution.py:530
  221.7 11.8 %product.4.refs_0_.refs_1_ = bf16[2048,1408]{1,0:T(8,128)(2,1)} custom-call(bf16[2048,1024]{1,0:T(8,128)(2,1)} %get-tuple-element.792.left, bf16[1024,1408]{1,0:T(8,128)(2,1)} %get-tuple-element.916.right.refs_0_), custom_call_target="tpu_custom_call" | custom-call | tf_op jit(solution)/shard_map/product/pallas_call | solution.py:604
  239.7 13.4 %collective-permute-done.36.refs_7_.refs_5_ = bf16[256,1408]{1,0:T(8,128)(2,1)S(1)} collective-permute-done((bf16[256,1408]{1,0:T(8,128)(2,1)}, bf16[256,1408]{1,0:T(8,128)(2,1)S(1)}, u32[]{:S(2)}, u32[]{:S(2)}) %collective-permute-start.36) | collective-permute-done | bytes 720928 | tf_op jit(solution)/shard_map/ppermute | solution.py:58
  258.3 6.9 %collective-permute-done.39.refs_11_.refs_9_ = bf16[256,640]{1,0:T(8,128)(2,1)S(1)} collective-permute-done((bf16[256,640]{1,0:T(8,128)(2,1)S(1)}, bf16[256,640]{1,0:T(8,128)(2,1)S(1)}, u32[]{:S(2)}, u32[]{:S(2)}) %collective-permute-start.39) | collective-permute-done | bytes 327712 | tf_op jit(solution)/shard_map/ppermute | solution.py:58
  274.9 12.5 %feed_back.1.right.refs_0_ = bf16[1024,2816]{1,0:T(8,128)(2,1)} custom-call(bf16[1024,2048]{1,0:T(8,128)(2,1)} %get-tuple-element.827.refs_0_, bf16[1024,1408]{1,0:T(8,128)(2,1)} %get-tuple-element.828.refs_1_, bf16[1024,1408]{1,0:T(8,128)(2,1)} %get-tuple-element.829.refs_2_, bf16[256,1408]{1,0:T(8,128)(2,1)} %bitcast.35, bf16[256,1408]{1,0:T(8,128)(2,1)} %copy-done.20, ...), custom_call_target="tpu_custom_call" | custom-call | tf_op jit(solution)/shard_map/feed_back/pallas_call | solution.py:557
  293.9 17.4 %product.5.refs_0_.refs_1_ = bf16[2048,2816]{1,0:T(8,128)(2,1)} custom-call(bf16[2048,1024]{1,0:T(8,128)(2,1)} %get-tuple-element.855.left, bf16[1024,2816]{1,0:T(8,128)(2,1)} %feed_back.1.right.refs_0_), custom_call_target="tpu_custom_call" | custom-call | tf_op jit(solution)/shard_map/product/pallas_call | solution.py:604
  322.4 20.6 %spread.2 = (bf16[256,2048]{1,0:T(8,128)(2,1)}, bf16[256,2048]{1,0:T(8,128)(2,1)}, bf16[256,2048]{1,0:T(8,128)(2,1)}, bf16[256,2048]{1,0:T(8,128)(2,1)}) custom-call(bf16[1024,2816]{1,0:T(8,128)(2,1)} %feed_back.1.right.refs_0_, bf16[256,2816]{1,0:T(8,128)(2,1)} %copy-done, bf16[256,2816]{1,0:T(8,128)(2,1)} %collective-permute-done.13.refs_2_, ...), custom_call_target="tpu_custom_call" | custom-call | tf_op jit(solution)/shard_map/spread/pallas_call | solution.py:586
  364.7 12.3 %spread.3 = (bf16[256,2048]{1,0:T(8,128)(2,1)}, bf16[256,2048]{1,0:T(8,128)(2,1)}, bf16[256,2048]{1,0:T(8,128)(2,1)}, bf16[256,2048]{1,0:T(8,128)(2,1)}) custom-call(bf16[1024,1408]{1,0:T(8,128)(2,1)} %get-tuple-element.916.right.refs_0_, bf16[256,1408]{1,0:T(8,128)(2,1)} %bitcast.36, bf16[256,1408]{1,0:T(8,128)(2,1)} %copy-done.20, ...), custom_call_target="tpu_custom_call" | custom-call | tf_op jit(solution)/shard_map/spread/pallas_call | solution.py:586
  381.8 3.9 grow.13
  387.8 5.0 norm_back.2
  396.6 15.9 %attend_back.2 = (bf16[1024,640]{1,0:T(8,128)(2,1)}, bf16[256,2048]{1,0:T(8,128)(2,1)}, bf16[256,2048]{1,0:T(8,128)(2,1)}) custom-call(bf16[256,2048]{1,0:T(8,128)(2,1)} %get-tuple-element.1052.refs_0_.own, bf16[256,2048]{1,0:T(8,128)(2,1)} %copy-done.17, bf16[1024,512]{1,0:T(8,128)(2,1)} %get-tuple-element.1019.refs_2_.refs_3_, ...), custom_call_target="tpu_custom_call" | custom-call | tf_op jit(solution)/shard_map/attend_back/pallas_call | solution.py:415
  412.5 4.4 collective-permute-done.57.refs_2_
  418.1 3.9 grow.14
  425.8 16.0 %attend_back.3 = (bf16[1024,640]{1,0:T(8,128)(2,1)}, bf16[256,2048]{1,0:T(8,128)(2,1)}, bf16[256,2048]{1,0:T(8,128)(2,1)}) custom-call(bf16[256,2048]{1,0:T(8,128)(2,1)} %copy-done.4, bf16[128,2048]{1,0:T(8,128)(2,1)} %copy-done.22, bf16[128,2048]{1,0:T(8,128)(2,1)} %copy-done.23, ...), custom_call_target="tpu_custom_call", output_to_operand_aliasing={{0}: (19, {})} | custom-call | tf_op jit(solution)/shard_map/attend_back/pallas_call | solution.py:415
  450.2 5.2 gathered.7.left
  455.4 8.0 %product.6.refs_1_.refs_3_ = bf16[2048,512]{1,0:T(8,128)(2,1)} custom-call(bf16[2048,1024]{1,0:T(8,128)(2,1)} %gathered.7.left, bf16[1024,512]{1,0:T(8,128)(2,1)} %get-tuple-element.1061.right), custom_call_target="tpu_custom_call" | custom-call | tf_op jit(solution)/shard_map/product/pallas_call | solution.py:604
  463.4 8.8 %product.7.refs_0_.refs_2_ = bf16[2048,640]{1,0:T(8,128)(2,1)} custom-call(bf16[2048,1024]{1,0:T(8,128)(2,1)} %get-tuple-element.1063.left, bf16[1024,640]{1,0:T(8,128)(2,1)} %get-tuple-element.1064.right), custom_call_target="tpu_custom_call" | custom-call | tf_op jit(solution)/shard_map/product/pallas_call | solution.py:604
  490.8 5.3 norm_back.3
  517.0 5.7 %collective-permute-done.79.refs_4_ = bf16[256,1152]{1,0:T(8,128)(2,1)S(1)} collective-permute-done((bf16[256,1152]{1,0:T(8,128)(2,1)}, bf16[256,1152]{1,0:T(8,128)(2,1)S(1)}, u32[]{:S(2)}, u32[]{:S(2)}) %collective-permute-start.79) | collective-permute-done | bytes 589856 | tf_op jit(solution)/shard_map/ppermute | solution.py:58
  529.6 11.6 %collective-permute-done.78 = f32[2,2048]{1,0:T(2,128)S(1)} collective-permute-done((f32[2,2048]{1,0:T(2,128)S(1)}, f32[2,2048]{1,0:T(2,128)S(1)}, u32[]{:S(2)}, u32[]{:S(2)}) %collective-permute-start.78) | collective-permute-done | bytes 16416 | tf_op jit(solution)/shard_map/ppermute | solution.py:58
  543.9 4.4 shuffle.7
  (386 shorter events, 232.0 us)
Async XLA Ops:
  28.7 26.6 %collective-permute-start.8 = (bf16[256,2176]{1,0:T(8,128)(2,1)}, bf16[256,2176]{1,0:T(8,128)(2,1)}, u32[]{:S(2)}, u32[]{:S(2)}) collective-permute-start(bf16[256,2176]{1,0:T(8,128)(2,1)} %pad_maximum_fusion.1.own), channel_id=1, source_target_pairs={{0,2},{1,3},{2,0},{3,1},{4,6},{5,7},{6,4},{7,5},{8,10},{9,11},{10,... | collective-permute-start | bytes 3342344 | tf_op jit(solution)/shard_map/ppermute | solution.py:58
  69.9 34.5 %collective-permute-start.12 = (bf16[256,2816]{1,0:T(8,128)(2,1)S(1)}, bf16[256,2816]{1,0:T(8,128)(2,1)}, u32[]{:S(2)}, u32[]{:S(2)}) collective-permute-start(bf16[256,2816]{1,0:T(8,128)(2,1)S(1)} %pad_maximum_fusion.refs_1_), channel_id=1, source_target_pairs={{0,8},{8,16},{16,24},{24,28},{28,20},{20,12},{12,4},{4,0},{1,9},{9... | collective-permute-start | bytes 4325384 | tf_op jit(solution)/shard_map/ppermute | solution.py:58
  71.0 33.5 %collective-permute-start.13 = (bf16[256,2816]{1,0:T(8,128)(2,1)S(1)}, bf16[256,2816]{1,0:T(8,128)(2,1)}, u32[]{:S(2)}, u32[]{:S(2)}) collective-permute-start(bf16[256,2816]{1,0:T(8,128)(2,1)S(1)} %pad_maximum_fusion.refs_1_), channel_id=1, source_target_pairs={{8,0},{16,8},{24,16},{28,24},{20,28},{12,20},{4,12},{0,4},{9,1},{1... | collective-permute-start | bytes 4325384 | tf_op jit(solution)/shard_map/ppermute | solution.py:58
  77.3 27.2 %collective-permute-start.16 = (bf16[256,2048]{1,0:T(8,128)(2,1)S(1)}, bf16[256,2048]{1,0:T(8,128)(2,1)}, u32[]{:S(2)}, u32[]{:S(2)}) collective-permute-start(bf16[256,2048]{1,0:T(8,128)(2,1)S(1)} %copy-done.3), channel_id=1, source_target_pairs={{0,2},{1,3},{2,0},{3,1},{4,6},{5,7},{6,4},{7,5},{8,10},{9,11},{10,... | collective-permute-start | bytes 3145736 | tf_op jit(solution)/shard_map/ppermute | solution.py:58
  106.5 34.1 %collective-permute-start.22 = (bf16[256,2816]{1,0:T(8,128)(2,1)}, bf16[256,2816]{1,0:T(8,128)(2,1)S(1)}, u32[]{:S(2)}, u32[]{:S(2)}) collective-permute-start(bf16[256,2816]{1,0:T(8,128)(2,1)} %collective-permute-done.12.refs_7_), channel_id=1, source_target_pairs={{0,8},{8,16},{16,24},{24,28},{28,20},{20,12},{12,4},{4,0},{1,9},{9... | collective-permute-start | bytes 4325384 | tf_op jit(solution)/shard_map/ppermute | solution.py:58
  107.5 34.2 %collective-permute-start.23 = (bf16[256,2816]{1,0:T(8,128)(2,1)}, bf16[256,2816]{1,0:T(8,128)(2,1)}, u32[]{:S(2)}, u32[]{:S(2)}) collective-permute-start(bf16[256,2816]{1,0:T(8,128)(2,1)} %collective-permute-done.13.refs_2_), channel_id=1, source_target_pairs={{8,0},{16,8},{24,16},{28,24},{20,28},{12,20},{4,12},{0,4},{9,1},{1... | collective-permute-start | bytes 4325384 | tf_op jit(solution)/shard_map/ppermute | solution.py:58
  121.0 22.8 %collective-permute-start.20 = (bf16[256,2048]{1,0:T(8,128)(2,1)}, bf16[256,2048]{1,0:T(8,128)(2,1)}, u32[]{:S(2)}, u32[]{:S(2)}) collective-permute-start(bf16[256,2048]{1,0:T(8,128)(2,1)} %get-tuple-element.718), channel_id=1, source_target_pairs={{0,1},{1,0},{2,3},{3,2},{4,5},{5,4},{6,7},{7,6},{8,9},{9,8},{10,11... | collective-permute-start | bytes 3145736 | tf_op jit(solution)/shard_map/ppermute | solution.py:58
  121.0 25.9 %collective-permute-start.21 = (bf16[256,2048]{1,0:T(8,128)(2,1)}, bf16[256,2048]{1,0:T(8,128)(2,1)}, u32[]{:S(2)}, u32[]{:S(2)}) collective-permute-start(bf16[256,2048]{1,0:T(8,128)(2,1)} %plus.4), channel_id=1, source_target_pairs={{0,2},{1,3},{2,0},{3,1},{4,6},{5,7},{6,4},{7,5},{8,10},{9,11},{10,... | collective-permute-start | bytes 3145736 | tf_op jit(solution)/shard_map/ppermute | solution.py:58
  141.7 33.5 %collective-permute-start.25 = (bf16[256,2816]{1,0:T(8,128)(2,1)}, bf16[256,2816]{1,0:T(8,128)(2,1)S(1)}, u32[]{:S(2)}, u32[]{:S(2)}) collective-permute-start(bf16[256,2816]{1,0:T(8,128)(2,1)} %copy-done.11), channel_id=1, source_target_pairs={{0,8},{8,16},{16,24},{24,28},{28,20},{20,12},{12,4},{4,0},{1,9},{9... | collective-permute-start | bytes 4325384 | tf_op jit(solution)/shard_map/ppermute | solution.py:58
  142.7 33.2 %collective-permute-start.26 = (bf16[256,2816]{1,0:T(8,128)(2,1)}, bf16[256,2816]{1,0:T(8,128)(2,1)S(1)}, u32[]{:S(2)}, u32[]{:S(2)}) collective-permute-start(bf16[256,2816]{1,0:T(8,128)(2,1)} %collective-permute-done.23.refs_3_), channel_id=1, source_target_pairs={{8,0},{16,8},{24,16},{28,24},{20,28},{12,20},{4,12},{0,4},{9,1},{1... | collective-permute-start | bytes 4325384 | tf_op jit(solution)/shard_map/ppermute | solution.py:58
  150.8 29.2 %collective-permute-start.24 = (bf16[256,2048]{1,0:T(8,128)(2,1)}, bf16[256,2048]{1,0:T(8,128)(2,1)S(1)}, u32[]{:S(2)}, u32[]{:S(2)}) collective-permute-start(bf16[256,2048]{1,0:T(8,128)(2,1)} %get-tuple-element.754.own), channel_id=1, source_target_pairs={{0,2},{1,3},{2,0},{3,1},{4,6},{5,7},{6,4},{7,5},{8,10},{9,11},{10,... | collective-permute-start | bytes 3145736 | tf_op jit(solution)/shard_map/ppermute | solution.py:58
  197.3 22.2 %collective-permute-start.32 = (bf16[256,1408]{1,0:T(8,128)(2,1)S(1)}, bf16[256,1408]{1,0:T(8,128)(2,1)S(1)}, u32[]{:S(2)}, u32[]{:S(2)}) collective-permute-start(bf16[256,1408]{1,0:T(8,128)(2,1)S(1)} %bitcast.33), channel_id=1, source_target_pairs={{0,8},{8,16},{16,24},{24,28},{28,20},{20,12},{12,4},{4,0},{1,9},{9... | collective-permute-start | bytes 2162696 | tf_op jit(solution)/shard_map/ppermute | solution.py:58
  197.9 21.7 %collective-permute-start.33 = (bf16[256,1408]{1,0:T(8,128)(2,1)S(1)}, bf16[256,1408]{1,0:T(8,128)(2,1)S(1)}, u32[]{:S(2)}, u32[]{:S(2)}) collective-permute-start(bf16[256,1408]{1,0:T(8,128)(2,1)S(1)} %bitcast.34), channel_id=1, source_target_pairs={{8,0},{16,8},{24,16},{28,24},{20,28},{12,20},{4,12},{0,4},{9,1},{1... | collective-permute-start | bytes 2162696 | tf_op jit(solution)/shard_map/ppermute | solution.py:58
  291.9 21.9 %collective-permute-start.44 = (bf16[256,1408]{1,0:T(8,128)(2,1)}, bf16[256,1408]{1,0:T(8,128)(2,1)S(1)}, u32[]{:S(2)}, u32[]{:S(2)}) collective-permute-start(bf16[256,1408]{1,0:T(8,128)(2,1)} %get-tuple-element.850), channel_id=1, source_target_pairs={{0,8},{8,16},{16,24},{24,28},{28,20},{20,12},{12,4},{4,0},{1,9},{9... | collective-permute-start | bytes 2162696 | tf_op jit(solution)/shard_map/ppermute | solution.py:58
  318.2 24.9 %collective-permute-start.46 = (bf16[256,1408]{1,0:T(8,128)(2,1)}, bf16[256,1408]{1,0:T(8,128)(2,1)S(1)}, u32[]{:S(2)}, u32[]{:S(2)}) collective-permute-start(bf16[256,1408]{1,0:T(8,128)(2,1)} %get-tuple-element.868), channel_id=1, source_target_pairs={{0,8},{8,16},{16,24},{24,28},{28,20},{20,12},{12,4},{4,0},{1,9},{9... | collective-permute-start | bytes 2162696 | tf_op jit(solution)/shard_map/ppermute | solution.py:58
  319.7 23.4 %collective-permute-start.47 = (bf16[256,1408]{1,0:T(8,128)(2,1)}, bf16[256,1408]{1,0:T(8,128)(2,1)S(1)}, u32[]{:S(2)}, u32[]{:S(2)}) collective-permute-start(bf16[256,1408]{1,0:T(8,128)(2,1)} %get-tuple-element.870), channel_id=1, source_target_pairs={{8,0},{16,8},{24,16},{28,24},{20,28},{12,20},{4,12},{0,4},{9,1},{1... | collective-permute-start | bytes 2162696 | tf_op jit(solution)/shard_map/ppermute | solution.py:58
  320.2 26.6 %collective-permute-start.48 = (bf16[256,1408]{1,0:T(8,128)(2,1)}, bf16[256,1408]{1,0:T(8,128)(2,1)S(1)}, u32[]{:S(2)}, u32[]{:S(2)}) collective-permute-start(bf16[256,1408]{1,0:T(8,128)(2,1)} %get-tuple-element.891), channel_id=1, source_target_pairs={{0,8},{8,16},{16,24},{24,28},{28,20},{20,12},{12,4},{4,0},{1,9},{9... | collective-permute-start | bytes 2162696 | tf_op jit(solution)/shard_map/ppermute | solution.py:58
  321.7 25.2 %collective-permute-start.49 = (bf16[256,1408]{1,0:T(8,128)(2,1)}, bf16[256,1408]{1,0:T(8,128)(2,1)S(1)}, u32[]{:S(2)}, u32[]{:S(2)}) collective-permute-start(bf16[256,1408]{1,0:T(8,128)(2,1)} %get-tuple-element.892), channel_id=1, source_target_pairs={{8,0},{16,8},{24,16},{28,24},{20,28},{12,20},{4,12},{0,4},{9,1},{1... | collective-permute-start | bytes 2162696 | tf_op jit(solution)/shard_map/ppermute | solution.py:58
  351.9 27.7 %collective-permute-start.54 = (bf16[256,2816]{1,0:T(8,128)(2,1)}, bf16[256,2816]{1,0:T(8,128)(2,1)S(1)}, u32[]{:S(2)}, u32[]{:S(2)}) collective-permute-start(bf16[256,2816]{1,0:T(8,128)(2,1)} %get-tuple-element.940), channel_id=1, source_target_pairs={{0,8},{8,16},{16,24},{24,28},{28,20},{20,12},{12,4},{4,0},{1,9},{9... | collective-permute-start | bytes 4325384 | tf_op jit(solution)/shard_map/ppermute | solution.py:58
  352.7 27.5 %collective-permute-start.55 = (bf16[256,2816]{1,0:T(8,128)(2,1)}, bf16[256,2816]{1,0:T(8,128)(2,1)S(1)}, u32[]{:S(2)}, u32[]{:S(2)}) collective-permute-start(bf16[256,2816]{1,0:T(8,128)(2,1)} %get-tuple-element.942), channel_id=1, source_target_pairs={{8,0},{16,8},{24,16},{28,24},{20,28},{12,20},{4,12},{0,4},{9,1},{1... | collective-permute-start | bytes 4325384 | tf_op jit(solution)/shard_map/ppermute | solution.py:58
  361.0 26.8 %collective-permute-start.52 = (bf16[256,2048]{1,0:T(8,128)(2,1)}, bf16[256,2048]{1,0:T(8,128)(2,1)}, u32[]{:S(2)}, u32[]{:S(2)}) collective-permute-start(bf16[256,2048]{1,0:T(8,128)(2,1)} %get-tuple-element.937), channel_id=1, source_target_pairs={{0,1},{1,0},{2,3},{3,2},{4,5},{5,4},{6,7},{7,6},{8,9},{9,8},{10,11... | collective-permute-start | bytes 3145736 | tf_op jit(solution)/shard_map/ppermute | solution.py:58
  361.1 26.7 %collective-permute-start.53 = (bf16[256,2048]{1,0:T(8,128)(2,1)}, bf16[256,2048]{1,0:T(8,128)(2,1)}, u32[]{:S(2)}, u32[]{:S(2)}) collective-permute-start(bf16[256,2048]{1,0:T(8,128)(2,1)} %plus.5), channel_id=1, source_target_pairs={{0,2},{1,3},{2,0},{3,1},{4,6},{5,7},{6,4},{7,5},{8,10},{9,11},{10,... | collective-permute-start | bytes 3145736 | tf_op jit(solution)/shard_map/ppermute | solution.py:58
  385.7 31.2 %collective-permute-start.57 = (bf16[256,2816]{1,0:T(8,128)(2,1)}, bf16[256,2816]{1,0:T(8,128)(2,1)S(1)}, u32[]{:S(2)}, u32[]{:S(2)}) collective-permute-start(bf16[256,2816]{1,0:T(8,128)(2,1)} %get-tuple-element.969), channel_id=1, source_target_pairs={{0,8},{8,16},{16,24},{24,28},{28,20},{20,12},{12,4},{4,0},{1,9},{9... | collective-permute-start | bytes 4325384 | tf_op jit(solution)/shard_map/ppermute | solution.py:58
  386.0 31.6 %collective-permute-start.58 = (bf16[256,2816]{1,0:T(8,128)(2,1)}, bf16[256,2816]{1,0:T(8,128)(2,1)}, u32[]{:S(2)}, u32[]{:S(2)}) collective-permute-start(bf16[256,2816]{1,0:T(8,128)(2,1)} %get-tuple-element.971), channel_id=1, source_target_pairs={{8,0},{16,8},{24,16},{28,24},{20,28},{12,20},{4,12},{0,4},{9,1},{1... | collective-permute-start | bytes 4325384 | tf_op jit(solution)/shard_map/ppermute | solution.py:58
  392.8 29.2 %collective-permute-start.56 = (bf16[256,2048]{1,0:T(8,128)(2,1)}, bf16[256,2048]{1,0:T(8,128)(2,1)S(1)}, u32[]{:S(2)}, u32[]{:S(2)}) collective-permute-start(bf16[256,2048]{1,0:T(8,128)(2,1)} %get-tuple-element.1052.refs_0_.own), channel_id=1, source_target_pairs={{0,2},{1,3},{2,0},{3,1},{4,6},{5,7},{6,4},{7,5},{8,10},{9,11},{10,... | collective-permute-start | bytes 3145736 | tf_op jit(solution)/shard_map/ppermute | solution.py:58
  422.7 52.2 %collective-permute-start.64 = (bf16[256,2816]{1,0:T(8,128)(2,1)}, bf16[256,2816]{1,0:T(8,128)(2,1)S(1)}, u32[]{:S(2)}, u32[]{:S(2)}) collective-permute-start(bf16[256,2816]{1,0:T(8,128)(2,1)} %get-tuple-element.1068), channel_id=1, source_target_pairs={{0,8},{8,16},{16,24},{24,28},{28,20},{20,12},{12,4},{4,0},{1,9},{9... | collective-permute-start | bytes 4325384 | tf_op jit(solution)/shard_map/ppermute | solution.py:58
  423.5 51.4 %collective-permute-start.65 = (bf16[256,2816]{1,0:T(8,128)(2,1)}, bf16[256,2816]{1,0:T(8,128)(2,1)}, u32[]{:S(2)}, u32[]{:S(2)}) collective-permute-start(bf16[256,2816]{1,0:T(8,128)(2,1)} %get-tuple-element.1070), channel_id=1, source_target_pairs={{8,0},{16,8},{24,16},{28,24},{20,28},{12,20},{4,12},{0,4},{9,1},{1... | collective-permute-start | bytes 4325384 | tf_op jit(solution)/shard_map/ppermute | solution.py:58
  449.0 40.8 %collective-permute-start.70 = (bf16[256,2048]{1,0:T(8,128)(2,1)}, bf16[256,2048]{1,0:T(8,128)(2,1)S(1)}, u32[]{:S(2)}, u32[]{:S(2)}) collective-permute-start(bf16[256,2048]{1,0:T(8,128)(2,1)} %get-tuple-element.1098), channel_id=1, source_target_pairs={{0,1},{1,0},{2,3},{3,2},{4,5},{5,4},{6,7},{7,6},{8,9},{9,8},{10,11... | collective-permute-start | bytes 3145736 | tf_op jit(solution)/shard_map/ppermute | solution.py:58
  449.2 40.6 %collective-permute-start.71 = (bf16[256,2048]{1,0:T(8,128)(2,1)}, bf16[256,2048]{1,0:T(8,128)(2,1)}, u32[]{:S(2)}, u32[]{:S(2)}) collective-permute-start(bf16[256,2048]{1,0:T(8,128)(2,1)} %plus.6), channel_id=1, source_target_pairs={{0,2},{1,3},{2,0},{3,1},{4,6},{5,7},{6,4},{7,5},{8,10},{9,11},{10,... | collective-permute-start | bytes 3145736 | tf_op jit(solution)/shard_map/ppermute | solution.py:58
  513.2 29.7 %collective-permute-start.76 = (bf16[256,2048]{1,0:T(8,128)(2,1)}, bf16[256,2048]{1,0:T(8,128)(2,1)S(1)}, u32[]{:S(2)}, u32[]{:S(2)}) collective-permute-start(bf16[256,2048]{1,0:T(8,128)(2,1)} %get-tuple-element.1145), channel_id=1, source_target_pairs={{0,1},{1,0},{2,3},{3,2},{4,5},{5,4},{6,7},{7,6},{8,9},{9,8},{10,11... | collective-permute-start | bytes 3145736 | tf_op jit(solution)/shard_map/ppermute | solution.py:58
  513.2 30.7 %collective-permute-start.77 = (bf16[256,2048]{1,0:T(8,128)(2,1)}, bf16[256,2048]{1,0:T(8,128)(2,1)}, u32[]{:S(2)}, u32[]{:S(2)}) collective-permute-start(bf16[256,2048]{1,0:T(8,128)(2,1)} %plus.7), channel_id=1, source_target_pairs={{0,2},{1,3},{2,0},{3,1},{4,6},{5,7},{6,4},{7,5},{8,10},{9,11},{10,... | collective-permute-start | bytes 3145736 | tf_op jit(solution)/shard_map/ppermute | solution.py:58
  526.2 22.1 %collective-permute-start.82 = (bf16[256,1152]{1,0:T(8,128)(2,1)}, bf16[256,1152]{1,0:T(8,128)(2,1)S(1)}, u32[]{:S(2)}, u32[]{:S(2)}) collective-permute-start(bf16[256,1152]{1,0:T(8,128)(2,1)} %get-tuple-element.1184), channel_id=1, source_target_pairs={{0,8},{8,16},{16,24},{24,28},{28,20},{20,12},{12,4},{4,0},{1,9},{9... | collective-permute-start | bytes 1769480 | tf_op jit(solution)/shard_map/ppermute | solution.py:58
  (117 other events, 899.3 us)

commit v4 on v3

--- a/solution.py
+++ b/solution.py
@@ -50,9 +50,11 @@
 
     def run(self, work, *values):
         result = work(*lax.optimization_barrier((*values, self.token))[:-1])
-        if isinstance(result, (tuple, list)):
-            return self.passed(*result)
-        return self.passed(result)
+        if not isinstance(result, (tuple, list)):
+            return self.passed(result)
+        out = lax.optimization_barrier((*result, self.token))
+        self.token = out[-1]
+        return out[:-1]
 
     def send(self, value, axis, pairs):
         return lax.ppermute(self.after(value), axis, pairs)
@@ -93,33 +95,27 @@
 
 
 class RingReduce:
-    def __init__(self, line, products, n, split):
-        self.line, self.products, self.n, self.split = line, products, n, split
+    def __init__(self, line, products, far, n, split):
+        self.line, self.products, self.far, self.n, self.split = line, products, far, n, split
         self.came = ()
-
-    def grown(self, away):
-        k = len(self.products)
-        return self.line.run(
-            lambda *v: grow(v[:k], v[k:], self.n, away, self.split), *self.products, *self.came
-        )
 
     def start(self, hop):
         n, pairs = self.n, ring_perms(self.n)
-        if hop == 1:
-            part = self.products[0].shape[0] // n
-            far = [v[n // 2 * part : (n // 2 + 1) * part] for v in self.products]
-            if len(far) == 1:
-                far = [far[0][:, : self.split], far[0][:, self.split :]]
-            ahead, behind = far
-        else:
-            ahead, behind = self.grown(n // 2 - hop + 1)
+        k = len(self.products)
+        ahead, behind = self.far
+        if hop > 1:
+            away = n // 2 - hop + 1
+            ahead, behind = self.line.run(
+                lambda *v: grow(v[:k], v[k:], n, away, self.split), *self.products, *self.came
+            )
         self.came = (self.line.send(ahead, "dp", pairs[0]), self.line.send(behind, "dp", pairs[1]))
 
     def wait(self, hop):
         self.came = self.line.passed(*self.came)
 
-    def total(self):
-        return self.grown(0)
+    def total(self, outputs):
+        k = len(self.products)
+        return self.line.run(lambda *v: last(v[:k], v[k:], self.n, outputs), *self.products, *self.came)
 
 
 CORE = [(i, i ^ 1) for i in range(4)]
@@ -220,6 +216,14 @@
     return left[:at] + [far[0]] + left[at:], right[:at] + [far[1]] + right[at:]
 
 
+def into_block(out_refs, value_ref):
+    for block, out_ref in enumerate(out_refs):
+
+        @pl.when(pl.program_id(0) == block)
+        def _(out_ref=out_ref):
+            out_ref[...] = value_ref[...]
+
+
 def turn(values, first_half):
     width = values.shape[-1]
     left = pltpu.roll(values, width - HEAD_DIM // 2, 1)
@@ -246,7 +250,7 @@
 def attention_forward(count, *refs):
     x_ref, gain_ref, cos_ref, sin_ref, col_ref, row_ref = refs[:6]
     turned_ref, q_ref, kv_ref, o_ref, lse_ref = refs[6 + count : 11 + count]
-    branch_refs, qkv_ref = refs[11 + count : 15 + count], refs[15 + count]
+    branch_refs, qkv_ref, made_ref = refs[11 + count : 15 + count], refs[15 + count], refs[16 + count]
     q_chunks, o_chunks = pieces_of(refs[6 : 6 + count], qkv_ref.shape[1], gain_ref.shape[1])
     depth = gain_ref.shape[1]
     rows, width = q_ref.shape
@@ -284,11 +288,8 @@
             log_sums = jnp.where(lanes == 2 * pair + side, peak + jnp.log(total), log_sums)
         o_ref[:, pair * LANES : (pair + 1) * LANES] = jnp.where(even, mixed[0], mixed[1]).astype(LOW)
     lse_ref[...] = log_sums
-    for block, branch_ref in enumerate(branch_refs):
-
-        @pl.when(pl.program_id(0) == block)
-        def _(branch_ref=branch_ref):
-            into_chunks(branch_ref, [o_ref[...]], [o_chunks])
+    into_chunks(made_ref, [o_ref[...]], [o_chunks])
+    into_block(branch_refs, made_ref)
 
 
 def fixed(rows, width):
@@ -325,7 +326,7 @@
             shaped((total, LANES), WIDE),
         ]
         + [shaped((rows, depth), LOW)] * 4,
-        scratch_shapes=[pltpu.VMEM((rows, width + LANES), WIDE)],
+        scratch_shapes=[pltpu.VMEM((rows, width + LANES), WIDE), pltpu.VMEM((rows, depth), LOW)],
         name="attend",
     )(x, gain, cosine, sine, column, row, *panel)
 
@@ -333,8 +334,8 @@
 def attention_backward(sizes, count, *refs):
     dh_refs, refs = refs[: sum(sizes)], refs[sum(sizes) :]
     q_ref, kv_ref, lse_ref, cos_ref, sin_ref, col_ref, row_ref = refs[:7]
-    panel, refs = refs[7 : 7 + count], refs[-len(sizes) - 2 :]
-    grad_ref, part_refs, do_ref = refs[0], refs[1:-1], refs[-1]
+    panel, refs = refs[7 : 7 + count], refs[-len(sizes) - 3 :]
+    grad_ref, part_refs, do_ref, made_ref = refs[0], refs[1:-2], refs[-2], refs[-1]
     q_chunks, o_chunks = pieces_of(panel, grad_ref.shape[1], dh_refs[0].shape[1])
     rows, width = q_ref.shape
     pairs = width // LANES
@@ -346,9 +347,10 @@
             at = 0
             for ref in mine:
                 end = at + ref.shape[0]
-                do_ref[at:end, :] = times_chunks(ref, o_chunks).astype(LOW)
+                made_ref[at:end, :] = ref[...]
                 at = end
 
+    do_ref[...] = times_chunks(made_ref, o_chunks).astype(LOW)
     cosine, sine = cos_ref[...], sin_ref[...]
     lanes = lane_ids(rows, LANES)
     even = lanes < HEAD_DIM
@@ -359,18 +361,19 @@
     vals = jnp.where(even, other, keyval).astype(LOW)
     allowed = allowed_pairs(col_ref[...], row_ref[0])
     log_sums = lse_ref[...]
-    grad_keys = jnp.zeros((rows, LANES), WIDE)
-    grad_vals = jnp.zeros((rows, LANES), WIDE)
-    for pair in range(pairs):
-        piece = q_ref[:, pair * LANES : (pair + 1) * LANES]
-        grads = do_ref[:, pair * LANES : (pair + 1) * LANES]
+
+    def heads(pair, totals):
+        grad_keys, grad_vals = totals
+        span = pl.ds(pl.multiple_of(pair * LANES, LANES), LANES)
+        piece = q_ref[:, span]
+        grads = do_ref[:, span]
         turned = []
         for side in range(2):
             mine = even if side == 0 else ~even
             chosen = jnp.where(mine, piece, jnp.zeros_like(piece))
             chosen_grad = jnp.where(mine, grads, jnp.zeros_like(grads))
-            head = 2 * pair + side
-            log_sum = log_sums[:, head : head + 1]
+            own = jnp.where(lanes == 2 * pair + side, log_sums, 0.0)
+            log_sum = jnp.sum(own, axis=1, keepdims=True)
             scores = jnp.where(allowed, dot_rows(chosen, keys) * scale, -1e30)
             soft = jnp.exp(scores - log_sum)
             grad_soft = dot_rows(chosen_grad, vals)
@@ -381,16 +384,17 @@
             turned.append(dot(grad_scores, keys))
         grad_q = jnp.where(even, turned[0], turned[1]) * scale
         grad_q = grad_q * cosine - turn(grad_q, first) * sine
-        grad_ref[:, pair * LANES : (pair + 1) * LANES] = grad_q.astype(LOW)
+        grad_ref[:, span] = grad_q.astype(LOW)
+        return grad_keys, grad_vals
+
+    nothing = jnp.zeros((rows, LANES), WIDE)
+    grad_keys, grad_vals = lax.fori_loop(0, pairs, heads, (nothing, nothing), unroll=2)
     grad_keys = (grad_keys + pltpu.roll(grad_keys, HEAD_DIM, 1)) * scale
     grad_keys = grad_keys * cosine - turn(grad_keys, first) * sine
     grad_vals = grad_vals + pltpu.roll(grad_vals, HEAD_DIM, 1)
     grad_ref[:, width:] = jnp.where(even, grad_keys, grad_vals).astype(LOW)
-    for block, part_ref in enumerate(part_refs):
-
-        @pl.when(pl.program_id(0) == block)
-        def _(part_ref=part_ref):
-            into_chunks(part_ref, [grad_ref[...]], [q_chunks])
+    into_chunks(made_ref, [grad_ref[...]], [q_chunks])
+    into_block(part_refs, made_ref)
 
 
 def attend_back(blocks, groups, query, keyval, log_sums, cosine, sine, column, row, panel, rows, before=None):
@@ -418,7 +422,7 @@
         in_specs=in_specs,
         out_specs=[chosen(width + LANES)] + [fixed(rows, depth)] * len(groups),
         out_shape=[shaped((total, width + LANES), LOW)] + [shaped((rows, depth), LOW)] * len(groups),
-        scratch_shapes=[pltpu.VMEM((rows, width), LOW)],
+        scratch_shapes=[pltpu.VMEM((rows, width), LOW), pltpu.VMEM((rows, depth), LOW)],
         input_output_aliases=aliases,
         name="attend_back",
     )(*operands)
@@ -526,10 +530,10 @@
 
 def feed(x, panel, wide):
     total, depth = x.shape
-    step = total // 4
+    step = total // 8
     return pl.pallas_call(
         functools.partial(feed_kernel, len(panel)),
-        grid=(4,),
+        grid=(8,),
         in_specs=[by_rows(step, depth)] + [whole(v) for v in panel],
         out_specs=[by_rows(step, wide)] * 3,
         out_shape=[shaped((total, wide), LOW)] * 3,
@@ -566,17 +570,10 @@
 
 
 def spread_kernel(count, split, *refs):
-    value, out_refs = refs[0], refs[1 + count :]
-    left, right = pieces_of(refs[1 : 1 + count], split, out_refs[0].shape[1])
-    rows = out_refs[0].shape[0]
-    each = value.shape[0] // rows
-    for block, out_ref in enumerate(out_refs):
-        inside = block % each
-
-        @pl.when(pl.program_id(0) == block // each)
-        def _(out_ref=out_ref, at=inside * rows):
-            pieces = [value[at : at + rows, :split], value[at : at + rows, split:]]
-            into_chunks(out_ref, pieces, [left, right])
+    value, out_refs, made_ref = refs[0], refs[1 + count : -1], refs[-1]
+    left, right = pieces_of(refs[1 : 1 + count], split, made_ref.shape[1])
+    into_chunks(made_ref, [value[:, :split], value[:, split:]], [left, right])
+    into_block(out_refs, made_ref)
 
 
 def spread(value, panel, split, rows):
@@ -586,18 +583,28 @@
     return pl.pallas_call(
         functools.partial(spread_kernel, n, split),
         grid=(4,),
-        in_specs=[by_rows(total // 4, wide)] + [whole(c) for c in panel],
+        in_specs=[by_rows(rows, wide)] + [whole(c) for c in panel],
         out_specs=[fixed(rows, depth)] * 4,
         out_shape=[shaped((rows, depth), LOW)] * 4,
+        scratch_shapes=[pltpu.VMEM((rows, depth), LOW)],
         name="spread",
     )(value, *panel)
 
 
-def product_kernel(left, right, out):
-    out[...] = dot(left[...], right[...]).astype(LOW)
-
-
-def product(left, right):
+def product_kernel(left, right, out, *far_refs):
+    total = dot(left[...], right[...]).astype(LOW)
+    out[...] = total
+
+    @pl.when(pl.program_id(0) == pl.num_programs(0) // 2)
+    def _():
+        at = 0
+        for far_ref in far_refs:
+            part, width = far_ref.shape
+            far_ref[...] = total[:part, at : at + width]
+            at += width
+
+
+def product(left, right, n, widths):
     depth, total = left.shape
     wide = right.shape[1]
     step = depth // 8
@@ -605,8 +612,8 @@
         product_kernel,
         grid=(8,),
         in_specs=[by_rows(step, total), whole(right)],
-        out_specs=by_rows(step, wide),
-        out_shape=shaped((depth, wide), LOW),
+        out_specs=[by_rows(step, wide)] + [fixed(depth // n, width) for width in widths],
+        out_shape=[shaped((depth, wide), LOW)] + [shaped((depth // n, width), LOW) for width in widths],
         name="product",
     )(left, right)
 
@@ -632,13 +639,43 @@
         at += width
 
 
-def last_kernel(count, *refs):
-    ahead, behind, out = refs[count:]
-    at = 0
-    for term in refs[:count]:
+def last_kernel(count, outputs, *refs):
+    terms, (ahead, behind), outs = refs[:count], refs[count : count + 2], refs[count + 2 :]
+    totals, at = [], 0
+    for term in terms:
         end = at + term.shape[1]
-        out[:, at:end] = term[...].astype(WIDE) + ahead[:, at:end].astype(WIDE) + behind[:, at:end].astype(WIDE)
+        totals.append(term[...].astype(WIDE) + ahead[:, at:end].astype(WIDE) + behind[:, at:end].astype(WIDE))
         at = end
+    which, at = 0, 0
+    for (width, turned), out in zip(outputs, outs):
+        if at == totals[which].shape[1]:
+            which, at = which + 1, 0
+        value = totals[which][:, at : at + width]
+        out[...] = value.T if turned else value
+        at += width
+
+
+def last(products, came, n, outputs):
+    part = products[0].shape[0] // n
+    step = part // 2 if part // 2 % LANES == 0 else part
+    specs, shapes = [], []
+    for width, turned in outputs:
+        if turned:
+            specs.append(pl.BlockSpec((width, step), lambda i: (0, i)))
+            shapes.append(shaped((width, part), WIDE))
+        else:
+            specs.append(by_rows(step, width))
+            shapes.append(shaped((part, width), WIDE))
+    return tuple(
+        pl.pallas_call(
+            functools.partial(last_kernel, len(products), outputs),
+            grid=(part // step,),
+            in_specs=[by_rows(step, v.shape[1]) for v in (*products, *came)],
+            out_specs=specs,
+            out_shape=shapes,
+            name="last",
+        )(*products, *came)
+    )
 
 
 def grow(products, came, n, away, split):
@@ -651,15 +688,6 @@
     def rows_at(offset):
         return [pl.BlockSpec((step, v.shape[1]), lambda i: (2 * offset + i, 0)) for v in products]
 
-    if away == 0:
-        return pl.pallas_call(
-            functools.partial(last_kernel, len(products)),
-            grid=(2,),
-            in_specs=rows_at(0) + came_specs,
-            out_specs=by_rows(step, wide),
-            out_shape=shaped((part, wide), WIDE),
-            name="last",
-        )(*products, *came)
     return tuple(
         pl.pallas_call(
             functools.partial(grow_kernel, split, narrow, len(products)),
@@ -825,8 +853,10 @@
         down.wait(hop)
         down.start(hop + 1)
         if hop == 1:
-            down_terms = line.run(lambda a, b: product(a, b), grads_turned, activation)
-            r_down = RingReduce(line, [down_terms], n, split)
+            down_terms, *far = line.run(
+                lambda a, b: product(a, b, n, (split, hidden_wide - split)), grads_turned, activation
+            )
+            r_down = RingReduce(line, [down_terms], far, n, split)
     r_down.start(1)
     down.wait(hops)
     down_panel = down.panel()
@@ -839,8 +869,10 @@
     for hop in range(2, hops - 1):
         r_down.wait(hop)
         r_down.start(hop + 1)
-    feed_terms = line.run(lambda a, b: product(a, b), mlp_turned, grad_feed)
-    r_feed = RingReduce(line, [feed_terms], n, hidden_wide)
+    feed_terms, *far = line.run(
+        lambda a, b: product(a, b, n, (hidden_wide, hidden_wide)), mlp_turned, grad_feed
+    )
+    r_feed = RingReduce(line, [feed_terms], far, n, hidden_wide)
     r_down.wait(hops - 1)
     r_down.start(hops)
     r_feed.start(1)
@@ -850,7 +882,7 @@
     r_feed.start(2)
     grad_normed = GroupReduce(line, grad_normed)
     grad_normed.relay()
-    grad_down = r_down.total()
+    (grad_down,) = r_down.total([(hidden_wide, True)])
     layer_part = line.run(lambda a, *v: spread(a, v, split, rows), activation, *down_panel)
     for hop in range(2, hops - 1):
         r_feed.wait(hop)
@@ -880,18 +912,19 @@
     r_feed.wait(hops - 1)
     r_feed.start(hops)
     upper, lower = b.relay()
+    branch_turned = line.run(
+        lambda *v: gathered(v, with_all=False), b.own, b.pair, b_core, upper, lower
+    )
+    out_terms, out_far = line.run(lambda a, b: product(a, b, n, (heads_wide,)), branch_turned, mixed)
     grad_qkv, pair, diagonal = backward((1, 3), [[b.pair], [upper, lower]], grad_qkv)
     grad_input_sum = GroupReduce(line, [own, pair, core, diagonal])
     grad_input_sum.relay()
-    branch_turned = line.run(
-        lambda *v: gathered(v, with_all=False), b.own, b.pair, b_core, upper, lower
-    )
-    out_terms = line.run(product, branch_turned, mixed)
-    attn_terms = line.run(product, normed_turned, grad_qkv)
-    r_attn = RingReduce(line, [attn_terms, out_terms], n, qkv_wide)
+    attn_terms, attn_far = line.run(lambda a, b: product(a, b, n, (qkv_wide,)), normed_turned, grad_qkv)
+    r_attn = RingReduce(line, [attn_terms, out_terms], [attn_far, out_far], n, qkv_wide)
     r_feed.wait(hops)
     r_attn.start(1)
-    grad_w_feed = r_feed.total()
+    grad_w_gate, grad_w_up = r_feed.total([(hidden_wide, False)] * 2)
+    layer_sum = GroupReduce(line, layer_part)
     r_attn.wait(1)
     r_attn.start(2)
     _, grad_tokens, gain_attn_terms = line.run(
@@ -899,53 +932,47 @@
     )
     gain_terms = jnp.concatenate([gain_attn_terms, gain_mlp_terms], axis=0).reshape(2, n, part)
     gain_terms = jnp.take(gain_terms, offsets, axis=1).reshape(2, depth)
-    gain_steps = [("fsdp", 4, 1), ("fsdp", 4, 2)] + [("dp", n, 1 << i) for i in range((n - 1).bit_length())]
-    flying = []
-
-    def gain_send():
-        if gain_steps:
-            axis, size, bit = gain_steps.pop(0)
-            flying.append(line.send(gain_terms, axis, [(i, i ^ bit) for i in range(size)]))
-
-    def gain_take(value):
-        return line.run(jnp.add, value, line.passed(flying.pop())) if flying else value
-
-    for _ in range(2):
-        gain_send()
-        gain_terms = gain_take(gain_terms)
-    for hop in range(2, hops - 1):
+
+    def gain_step(axis, bit):
+        nonlocal gain_terms
+        size = lax.axis_size(axis)
+        other = line.passed(line.send(gain_terms, axis, [(i, i ^ bit) for i in range(size)]))
+        gain_terms = line.run(jnp.add, gain_terms, other)
+
+    gain_step("fsdp", 1)
+    gain_step("fsdp", 2)
+    steps = [1 << i for i in range((n - 1).bit_length())]
+    for hop in range(2, hops):
         r_attn.wait(hop)
         r_attn.start(hop + 1)
-    gain_send()
-    layer_sum = GroupReduce(line, layer_part)
-    layer_sum.relay()
-    grad_tokens = line.run(lambda at, v: shuffle(at, n, v), offsets, grad_tokens)
-    r_attn.wait(hops - 1)
-    r_attn.start(hops)
-    while len(gain_steps) > 1:
-        gain_terms = gain_take(gain_terms)
-        gain_send()
+        if hop == 2:
+            layer_sum.relay()
+            grad_tokens = line.run(lambda at, v: shuffle(at, n, v), offsets, grad_tokens)
+        if len(steps) > 1:
+            gain_step("dp", steps.pop(0))
+    while len(steps) > 1:
+        gain_step("dp", steps.pop(0))
     layer_own = line.run(lambda at, *v: shuffle(at, n, *v), offsets, hidden, *layer_sum.terms())
+    gain_step("dp", steps.pop(0))
     r_attn.wait(hops)
-    while flying:
-        gain_terms = gain_take(gain_terms)
-        gain_send()
-    grad_attn = r_attn.total()
+    key_wide, value_wide = w_key.shape[1], w_value.shape[1]
+    grad_w_attn = r_attn.total(
+        [(heads_wide, False), (key_wide, True), (value_wide, True), (heads_wide, True)]
+    )
     gain_own = lax.dynamic_slice(gain_terms, (0, me * part), (2, part))
 
-    value_at = heads_wide + w_key.shape[1]
     return (
         layer_own,
         grad_tokens,
         gain_own[0],
-        grad_attn[:, :heads_wide],
-        grad_attn[:, heads_wide:value_at],
-        grad_attn[:, value_at:qkv_wide],
-        grad_attn[:, qkv_wide:].T,
+        grad_w_attn[0],
+        grad_w_attn[1].T,
+        grad_w_attn[2].T,
+        grad_w_attn[3],
         gain_own[1],
-        grad_w_feed[:, :hidden_wide],
-        grad_w_feed[:, hidden_wide:],
-        grad_down.T,
+        grad_w_gate,
+        grad_w_up,
+        grad_down,
     )
 
 

time: 568 us -> 567 us (level)
  local copies, waits for them, and re-layouts: 56.2 us -> 43.5 us
    slice x7 -> x0, local copies, waits for them, and re-layouts: 10.1 us -> none  [the longest x3 4.56 us: start(): far = [far[0][:, :self.split], far[0][:, self.split:]]]
    unnamed x140 -> x134, local copies, waits for them, and re-layouts: 27.5 us -> 26.1 us
  transfers between devices with their start and end apart: 85 -> 85, of which waited for: 40 -> 45; matrix products, arithmetic and copies ran while one was open for 8% -> 6% of each run, Pallas kernels for 43% -> 45%
where the time goes in v4:
time: 567 us; the launch traced here: 557 us
  Pallas kernels  262 us (46%)
  waiting for transfers between devices  160 us (28%)
  starting transfers between devices  72.4 us (13%)
  local copies, waits for them, and re-layouts  43.5 us (8%)
  other arithmetic  18.1 us (3%)
    ppermute x85, waiting for transfers between devices, send(): return lax.ppermute(self.after(value), axis, pairs)  160 us
    ppermute x85, starting transfers between devices, send(): return lax.ppermute(self.after(value), axis, pairs)  72.4 us
    pallas_call x4, Pallas kernels, product(): pl.pallas_call(product_kernel, grid=(8,), in_specs=[by_rows(step, total),...  47.1 us
    pallas_call x2, Pallas kernels, spread(): pl.pallas_call(functools.partial(spread_kernel, n, split), grid=(4,), in_...  33.5 us
    pallas_call x2, Pallas kernels, attend_back(): pl.pallas_call(functools.partial(attention_backward, [len(group) for grou...  33.4 us
    pallas_call x9, Pallas kernels, grow(): pl.pallas_call(functools.partial(grow_kernel, split, narrow, len(products...  26.8 us
    unnamed x134, local copies, waits for them, and re-layouts  26.1 us
    pallas_call x4, Pallas kernels, gathered(): pl.pallas_call(functools.partial(gathered_kernel, with_all), grid=(4,), i...  22.7 us
  transfers between devices with their start and end apart: 85, of which 45 were waited for; matrix products, arithmetic and copies ran while one was open for 6% of the time, Pallas kernels for 45%

profile of v4, /device:TPU:0, one launch (start us, length us, event | category | flops | bytes accessed | tf_op | source)
XLA Modules:
  0.0 556.8 jit_solution(18259708815178350338)
XLA Ops:
  12.7 10.0 %collective-permute-done.refs_12_.refs_15_.refs_16_ = bf16[272,1152]{1,0:T(8,128)(2,1)S(1)} collective-permute-done((bf16[272,1152]{1,0:T(8,128)(2,1)S(1)}, bf16[272,1152]{1,0:T(8,128)(2,1)S(1)}, u32[]{:S(2)}, u32[]{:S(2)}) %collective-permute-start) | collective-permute-done | bytes 626720 | tf_op jit(solution)/shard_map/ppermute | solution.py:60
  33.0 5.9 %collective-permute-done.2.refs_11_.refs_14_.refs_15_ = bf16[272,1152]{1,0:T(8,128)(2,1)S(1)} collective-permute-done((bf16[272,1152]{1,0:T(8,128)(2,1)S(1)}, bf16[272,1152]{1,0:T(8,128)(2,1)S(1)}, u32[]{:S(2)}, u32[]{:S(2)}) %collective-permute-start.2) | collective-permute-done | bytes 626720 | tf_op jit(solution)/shard_map/ppermute | solution.py:60
  44.1 10.0 %collective-permute-done.4.refs_10_.refs_13_.refs_14_ = bf16[272,1152]{1,0:T(8,128)(2,1)S(1)} collective-permute-done((bf16[272,1152]{1,0:T(8,128)(2,1)}, bf16[272,1152]{1,0:T(8,128)(2,1)S(1)}, u32[]{:S(2)}, u32[]{:S(2)}) %collective-permute-start.4) | collective-permute-done | bytes 626720 | tf_op jit(solution)/shard_map/ppermute | solution.py:60
  62.4 4.9 gathered.4.refs_0_
  83.4 20.0 %attend.1 = (bf16[2048,1024]{1,0:T(8,128)(2,1)}, bf16[1024,512]{1,0:T(8,128)(2,1)}, bf16[1024,128]{1,0:T(8,128)(2,1)}, bf16[1024,512]{1,0:T(8,128)(2,1)}, f32[10...) custom-call(bf16[1024,2176]{1,0:T(8,128)(2,1)} %gathered.4.refs_0_, ...), custom_call_target="tpu_custom_call" | custom-call | tf_op jit(solution)/shard_map/attend/pallas_call | solution.py:301
  112.2 6.3 %gathered.5 = (bf16[1024,2048]{1,0:T(8,128)(2,1)}, bf16[2048,1024]{1,0:T(8,128)(2,1)}) custom-call(bf16[256,2048]{1,0:T(8,128)(2,1)} %shuffle.5.own.rest_ref, bf16[256,2048]{1,0:T(8,128)(2,1)} %collective-permute-done.16.pair, bf16[256,2048]{1,0:T(8,128)(2,1)} %copy-done.34, bf16[128,2048]{1,0:T(8,128)(2,1)} %copy-done.54, bf16[128,2048]{1,0:T(8,128)(2,1)} %copy-done.55), custom_call_target="tpu_custom_call" | custom-call | tf_op jit(solution)/shard_map/gathered/pallas_call | solution.py:481
  122.5 18.1 %collective-permute-done.22.refs_6_ = bf16[256,2816]{1,0:T(8,128)(2,1)S(1)} collective-permute-done((bf16[256,2816]{1,0:T(8,128)(2,1)}, bf16[256,2816]{1,0:T(8,128)(2,1)S(1)}, u32[]{:S(2)}, u32[]{:S(2)}) %collective-permute-start.22) | collective-permute-done | bytes 1441824 | tf_op jit(solution)/shard_map/ppermute | solution.py:60
  146.8 3.8 join.1
  152.2 22.9 %collective-permute-done.25.refs_5_ = bf16[256,2816]{1,0:T(8,128)(2,1)S(1)} collective-permute-done((bf16[256,2816]{1,0:T(8,128)(2,1)}, bf16[256,2816]{1,0:T(8,128)(2,1)S(1)}, u32[]{:S(2)}, u32[]{:S(2)}) %collective-permute-start.25) | collective-permute-done | bytes 1441824 | tf_op jit(solution)/shard_map/ppermute | solution.py:60
  184.0 6.3 %gathered.6 = (bf16[1024,2048]{1,0:T(8,128)(2,1)}, bf16[2048,1024]{1,0:T(8,128)(2,1)}) custom-call(bf16[256,2048]{1,0:T(8,128)(2,1)} %get-tuple-element.780.own, bf16[256,2048]{1,0:T(8,128)(2,1)} %copy-done.15, bf16[256,2048]{1,0:T(8,128)(2,1)} %collective-permute-done.27.core, bf16[128,2048]{1,0:T(8,128)(2,1)} %copy-done.56, bf16[128,2048]{1,0:T(8,128)(2,1)} %copy-done.57), custom_call_target="tpu_custom_call" | custom-call | tf_op jit(solution)/shard_map/gathered/pallas_call | solution.py:481
  190.2 5.8 %collective-permute-done.30.refs_8_ = bf16[256,1408]{1,0:T(8,128)(2,1)} collective-permute-done((bf16[256,1408]{1,0:T(8,128)(2,1)}, bf16[256,1408]{1,0:T(8,128)(2,1)}, u32[]{:S(2)}, u32[]{:S(2)}) %collective-permute-start.30) | collective-permute-done | bytes 720928 | tf_op jit(solution)/shard_map/ppermute | solution.py:60
  199.5 20.8 %feed.1 = (bf16[1024,1408]{1,0:T(8,128)(2,1)}, bf16[1024,1408]{1,0:T(8,128)(2,1)}, bf16[1024,1408]{1,0:T(8,128)(2,1)}) custom-call(bf16[1024,2048]{1,0:T(8,128)(2,1)} %get-tuple-element.796.refs_0_, bf16[256,2816]{1,0:T(8,128)(2,1)} %copy-done, bf16[256,2816]{1,0:T(8,128)(2,1)} %collective-permute-done.13.refs_2_, ...), custom_call_target="tpu_custom_call" | custom-call | tf_op jit(solution)/shard_map/feed/pallas_call | solution.py:534
  222.5 12.1 %product.4 = (bf16[2048,1408]{1,0:T(8,128)(2,1)}, bf16[256,768]{1,0:T(8,128)(2,1)}, bf16[256,640]{1,0:T(8,128)(2,1)}) custom-call(bf16[2048,1024]{1,0:T(8,128)(2,1)} %get-tuple-element.818.left, bf16[1024,1408]{1,0:T(8,128)(2,1)} %get-tuple-element.952.right.refs_0_), custom_call_target="tpu_custom_call" | custom-call | tf_op jit(solution)/shard_map/product/pallas_call | solution.py:611
  239.5 14.4 %collective-permute-done.36.refs_7_.refs_5_ = bf16[256,1408]{1,0:T(8,128)(2,1)S(1)} collective-permute-done((bf16[256,1408]{1,0:T(8,128)(2,1)}, bf16[256,1408]{1,0:T(8,128)(2,1)S(1)}, u32[]{:S(2)}, u32[]{:S(2)}) %collective-permute-start.36) | collective-permute-done | bytes 720928 | tf_op jit(solution)/shard_map/ppermute | solution.py:60
  258.1 6.7 %collective-permute-done.39.refs_11_.refs_9_ = bf16[256,640]{1,0:T(8,128)(2,1)S(1)} collective-permute-done((bf16[256,640]{1,0:T(8,128)(2,1)S(1)}, bf16[256,640]{1,0:T(8,128)(2,1)S(1)}, u32[]{:S(2)}, u32[]{:S(2)}) %collective-permute-start.39) | collective-permute-done | bytes 327712 | tf_op jit(solution)/shard_map/ppermute | solution.py:60
  275.7 12.5 %feed_back.1.right.refs_0_ = bf16[1024,2816]{1,0:T(8,128)(2,1)} custom-call(bf16[1024,2048]{1,0:T(8,128)(2,1)} %get-tuple-element.858.refs_0_, bf16[1024,1408]{1,0:T(8,128)(2,1)} %get-tuple-element.859.refs_1_, bf16[1024,1408]{1,0:T(8,128)(2,1)} %get-tuple-element.860.refs_2_, bf16[256,1408]{1,0:T(8,128)(2,1)} %bitcast.34, bf16[256,1408]{1,0:T(8,128)(2,1)} %copy-done.19, ...), custom_call_target="tpu_custom_call" | custom-call | tf_op jit(solution)/shard_map/feed_back/pallas_call | solution.py:561
  295.0 18.0 %product.5 = (bf16[2048,2816]{1,0:T(8,128)(2,1)}, bf16[256,1408]{1,0:T(8,128)(2,1)}, bf16[256,1408]{1,0:T(8,128)(2,1)}) custom-call(bf16[2048,1024]{1,0:T(8,128)(2,1)} %get-tuple-element.886.left, bf16[1024,2816]{1,0:T(8,128)(2,1)} %feed_back.1.right.refs_0_), custom_call_target="tpu_custom_call" | custom-call | tf_op jit(solution)/shard_map/product/pallas_call | solution.py:611
  321.4 20.9 %spread.2 = (bf16[256,2048]{1,0:T(8,128)(2,1)}, bf16[256,2048]{1,0:T(8,128)(2,1)}, bf16[256,2048]{1,0:T(8,128)(2,1)}, bf16[256,2048]{1,0:T(8,128)(2,1)}) custom-call(bf16[1024,2816]{1,0:T(8,128)(2,1)} %feed_back.1.right.refs_0_, bf16[256,2816]{1,0:T(8,128)(2,1)} %copy-done, bf16[256,2816]{1,0:T(8,128)(2,1)} %collective-permute-done.13.refs_2_, ...), custom_call_target="tpu_custom_call" | custom-call | tf_op jit(solution)/shard_map/spread/pallas_call | solution.py:583
  364.1 12.5 %spread.3 = (bf16[256,2048]{1,0:T(8,128)(2,1)}, bf16[256,2048]{1,0:T(8,128)(2,1)}, bf16[256,2048]{1,0:T(8,128)(2,1)}, bf16[256,2048]{1,0:T(8,128)(2,1)}) custom-call(bf16[1024,1408]{1,0:T(8,128)(2,1)} %get-tuple-element.952.right.refs_0_, bf16[256,1408]{1,0:T(8,128)(2,1)} %bitcast.35, bf16[256,1408]{1,0:T(8,128)(2,1)} %copy-done.19, ...), custom_call_target="tpu_custom_call" | custom-call | tf_op jit(solution)/shard_map/spread/pallas_call | solution.py:583
  381.1 3.9 grow.13
  387.2 5.0 norm_back.2
  396.1 16.7 %attend_back.2 = (bf16[1024,640]{1,0:T(8,128)(2,1)}, bf16[256,2048]{1,0:T(8,128)(2,1)}, bf16[256,2048]{1,0:T(8,128)(2,1)}) custom-call(bf16[256,2048]{1,0:T(8,128)(2,1)} %get-tuple-element.1056.refs_0_.own, bf16[256,2048]{1,0:T(8,128)(2,1)} %copy-done.16, bf16[1024,512]{1,0:T(8,128)(2,1)} %get-tuple-element.1072.refs_2_.refs_3_, ...), custom_call_target="tpu_custom_call" | custom-call | tf_op jit(solution)/shard_map/attend_back/pallas_call | solution.py:419
  412.8 3.8 collective-permute-done.54.refs_2_
  416.8 3.9 grow.14
  425.1 5.2 gathered.7.left
  430.3 8.1 %product.6 = (bf16[2048,512]{1,0:T(8,128)(2,1)}, bf16[256,512]{1,0:T(8,128)(2,1)}) custom-call(bf16[2048,1024]{1,0:T(8,128)(2,1)} %gathered.7.left, bf16[1024,512]{1,0:T(8,128)(2,1)} %get-tuple-element.1065.right), custom_call_target="tpu_custom_call" | custom-call | tf_op jit(solution)/shard_map/product/pallas_call | solution.py:611
  439.0 16.7 %attend_back.3 = (bf16[1024,640]{1,0:T(8,128)(2,1)}, bf16[256,2048]{1,0:T(8,128)(2,1)}, bf16[256,2048]{1,0:T(8,128)(2,1)}) custom-call(bf16[256,2048]{1,0:T(8,128)(2,1)} %copy-done.3, bf16[128,2048]{1,0:T(8,128)(2,1)} %copy-done.21, bf16[128,2048]{1,0:T(8,128)(2,1)} %copy-done.22, ...), custom_call_target="tpu_custom_call", output_to_operand_aliasing={{0}: (19, {})} | custom-call | tf_op jit(solution)/shard_map/attend_back/pallas_call | solution.py:419
  465.1 8.9 %product.7 = (bf16[2048,640]{1,0:T(8,128)(2,1)}, bf16[256,640]{1,0:T(8,128)(2,1)}) custom-call(bf16[2048,1024]{1,0:T(8,128)(2,1)} %get-tuple-element.1105.left, bf16[1024,640]{1,0:T(8,128)(2,1)} %get-tuple-element.1106.right), custom_call_target="tpu_custom_call" | custom-call | tf_op jit(solution)/shard_map/product/pallas_call | solution.py:611
  488.9 5.2 norm_back.3
  516.2 5.2 collective-permute-done.78
  529.4 11.6 %collective-permute-done.81 = f32[2,2048]{1,0:T(2,128)S(1)} collective-permute-done((f32[2,2048]{1,0:T(2,128)S(1)}, f32[2,2048]{1,0:T(2,128)S(1)}, u32[]{:S(2)}, u32[]{:S(2)}) %collective-permute-start.81) | collective-permute-done | bytes 16416 | tf_op jit(solution)/shard_map/ppermute | solution.py:60
  543.0 4.2 shuffle.7
  (372 shorter events, 224.7 us)
Async XLA Ops:
  28.7 26.6 %collective-permute-start.8 = (bf16[256,2176]{1,0:T(8,128)(2,1)}, bf16[256,2176]{1,0:T(8,128)(2,1)}, u32[]{:S(2)}, u32[]{:S(2)}) collective-permute-start(bf16[256,2176]{1,0:T(8,128)(2,1)} %pad_maximum_fusion.1.own), channel_id=1, source_target_pairs={{0,2},{1,3},{2,0},{3,1},{4,6},{5,7},{6,4},{7,5},{8,10},{9,11},{10,... | collective-permute-start | bytes 3342344 | tf_op jit(solution)/shard_map/ppermute | solution.py:60
  70.6 32.8 %collective-permute-start.12 = (bf16[256,2816]{1,0:T(8,128)(2,1)S(1)}, bf16[256,2816]{1,0:T(8,128)(2,1)}, u32[]{:S(2)}, u32[]{:S(2)}) collective-permute-start(bf16[256,2816]{1,0:T(8,128)(2,1)S(1)} %pad_maximum_fusion.refs_1_), channel_id=1, source_target_pairs={{0,8},{8,16},{16,24},{24,28},{28,20},{20,12},{12,4},{4,0},{1,9},{9... | collective-permute-start | bytes 4325384 | tf_op jit(solution)/shard_map/ppermute | solution.py:60
  72.0 32.5 %collective-permute-start.13 = (bf16[256,2816]{1,0:T(8,128)(2,1)S(1)}, bf16[256,2816]{1,0:T(8,128)(2,1)}, u32[]{:S(2)}, u32[]{:S(2)}) collective-permute-start(bf16[256,2816]{1,0:T(8,128)(2,1)S(1)} %pad_maximum_fusion.refs_1_), channel_id=1, source_target_pairs={{8,0},{16,8},{24,16},{28,24},{20,28},{12,20},{4,12},{0,4},{9,1},{1... | collective-permute-start | bytes 4325384 | tf_op jit(solution)/shard_map/ppermute | solution.py:60
  77.5 27.0 %collective-permute-start.16 = (bf16[256,2048]{1,0:T(8,128)(2,1)S(1)}, bf16[256,2048]{1,0:T(8,128)(2,1)}, u32[]{:S(2)}, u32[]{:S(2)}) collective-permute-start(bf16[256,2048]{1,0:T(8,128)(2,1)S(1)} %copy-done.2), channel_id=1, source_target_pairs={{0,2},{1,3},{2,0},{3,1},{4,6},{5,7},{6,4},{7,5},{8,10},{9,11},{10,... | collective-permute-start | bytes 3145736 | tf_op jit(solution)/shard_map/ppermute | solution.py:60
  106.4 34.1 %collective-permute-start.22 = (bf16[256,2816]{1,0:T(8,128)(2,1)}, bf16[256,2816]{1,0:T(8,128)(2,1)S(1)}, u32[]{:S(2)}, u32[]{:S(2)}) collective-permute-start(bf16[256,2816]{1,0:T(8,128)(2,1)} %collective-permute-done.12.refs_7_), channel_id=1, source_target_pairs={{0,8},{8,16},{16,24},{24,28},{28,20},{20,12},{12,4},{4,0},{1,9},{9... | collective-permute-start | bytes 4325384 | tf_op jit(solution)/shard_map/ppermute | solution.py:60
  107.7 34.2 %collective-permute-start.23 = (bf16[256,2816]{1,0:T(8,128)(2,1)}, bf16[256,2816]{1,0:T(8,128)(2,1)}, u32[]{:S(2)}, u32[]{:S(2)}) collective-permute-start(bf16[256,2816]{1,0:T(8,128)(2,1)} %collective-permute-done.13.refs_2_), channel_id=1, source_target_pairs={{8,0},{16,8},{24,16},{28,24},{20,28},{12,20},{4,12},{0,4},{9,1},{1... | collective-permute-start | bytes 4325384 | tf_op jit(solution)/shard_map/ppermute | solution.py:60
  120.9 23.0 %collective-permute-start.20 = (bf16[256,2048]{1,0:T(8,128)(2,1)}, bf16[256,2048]{1,0:T(8,128)(2,1)}, u32[]{:S(2)}, u32[]{:S(2)}) collective-permute-start(bf16[256,2048]{1,0:T(8,128)(2,1)} %get-tuple-element.744), channel_id=1, source_target_pairs={{0,1},{1,0},{2,3},{3,2},{4,5},{5,4},{6,7},{7,6},{8,9},{9,8},{10,11... | collective-permute-start | bytes 3145736 | tf_op jit(solution)/shard_map/ppermute | solution.py:60
  120.9 25.9 %collective-permute-start.21 = (bf16[256,2048]{1,0:T(8,128)(2,1)}, bf16[256,2048]{1,0:T(8,128)(2,1)}, u32[]{:S(2)}, u32[]{:S(2)}) collective-permute-start(bf16[256,2048]{1,0:T(8,128)(2,1)} %plus.4), channel_id=1, source_target_pairs={{0,2},{1,3},{2,0},{3,1},{4,6},{5,7},{6,4},{7,5},{8,10},{9,11},{10,... | collective-permute-start | bytes 3145736 | tf_op jit(solution)/shard_map/ppermute | solution.py:60
  141.9 33.2 %collective-permute-start.25 = (bf16[256,2816]{1,0:T(8,128)(2,1)}, bf16[256,2816]{1,0:T(8,128)(2,1)S(1)}, u32[]{:S(2)}, u32[]{:S(2)}) collective-permute-start(bf16[256,2816]{1,0:T(8,128)(2,1)} %copy-done.9), channel_id=1, source_target_pairs={{0,8},{8,16},{16,24},{24,28},{28,20},{20,12},{12,4},{4,0},{1,9},{9... | collective-permute-start | bytes 4325384 | tf_op jit(solution)/shard_map/ppermute | solution.py:60
  143.0 33.2 %collective-permute-start.26 = (bf16[256,2816]{1,0:T(8,128)(2,1)}, bf16[256,2816]{1,0:T(8,128)(2,1)S(1)}, u32[]{:S(2)}, u32[]{:S(2)}) collective-permute-start(bf16[256,2816]{1,0:T(8,128)(2,1)} %collective-permute-done.23.refs_3_), channel_id=1, source_target_pairs={{8,0},{16,8},{24,16},{28,24},{20,28},{12,20},{4,12},{0,4},{9,1},{1... | collective-permute-start | bytes 4325384 | tf_op jit(solution)/shard_map/ppermute | solution.py:60
  150.7 29.5 %collective-permute-start.24 = (bf16[256,2048]{1,0:T(8,128)(2,1)}, bf16[256,2048]{1,0:T(8,128)(2,1)S(1)}, u32[]{:S(2)}, u32[]{:S(2)}) collective-permute-start(bf16[256,2048]{1,0:T(8,128)(2,1)} %get-tuple-element.780.own), channel_id=1, source_target_pairs={{0,2},{1,3},{2,0},{3,1},{4,6},{5,7},{6,4},{7,5},{8,10},{9,11},{10,... | collective-permute-start | bytes 3145736 | tf_op jit(solution)/shard_map/ppermute | solution.py:60
  317.4 25.0 %collective-permute-start.46 = (bf16[256,1408]{1,0:T(8,128)(2,1)}, bf16[256,1408]{1,0:T(8,128)(2,1)S(1)}, u32[]{:S(2)}, u32[]{:S(2)}) collective-permute-start(bf16[256,1408]{1,0:T(8,128)(2,1)} %get-tuple-element.902), channel_id=1, source_target_pairs={{0,8},{8,16},{16,24},{24,28},{28,20},{20,12},{12,4},{4,0},{1,9},{9... | collective-permute-start | bytes 2162696 | tf_op jit(solution)/shard_map/ppermute | solution.py:60
  317.7 24.7 %collective-permute-start.47 = (bf16[256,1408]{1,0:T(8,128)(2,1)}, bf16[256,1408]{1,0:T(8,128)(2,1)S(1)}, u32[]{:S(2)}, u32[]{:S(2)}) collective-permute-start(bf16[256,1408]{1,0:T(8,128)(2,1)} %get-tuple-element.904), channel_id=1, source_target_pairs={{8,0},{16,8},{24,16},{28,24},{20,28},{12,20},{4,12},{0,4},{9,1},{1... | collective-permute-start | bytes 2162696 | tf_op jit(solution)/shard_map/ppermute | solution.py:60
  319.4 26.6 %collective-permute-start.48 = (bf16[256,1408]{1,0:T(8,128)(2,1)}, bf16[256,1408]{1,0:T(8,128)(2,1)S(1)}, u32[]{:S(2)}, u32[]{:S(2)}) collective-permute-start(bf16[256,1408]{1,0:T(8,128)(2,1)} %get-tuple-element.926), channel_id=1, source_target_pairs={{0,8},{8,16},{16,24},{24,28},{28,20},{20,12},{12,4},{4,0},{1,9},{9... | collective-permute-start | bytes 2162696 | tf_op jit(solution)/shard_map/ppermute | solution.py:60
  319.7 26.4 %collective-permute-start.49 = (bf16[256,1408]{1,0:T(8,128)(2,1)}, bf16[256,1408]{1,0:T(8,128)(2,1)S(1)}, u32[]{:S(2)}, u32[]{:S(2)}) collective-permute-start(bf16[256,1408]{1,0:T(8,128)(2,1)} %get-tuple-element.928), channel_id=1, source_target_pairs={{8,0},{16,8},{24,16},{28,24},{20,28},{12,20},{4,12},{0,4},{9,1},{1... | collective-permute-start | bytes 2162696 | tf_op jit(solution)/shard_map/ppermute | solution.py:60
  351.1 27.7 %collective-permute-start.52 = (bf16[256,2816]{1,0:T(8,128)(2,1)}, bf16[256,2816]{1,0:T(8,128)(2,1)S(1)}, u32[]{:S(2)}, u32[]{:S(2)}) collective-permute-start(bf16[256,2816]{1,0:T(8,128)(2,1)} %get-tuple-element.971), channel_id=1, source_target_pairs={{0,8},{8,16},{16,24},{24,28},{28,20},{20,12},{12,4},{4,0},{1,9},{9... | collective-permute-start | bytes 4325384 | tf_op jit(solution)/shard_map/ppermute | solution.py:60
  351.5 27.5 %collective-permute-start.53 = (bf16[256,2816]{1,0:T(8,128)(2,1)}, bf16[256,2816]{1,0:T(8,128)(2,1)S(1)}, u32[]{:S(2)}, u32[]{:S(2)}) collective-permute-start(bf16[256,2816]{1,0:T(8,128)(2,1)} %get-tuple-element.973), channel_id=1, source_target_pairs={{8,0},{16,8},{24,16},{28,24},{20,28},{12,20},{4,12},{0,4},{9,1},{1... | collective-permute-start | bytes 4325384 | tf_op jit(solution)/shard_map/ppermute | solution.py:60
  359.8 27.4 %collective-permute-start.56 = (bf16[256,2048]{1,0:T(8,128)(2,1)}, bf16[256,2048]{1,0:T(8,128)(2,1)}, u32[]{:S(2)}, u32[]{:S(2)}) collective-permute-start(bf16[256,2048]{1,0:T(8,128)(2,1)} %get-tuple-element.990), channel_id=1, source_target_pairs={{0,1},{1,0},{2,3},{3,2},{4,5},{5,4},{6,7},{7,6},{8,9},{9,8},{10,11... | collective-permute-start | bytes 3145736 | tf_op jit(solution)/shard_map/ppermute | solution.py:60
  359.9 27.3 %collective-permute-start.57 = (bf16[256,2048]{1,0:T(8,128)(2,1)}, bf16[256,2048]{1,0:T(8,128)(2,1)}, u32[]{:S(2)}, u32[]{:S(2)}) collective-permute-start(bf16[256,2048]{1,0:T(8,128)(2,1)} %plus.5), channel_id=1, source_target_pairs={{0,2},{1,3},{2,0},{3,1},{4,6},{5,7},{6,4},{7,5},{8,10},{9,11},{10,... | collective-permute-start | bytes 3145736 | tf_op jit(solution)/shard_map/ppermute | solution.py:60
  385.0 31.6 %collective-permute-start.54 = (bf16[256,2816]{1,0:T(8,128)(2,1)}, bf16[256,2816]{1,0:T(8,128)(2,1)}, u32[]{:S(2)}, u32[]{:S(2)}) collective-permute-start(bf16[256,2816]{1,0:T(8,128)(2,1)} %get-tuple-element.985), channel_id=1, source_target_pairs={{0,8},{8,16},{16,24},{24,28},{28,20},{20,12},{12,4},{4,0},{1,9},{9... | collective-permute-start | bytes 4325384 | tf_op jit(solution)/shard_map/ppermute | solution.py:60
  385.4 31.4 %collective-permute-start.55 = (bf16[256,2816]{1,0:T(8,128)(2,1)}, bf16[256,2816]{1,0:T(8,128)(2,1)}, u32[]{:S(2)}, u32[]{:S(2)}) collective-permute-start(bf16[256,2816]{1,0:T(8,128)(2,1)} %get-tuple-element.987), channel_id=1, source_target_pairs={{8,0},{16,8},{24,16},{28,24},{20,28},{12,20},{4,12},{0,4},{9,1},{1... | collective-permute-start | bytes 4325384 | tf_op jit(solution)/shard_map/ppermute | solution.py:60
  392.3 28.5 %collective-permute-start.61 = (bf16[256,2048]{1,0:T(8,128)(2,1)}, bf16[256,2048]{1,0:T(8,128)(2,1)S(1)}, u32[]{:S(2)}, u32[]{:S(2)}) collective-permute-start(bf16[256,2048]{1,0:T(8,128)(2,1)} %get-tuple-element.1056.refs_0_.own), channel_id=1, source_target_pairs={{0,2},{1,3},{2,0},{3,1},{4,6},{5,7},{6,4},{7,5},{8,10},{9,11},{10,... | collective-permute-start | bytes 3145736 | tf_op jit(solution)/shard_map/ppermute | solution.py:60
  421.4 52.6 %collective-permute-start.59 = (bf16[256,2816]{1,0:T(8,128)(2,1)}, bf16[256,2816]{1,0:T(8,128)(2,1)S(1)}, u32[]{:S(2)}, u32[]{:S(2)}) collective-permute-start(bf16[256,2816]{1,0:T(8,128)(2,1)} %get-tuple-element.1044), channel_id=1, source_target_pairs={{0,8},{8,16},{16,24},{24,28},{28,20},{20,12},{12,4},{4,0},{1,9},{9... | collective-permute-start | bytes 4325384 | tf_op jit(solution)/shard_map/ppermute | solution.py:60
  422.2 51.9 %collective-permute-start.60 = (bf16[256,2816]{1,0:T(8,128)(2,1)}, bf16[256,2816]{1,0:T(8,128)(2,1)}, u32[]{:S(2)}, u32[]{:S(2)}) collective-permute-start(bf16[256,2816]{1,0:T(8,128)(2,1)} %get-tuple-element.1046), channel_id=1, source_target_pairs={{8,0},{16,8},{24,16},{28,24},{20,28},{12,20},{4,12},{0,4},{9,1},{1... | collective-permute-start | bytes 4325384 | tf_op jit(solution)/shard_map/ppermute | solution.py:60
  463.0 24.6 %collective-permute-start.72 = (bf16[256,2048]{1,0:T(8,128)(2,1)}, bf16[256,2048]{1,0:T(8,128)(2,1)S(1)}, u32[]{:S(2)}, u32[]{:S(2)}) collective-permute-start(bf16[256,2048]{1,0:T(8,128)(2,1)} %get-tuple-element.1144), channel_id=1, source_target_pairs={{0,1},{1,0},{2,3},{3,2},{4,5},{5,4},{6,7},{7,6},{8,9},{9,8},{10,11... | collective-permute-start | bytes 3145736 | tf_op jit(solution)/shard_map/ppermute | solution.py:60
  463.1 25.8 %collective-permute-start.73 = (bf16[256,2048]{1,0:T(8,128)(2,1)}, bf16[256,2048]{1,0:T(8,128)(2,1)}, u32[]{:S(2)}, u32[]{:S(2)}) collective-permute-start(bf16[256,2048]{1,0:T(8,128)(2,1)} %plus.6), channel_id=1, source_target_pairs={{0,2},{1,3},{2,0},{3,1},{4,6},{5,7},{6,4},{7,5},{8,10},{9,11},{10,... | collective-permute-start | bytes 3145736 | tf_op jit(solution)/shard_map/ppermute | solution.py:60
  480.7 27.8 %collective-permute-start.66 = (bf16[128,2048]{1,0:T(8,128)(2,1)}, bf16[128,2048]{1,0:T(8,128)(2,1)}, u32[]{:S(2)}, u32[]{:S(2)}) collective-permute-start(bf16[128,2048]{1,0:T(8,128)(2,1)} %get-tuple-element.1119), channel_id=1, source_target_pairs={{0,1},{1,0},{2,3},{3,2},{4,5},{5,4},{6,7},{7,6},{8,9},{9,8},{10,11... | collective-permute-start | bytes 1572872 | tf_op jit(solution)/shard_map/ppermute | solution.py:60
  483.2 25.3 %collective-permute-start.67 = (bf16[128,2048]{1,0:T(8,128)(2,1)S(1)}, bf16[128,2048]{1,0:T(8,128)(2,1)}, u32[]{:S(2)}, u32[]{:S(2)}) collective-permute-start(bf16[128,2048]{1,0:T(8,128)(2,1)S(1)} %copy-done.50), channel_id=1, source_target_pairs={{0,1},{1,0},{2,3},{3,2},{4,5},{5,4},{6,7},{7,6},{8,9},{9,8},{10,11... | collective-permute-start | bytes 1572872 | tf_op jit(solution)/shard_map/ppermute | solution.py:60
  510.9 30.1 %collective-permute-start.76 = (bf16[256,2048]{1,0:T(8,128)(2,1)}, bf16[256,2048]{1,0:T(8,128)(2,1)S(1)}, u32[]{:S(2)}, u32[]{:S(2)}) collective-permute-start(bf16[256,2048]{1,0:T(8,128)(2,1)} %get-tuple-element.1189), channel_id=1, source_target_pairs={{0,1},{1,0},{2,3},{3,2},{4,5},{5,4},{6,7},{7,6},{8,9},{9,8},{10,11... | collective-permute-start | bytes 3145736 | tf_op jit(solution)/shard_map/ppermute | solution.py:60
  510.9 30.1 %collective-permute-start.77 = (bf16[256,2048]{1,0:T(8,128)(2,1)}, bf16[256,2048]{1,0:T(8,128)(2,1)S(1)}, u32[]{:S(2)}, u32[]{:S(2)}) collective-permute-start(bf16[256,2048]{1,0:T(8,128)(2,1)} %plus.7), channel_id=1, source_target_pairs={{0,2},{1,3},{2,0},{3,1},{4,6},{5,7},{6,4},{7,5},{8,10},{9,11},{10,... | collective-permute-start | bytes 3145736 | tf_op jit(solution)/shard_map/ppermute | solution.py:60
  525.7 26.8 %collective-permute-start.83 = (bf16[256,1152]{1,0:T(8,128)(2,1)}, bf16[256,1152]{1,0:T(8,128)(2,1)S(1)}, u32[]{:S(2)}, u32[]{:S(2)}) collective-permute-start(bf16[256,1152]{1,0:T(8,128)(2,1)} %get-tuple-element.1242), channel_id=1, source_target_pairs={{0,8},{8,16},{16,24},{24,28},{28,20},{20,12},{12,4},{4,0},{1,9},{9... | collective-permute-start | bytes 1769480 | tf_op jit(solution)/shard_map/ppermute | solution.py:60
  527.3 25.2 %collective-permute-start.84 = (bf16[256,1152]{1,0:T(8,128)(2,1)}, bf16[256,1152]{1,0:T(8,128)(2,1)S(1)}, u32[]{:S(2)}, u32[]{:S(2)}) collective-permute-start(bf16[256,1152]{1,0:T(8,128)(2,1)} %get-tuple-element.1244), channel_id=1, source_target_pairs={{8,0},{16,8},{24,16},{28,24},{20,28},{12,20},{4,12},{0,4},{9,1},{1... | collective-permute-start | bytes 1769480 | tf_op jit(solution)/shard_map/ppermute | solution.py:60
  (116 other events, 909.3 us)

commit v5 on v4

--- a/solution.py
+++ b/solution.py
@@ -388,7 +388,7 @@
         return grad_keys, grad_vals
 
     nothing = jnp.zeros((rows, LANES), WIDE)
-    grad_keys, grad_vals = lax.fori_loop(0, pairs, heads, (nothing, nothing), unroll=2)
+    grad_keys, grad_vals = lax.fori_loop(0, pairs, heads, (nothing, nothing))
     grad_keys = (grad_keys + pltpu.roll(grad_keys, HEAD_DIM, 1)) * scale
     grad_keys = grad_keys * cosine - turn(grad_keys, first) * sine
     grad_vals = grad_vals + pltpu.roll(grad_vals, HEAD_DIM, 1)
@@ -452,21 +452,21 @@
 
 
 def gathered_kernel(with_all, own, pair, core, upper, lower, *outs):
-    all_ref = outs[0] if with_all else None
-    turned_ref = outs[-1] if len(outs) == 2 or not with_all else None
+    outs, made_ref = outs[:-1], outs[-1]
     for block, refs in enumerate(((own,), (pair,), (core,), (upper, lower))):
 
         @pl.when(pl.program_id(0) == block)
         def _(refs=refs):
             at = 0
             for ref in refs:
-                value = ref[...]
-                end = at + value.shape[0]
-                if all_ref is not None:
-                    all_ref[at:end, :] = value
-                if turned_ref is not None:
-                    turned_ref[:, at:end] = value.T
+                end = at + ref.shape[0]
+                made_ref[at:end, :] = ref[...]
                 at = end
+
+    if with_all:
+        outs[0][...] = made_ref[...]
+    if not with_all or len(outs) == 2:
+        outs[-1][...] = made_ref[...].T
 
 
 def gathered(blocks, with_all=True, with_turned=True):
@@ -484,6 +484,7 @@
         in_specs=[whole(v) for v in blocks],
         out_specs=out_specs,
         out_shape=out_shape,
+        scratch_shapes=[pltpu.VMEM((rows, depth), LOW)],
         name="gathered",
     )(*blocks)
     return tuple(out) if len(out) == 2 else out[0]
@@ -769,16 +770,28 @@
     )(order, *values)
 
 
-def tables(segment_block):
-    rows = segment_block.shape[0]
-    places = jnp.arange(rows, dtype=jnp.int32)
-    same = segment_block[:, None] == segment_block[None, :]
-    first_index = jnp.min(jnp.where(same, places[None, :], rows), axis=1)
-    offsets = (places - first_index).astype(WIDE)
+UNIT = 64
+
+
+def angle_table(rows):
     half = HEAD_DIM // 2
-    frequencies = jnp.exp(jnp.arange(half, dtype=WIDE) * (-2.0 * math.log(ROPE_BASE) / HEAD_DIM))
-    angles = offsets[:, None] * frequencies[None, :]
-    cosine, sine = jnp.cos(angles), jnp.sin(angles)
+    frequencies = np.exp(np.arange(half, dtype=np.float32) * np.float32(-2.0 * math.log(ROPE_BASE) / HEAD_DIM))
+    angles = np.arange(rows, dtype=np.float32)[:, None] * frequencies[None, :].astype(np.float32)
+    both = np.concatenate([np.cos(angles), np.sin(angles)], axis=1).astype(np.float32)
+    return both.reshape(rows // UNIT, UNIT, HEAD_DIM)
+
+
+def tables(segment_blocks):
+    blocks, rows = segment_blocks.shape
+    units = rows // UNIT
+    marks = segment_blocks[:, ::UNIT]
+    places = jnp.arange(units, dtype=jnp.int32)
+    same = marks[:, :, None] == marks[:, None, :]
+    first = jnp.min(jnp.where(same, places[None, None, :], units), axis=2)
+    chosen = (places[None, :] - first).reshape(-1)
+    both = jnp.take(jnp.asarray(angle_table(rows)), chosen, axis=0, mode="clip").reshape(-1, HEAD_DIM)
+    half = HEAD_DIM // 2
+    cosine, sine = both[:, :half], both[:, half:]
     return jnp.concatenate([cosine] * 4, axis=1), jnp.concatenate([sine] * 4, axis=1)
 
 
@@ -821,8 +834,7 @@
     y = GroupGather(line, own_grads)
     segment_blocks = token_rows[:, depth].astype(jnp.int32).reshape(-1, rows)
     column, row = segment_blocks.reshape(-1, 1), segment_blocks[:, None, :]
-    cosine, sine = line.run(lambda v: jax.vmap(tables)(v), segment_blocks)
-    cosine, sine = cosine.reshape(-1, LANES), sine.reshape(-1, LANES)
+    cosine, sine = line.run(tables, segment_blocks)
     gains = attn.extra(2).astype(WIDE)
     gain_one, gain_two = gains[0:1], gains[1:2]
 
@@ -941,24 +953,25 @@
 
     gain_step("fsdp", 1)
     gain_step("fsdp", 2)
+    layer_sum.relay()
     steps = [1 << i for i in range((n - 1).bit_length())]
     for hop in range(2, hops):
         r_attn.wait(hop)
         r_attn.start(hop + 1)
         if hop == 2:
-            layer_sum.relay()
             grad_tokens = line.run(lambda at, v: shuffle(at, n, v), offsets, grad_tokens)
-        if len(steps) > 1:
+        if hop < hops - 1 and len(steps) > 1:
             gain_step("dp", steps.pop(0))
+    layer_own = line.run(lambda at, *v: shuffle(at, n, *v), offsets, hidden, *layer_sum.terms())
     while len(steps) > 1:
         gain_step("dp", steps.pop(0))
-    layer_own = line.run(lambda at, *v: shuffle(at, n, *v), offsets, hidden, *layer_sum.terms())
-    gain_step("dp", steps.pop(0))
+    flying = line.send(gain_terms, "dp", [(i, i ^ steps[0]) for i in range(n)])
     r_attn.wait(hops)
     key_wide, value_wide = w_key.shape[1], w_value.shape[1]
     grad_w_attn = r_attn.total(
         [(heads_wide, False), (key_wide, True), (value_wide, True), (heads_wide, True)]
     )
+    gain_terms = gain_terms + line.passed(flying)
     gain_own = lax.dynamic_slice(gain_terms, (0, me * part), (2, part))
 
     return (

time: 567 us -> 564 us (level)
    unnamed x134 -> x136, local copies, waits for them, and re-layouts: 26.1 us -> 23.2 us
  transfers between devices with their start and end apart: 85 -> 85, of which waited for: 45 -> 44; matrix products, arithmetic and copies ran while one was open for 6% -> 6% of each run, Pallas kernels for 45% -> 45%
where the time goes in v5:
time: 564 us; the launch traced here: 554 us
  Pallas kernels  264 us (47%)
  waiting for transfers between devices  159 us (28%)
  starting transfers between devices  73.3 us (13%)
  local copies, waits for them, and re-layouts  39.9 us (7%)
  other arithmetic  16.1 us (3%)
    ppermute x85, waiting for transfers between devices, send(): return lax.ppermute(self.after(value), axis, pairs)  159 us
    ppermute x85, starting transfers between devices, send(): return lax.ppermute(self.after(value), axis, pairs)  73.3 us
    pallas_call x4, Pallas kernels, product(): pl.pallas_call(product_kernel, grid=(8,), in_specs=[by_rows(step, total),...  47.1 us
    pallas_call x2, Pallas kernels, attend_back(): pl.pallas_call(functools.partial(attention_backward, [len(group) for grou...  34.8 us
    pallas_call x2, Pallas kernels, spread(): pl.pallas_call(functools.partial(spread_kernel, n, split), grid=(4,), in_...  33.5 us
    pallas_call x9, Pallas kernels, grow(): pl.pallas_call(functools.partial(grow_kernel, split, narrow, len(products...  26.8 us
    pallas_call x4, Pallas kernels, gathered(): pl.pallas_call(functools.partial(gathered_kernel, with_all), grid=(4,), i...  23.3 us
    unnamed x136, local copies, waits for them, and re-layouts  23.2 us
  transfers between devices with their start and end apart: 85, of which 44 were waited for; matrix products, arithmetic and copies ran while one was open for 6% of the time, Pallas kernels for 45%

profile of v5, /device:TPU:0, one launch (start us, length us, event | category | flops | bytes accessed | tf_op | source)
XLA Modules:
  0.0 553.5 jit_solution(331657388102926257)
XLA Ops:
  12.7 10.0 %collective-permute-done.refs_12_.refs_15_.refs_16_ = bf16[272,1152]{1,0:T(8,128)(2,1)S(1)} collective-permute-done((bf16[272,1152]{1,0:T(8,128)(2,1)S(1)}, bf16[272,1152]{1,0:T(8,128)(2,1)S(1)}, u32[]{:S(2)}, u32[]{:S(2)}) %collective-permute-start) | collective-permute-done | bytes 626720 | tf_op jit(solution)/shard_map/ppermute | solution.py:60
  33.0 5.9 %collective-permute-done.2.refs_11_.refs_14_.refs_15_ = bf16[272,1152]{1,0:T(8,128)(2,1)S(1)} collective-permute-done((bf16[272,1152]{1,0:T(8,128)(2,1)S(1)}, bf16[272,1152]{1,0:T(8,128)(2,1)S(1)}, u32[]{:S(2)}, u32[]{:S(2)}) %collective-permute-start.2) | collective-permute-done | bytes 626720 | tf_op jit(solution)/shard_map/ppermute | solution.py:60
  44.1 9.8 %collective-permute-done.4.refs_10_.refs_13_.refs_14_ = bf16[272,1152]{1,0:T(8,128)(2,1)S(1)} collective-permute-done((bf16[272,1152]{1,0:T(8,128)(2,1)S(1)}, bf16[272,1152]{1,0:T(8,128)(2,1)S(1)}, u32[]{:S(2)}, u32[]{:S(2)}) %collective-permute-start.4) | collective-permute-done | bytes 626720 | tf_op jit(solution)/shard_map/ppermute | solution.py:60
  60.4 5.0 gathered.4.refs_0_
  80.3 20.0 %attend.1 = (bf16[2048,1024]{1,0:T(8,128)(2,1)}, bf16[1024,512]{1,0:T(8,128)(2,1)}, bf16[1024,128]{1,0:T(8,128)(2,1)}, bf16[1024,512]{1,0:T(8,128)(2,1)}, f32[10...) custom-call(bf16[1024,2176]{1,0:T(8,128)(2,1)} %gathered.4.refs_0_, ...), custom_call_target="tpu_custom_call" | custom-call | tf_op jit(solution)/shard_map/attend/pallas_call | solution.py:301
  108.7 6.5 %gathered.5 = (bf16[1024,2048]{1,0:T(8,128)(2,1)}, bf16[2048,1024]{1,0:T(8,128)(2,1)}) custom-call(bf16[256,2048]{1,0:T(8,128)(2,1)} %shuffle.5.own.rest_ref, bf16[256,2048]{1,0:T(8,128)(2,1)} %collective-permute-done.16.pair, bf16[256,2048]{1,0:T(8,128)(2,1)} %collective-permute-done.17.core, bf16[128,2048]{1,0:T(8,128)(2,1)} %copy-done.55, ...), custom_call_target="tpu_custom_call" | custom-call | tf_op jit(solution)/shard_map/gathered/pallas_call | solution.py:481
  119.5 19.5 %collective-permute-done.22.refs_6_ = bf16[256,2816]{1,0:T(8,128)(2,1)S(1)} collective-permute-done((bf16[256,2816]{1,0:T(8,128)(2,1)}, bf16[256,2816]{1,0:T(8,128)(2,1)S(1)}, u32[]{:S(2)}, u32[]{:S(2)}) %collective-permute-start.22) | collective-permute-done | bytes 1441824 | tf_op jit(solution)/shard_map/ppermute | solution.py:60
  143.5 3.7 join.1
  148.7 24.8 %collective-permute-done.25.refs_5_ = bf16[256,2816]{1,0:T(8,128)(2,1)S(1)} collective-permute-done((bf16[256,2816]{1,0:T(8,128)(2,1)}, bf16[256,2816]{1,0:T(8,128)(2,1)S(1)}, u32[]{:S(2)}, u32[]{:S(2)}) %collective-permute-start.25) | collective-permute-done | bytes 1441824 | tf_op jit(solution)/shard_map/ppermute | solution.py:60
  182.1 6.4 %gathered.6 = (bf16[1024,2048]{1,0:T(8,128)(2,1)}, bf16[2048,1024]{1,0:T(8,128)(2,1)}) custom-call(bf16[256,2048]{1,0:T(8,128)(2,1)} %get-tuple-element.774.own, bf16[256,2048]{1,0:T(8,128)(2,1)} %copy-done.15, bf16[256,2048]{1,0:T(8,128)(2,1)} %collective-permute-done.27.core, bf16[128,2048]{1,0:T(8,128)(2,1)} %copy-done.57, bf16[128,2048]{1,0:T(8,128)(2,1)} %copy-done.58), custom_call_target="tpu_custom_call" | custom-call | tf_op jit(solution)/shard_map/gathered/pallas_call | solution.py:481
  188.4 5.5 collective-permute-done.30.refs_8_
  197.3 20.9 %feed.1 = (bf16[1024,1408]{1,0:T(8,128)(2,1)}, bf16[1024,1408]{1,0:T(8,128)(2,1)}, bf16[1024,1408]{1,0:T(8,128)(2,1)}) custom-call(bf16[1024,2048]{1,0:T(8,128)(2,1)} %get-tuple-element.790.refs_0_, bf16[256,2816]{1,0:T(8,128)(2,1)} %copy-done, bf16[256,2816]{1,0:T(8,128)(2,1)} %collective-permute-done.13.refs_2_, ...), custom_call_target="tpu_custom_call" | custom-call | tf_op jit(solution)/shard_map/feed/pallas_call | solution.py:535
  220.2 12.1 %product.4 = (bf16[2048,1408]{1,0:T(8,128)(2,1)}, bf16[256,768]{1,0:T(8,128)(2,1)}, bf16[256,640]{1,0:T(8,128)(2,1)}) custom-call(bf16[2048,1024]{1,0:T(8,128)(2,1)} %get-tuple-element.812.left, bf16[1024,1408]{1,0:T(8,128)(2,1)} %get-tuple-element.946.right.refs_0_), custom_call_target="tpu_custom_call" | custom-call | tf_op jit(solution)/shard_map/product/pallas_call | solution.py:612
  237.8 14.2 %collective-permute-done.36.refs_7_.refs_5_ = bf16[256,1408]{1,0:T(8,128)(2,1)S(1)} collective-permute-done((bf16[256,1408]{1,0:T(8,128)(2,1)}, bf16[256,1408]{1,0:T(8,128)(2,1)S(1)}, u32[]{:S(2)}, u32[]{:S(2)}) %collective-permute-start.36) | collective-permute-done | bytes 720928 | tf_op jit(solution)/shard_map/ppermute | solution.py:60
  256.2 7.0 %collective-permute-done.39.refs_11_.refs_9_ = bf16[256,640]{1,0:T(8,128)(2,1)S(1)} collective-permute-done((bf16[256,640]{1,0:T(8,128)(2,1)S(1)}, bf16[256,640]{1,0:T(8,128)(2,1)S(1)}, u32[]{:S(2)}, u32[]{:S(2)}) %collective-permute-start.39) | collective-permute-done | bytes 327712 | tf_op jit(solution)/shard_map/ppermute | solution.py:60
  273.7 12.5 %feed_back.1.right.refs_0_ = bf16[1024,2816]{1,0:T(8,128)(2,1)} custom-call(bf16[1024,2048]{1,0:T(8,128)(2,1)} %get-tuple-element.852.refs_0_, bf16[1024,1408]{1,0:T(8,128)(2,1)} %get-tuple-element.853.refs_1_, bf16[1024,1408]{1,0:T(8,128)(2,1)} %get-tuple-element.854.refs_2_, bf16[256,1408]{1,0:T(8,128)(2,1)} %bitcast.27, bf16[256,1408]{1,0:T(8,128)(2,1)} %copy-done.19, ...), custom_call_target="tpu_custom_call" | custom-call | tf_op jit(solution)/shard_map/feed_back/pallas_call | solution.py:562
  292.7 17.9 %product.5 = (bf16[2048,2816]{1,0:T(8,128)(2,1)}, bf16[256,1408]{1,0:T(8,128)(2,1)}, bf16[256,1408]{1,0:T(8,128)(2,1)}) custom-call(bf16[2048,1024]{1,0:T(8,128)(2,1)} %get-tuple-element.880.left, bf16[1024,2816]{1,0:T(8,128)(2,1)} %feed_back.1.right.refs_0_), custom_call_target="tpu_custom_call" | custom-call | tf_op jit(solution)/shard_map/product/pallas_call | solution.py:612
  319.3 20.9 %spread.2 = (bf16[256,2048]{1,0:T(8,128)(2,1)}, bf16[256,2048]{1,0:T(8,128)(2,1)}, bf16[256,2048]{1,0:T(8,128)(2,1)}, bf16[256,2048]{1,0:T(8,128)(2,1)}) custom-call(bf16[1024,2816]{1,0:T(8,128)(2,1)} %feed_back.1.right.refs_0_, bf16[256,2816]{1,0:T(8,128)(2,1)} %copy-done, bf16[256,2816]{1,0:T(8,128)(2,1)} %collective-permute-done.13.refs_2_, ...), custom_call_target="tpu_custom_call" | custom-call | tf_op jit(solution)/shard_map/spread/pallas_call | solution.py:584
  361.7 12.5 %spread.3 = (bf16[256,2048]{1,0:T(8,128)(2,1)}, bf16[256,2048]{1,0:T(8,128)(2,1)}, bf16[256,2048]{1,0:T(8,128)(2,1)}, bf16[256,2048]{1,0:T(8,128)(2,1)}) custom-call(bf16[1024,1408]{1,0:T(8,128)(2,1)} %get-tuple-element.946.right.refs_0_, bf16[256,1408]{1,0:T(8,128)(2,1)} %bitcast.28, bf16[256,1408]{1,0:T(8,128)(2,1)} %copy-done.19, ...), custom_call_target="tpu_custom_call" | custom-call | tf_op jit(solution)/shard_map/spread/pallas_call | solution.py:584
  378.7 3.9 grow.13
  384.6 5.0 norm_back.2
  393.5 17.4 %attend_back.2 = (bf16[1024,640]{1,0:T(8,128)(2,1)}, bf16[256,2048]{1,0:T(8,128)(2,1)}, bf16[256,2048]{1,0:T(8,128)(2,1)}) custom-call(bf16[256,2048]{1,0:T(8,128)(2,1)} %get-tuple-element.1050.refs_0_.own, bf16[256,2048]{1,0:T(8,128)(2,1)} %copy-done.16, bf16[1024,512]{1,0:T(8,128)(2,1)} %get-tuple-element.1066.refs_2_.refs_3_, ...), custom_call_target="tpu_custom_call" | custom-call | tf_op jit(solution)/shard_map/attend_back/pallas_call | solution.py:419
  414.5 3.9 grow.14
  423.0 5.4 gathered.7.left
  428.4 8.1 %product.6 = (bf16[2048,512]{1,0:T(8,128)(2,1)}, bf16[256,512]{1,0:T(8,128)(2,1)}) custom-call(bf16[2048,1024]{1,0:T(8,128)(2,1)} %gathered.7.left, bf16[1024,512]{1,0:T(8,128)(2,1)} %get-tuple-element.1059.right), custom_call_target="tpu_custom_call" | custom-call | tf_op jit(solution)/shard_map/product/pallas_call | solution.py:612
  437.1 17.4 %attend_back.3 = (bf16[1024,640]{1,0:T(8,128)(2,1)}, bf16[256,2048]{1,0:T(8,128)(2,1)}, bf16[256,2048]{1,0:T(8,128)(2,1)}) custom-call(bf16[256,2048]{1,0:T(8,128)(2,1)} %copy-done.3, bf16[128,2048]{1,0:T(8,128)(2,1)} %copy-done.22, bf16[128,2048]{1,0:T(8,128)(2,1)} %copy-done.23, ...), custom_call_target="tpu_custom_call", output_to_operand_aliasing={{0}: (19, {})} | custom-call | tf_op jit(solution)/shard_map/attend_back/pallas_call | solution.py:419
  463.9 9.0 %product.7 = (bf16[2048,640]{1,0:T(8,128)(2,1)}, bf16[256,640]{1,0:T(8,128)(2,1)}) custom-call(bf16[2048,1024]{1,0:T(8,128)(2,1)} %get-tuple-element.1099.left, bf16[1024,640]{1,0:T(8,128)(2,1)} %get-tuple-element.1100.right), custom_call_target="tpu_custom_call" | custom-call | tf_op jit(solution)/shard_map/product/pallas_call | solution.py:612
  476.0 3.6 last.4
  487.6 5.3 norm_back.3
  513.5 9.8 %collective-permute-done.80 = f32[2,2048]{1,0:T(2,128)S(1)} collective-permute-done((f32[2,2048]{1,0:T(2,128)S(1)}, f32[2,2048]{1,0:T(2,128)S(1)}, u32[]{:S(2)}, u32[]{:S(2)}) %collective-permute-start.80) | collective-permute-done | bytes 16416 | tf_op jit(solution)/shard_map/ppermute | solution.py:60
  531.6 4.2 shuffle.7
  537.2 6.4 %collective-permute-done.81 = f32[2,2048]{1,0:T(2,128)S(1)} collective-permute-done((f32[2,2048]{1,0:T(2,128)S(1)}, f32[2,2048]{1,0:T(2,128)S(1)}, u32[]{:S(2)}, u32[]{:S(2)}) %collective-permute-start.81) | collective-permute-done | bytes 16416 | tf_op jit(solution)/shard_map/ppermute | solution.py:60
  (377 shorter events, 217.4 us)
Async XLA Ops:
  28.7 26.6 %collective-permute-start.8 = (bf16[256,2176]{1,0:T(8,128)(2,1)}, bf16[256,2176]{1,0:T(8,128)(2,1)}, u32[]{:S(2)}, u32[]{:S(2)}) collective-permute-start(bf16[256,2176]{1,0:T(8,128)(2,1)} %pad_maximum_fusion.1.own), channel_id=1, source_target_pairs={{0,2},{1,3},{2,0},{3,1},{4,6},{5,7},{6,4},{7,5},{8,10},{9,11},{10,... | collective-permute-start | bytes 3342344 | tf_op jit(solution)/shard_map/ppermute | solution.py:60
  68.6 33.1 %collective-permute-start.12 = (bf16[256,2816]{1,0:T(8,128)(2,1)S(1)}, bf16[256,2816]{1,0:T(8,128)(2,1)}, u32[]{:S(2)}, u32[]{:S(2)}) collective-permute-start(bf16[256,2816]{1,0:T(8,128)(2,1)S(1)} %pad_maximum_fusion.refs_1_), channel_id=1, source_target_pairs={{0,8},{8,16},{16,24},{24,28},{28,20},{20,12},{12,4},{4,0},{1,9},{9... | collective-permute-start | bytes 4325384 | tf_op jit(solution)/shard_map/ppermute | solution.py:60
  70.1 32.8 %collective-permute-start.13 = (bf16[256,2816]{1,0:T(8,128)(2,1)S(1)}, bf16[256,2816]{1,0:T(8,128)(2,1)}, u32[]{:S(2)}, u32[]{:S(2)}) collective-permute-start(bf16[256,2816]{1,0:T(8,128)(2,1)S(1)} %pad_maximum_fusion.refs_1_), channel_id=1, source_target_pairs={{8,0},{16,8},{24,16},{28,24},{20,28},{12,20},{4,12},{0,4},{9,1},{1... | collective-permute-start | bytes 4325384 | tf_op jit(solution)/shard_map/ppermute | solution.py:60
  74.4 28.5 %collective-permute-start.16 = (bf16[256,2048]{1,0:T(8,128)(2,1)S(1)}, bf16[256,2048]{1,0:T(8,128)(2,1)}, u32[]{:S(2)}, u32[]{:S(2)}) collective-permute-start(bf16[256,2048]{1,0:T(8,128)(2,1)S(1)} %copy-done.2), channel_id=1, source_target_pairs={{0,2},{1,3},{2,0},{3,1},{4,6},{5,7},{6,4},{7,5},{8,10},{9,11},{10,... | collective-permute-start | bytes 3145736 | tf_op jit(solution)/shard_map/ppermute | solution.py:60
  104.8 34.1 %collective-permute-start.22 = (bf16[256,2816]{1,0:T(8,128)(2,1)}, bf16[256,2816]{1,0:T(8,128)(2,1)S(1)}, u32[]{:S(2)}, u32[]{:S(2)}) collective-permute-start(bf16[256,2816]{1,0:T(8,128)(2,1)} %collective-permute-done.12.refs_7_), channel_id=1, source_target_pairs={{0,8},{8,16},{16,24},{24,28},{28,20},{20,12},{12,4},{4,0},{1,9},{9... | collective-permute-start | bytes 4325384 | tf_op jit(solution)/shard_map/ppermute | solution.py:60
  105.6 34.4 %collective-permute-start.23 = (bf16[256,2816]{1,0:T(8,128)(2,1)}, bf16[256,2816]{1,0:T(8,128)(2,1)}, u32[]{:S(2)}, u32[]{:S(2)}) collective-permute-start(bf16[256,2816]{1,0:T(8,128)(2,1)} %collective-permute-done.13.refs_2_), channel_id=1, source_target_pairs={{8,0},{16,8},{24,16},{28,24},{20,28},{12,20},{4,12},{0,4},{9,1},{1... | collective-permute-start | bytes 4325384 | tf_op jit(solution)/shard_map/ppermute | solution.py:60
  117.6 24.5 %collective-permute-start.20 = (bf16[256,2048]{1,0:T(8,128)(2,1)}, bf16[256,2048]{1,0:T(8,128)(2,1)}, u32[]{:S(2)}, u32[]{:S(2)}) collective-permute-start(bf16[256,2048]{1,0:T(8,128)(2,1)} %get-tuple-element.738), channel_id=1, source_target_pairs={{0,1},{1,0},{2,3},{3,2},{4,5},{5,4},{6,7},{7,6},{8,9},{9,8},{10,11... | collective-permute-start | bytes 3145736 | tf_op jit(solution)/shard_map/ppermute | solution.py:60
  117.9 25.5 %collective-permute-start.21 = (bf16[256,2048]{1,0:T(8,128)(2,1)}, bf16[256,2048]{1,0:T(8,128)(2,1)}, u32[]{:S(2)}, u32[]{:S(2)}) collective-permute-start(bf16[256,2048]{1,0:T(8,128)(2,1)} %plus.4), channel_id=1, source_target_pairs={{0,2},{1,3},{2,0},{3,1},{4,6},{5,7},{6,4},{7,5},{8,10},{9,11},{10,... | collective-permute-start | bytes 3145736 | tf_op jit(solution)/shard_map/ppermute | solution.py:60
  140.0 33.5 %collective-permute-start.25 = (bf16[256,2816]{1,0:T(8,128)(2,1)}, bf16[256,2816]{1,0:T(8,128)(2,1)S(1)}, u32[]{:S(2)}, u32[]{:S(2)}) collective-permute-start(bf16[256,2816]{1,0:T(8,128)(2,1)} %copy-done.9), channel_id=1, source_target_pairs={{0,8},{8,16},{16,24},{24,28},{28,20},{20,12},{12,4},{4,0},{1,9},{9... | collective-permute-start | bytes 4325384 | tf_op jit(solution)/shard_map/ppermute | solution.py:60
  140.9 33.2 %collective-permute-start.26 = (bf16[256,2816]{1,0:T(8,128)(2,1)}, bf16[256,2816]{1,0:T(8,128)(2,1)S(1)}, u32[]{:S(2)}, u32[]{:S(2)}) collective-permute-start(bf16[256,2816]{1,0:T(8,128)(2,1)} %collective-permute-done.23.refs_3_), channel_id=1, source_target_pairs={{8,0},{16,8},{24,16},{28,24},{20,28},{12,20},{4,12},{0,4},{9,1},{1... | collective-permute-start | bytes 4325384 | tf_op jit(solution)/shard_map/ppermute | solution.py:60
  147.2 31.0 %collective-permute-start.24 = (bf16[256,2048]{1,0:T(8,128)(2,1)}, bf16[256,2048]{1,0:T(8,128)(2,1)S(1)}, u32[]{:S(2)}, u32[]{:S(2)}) collective-permute-start(bf16[256,2048]{1,0:T(8,128)(2,1)} %get-tuple-element.774.own), channel_id=1, source_target_pairs={{0,2},{1,3},{2,0},{3,1},{4,6},{5,7},{6,4},{7,5},{8,10},{9,11},{10,... | collective-permute-start | bytes 3145736 | tf_op jit(solution)/shard_map/ppermute | solution.py:60
  195.2 22.9 %collective-permute-start.32 = (bf16[256,1408]{1,0:T(8,128)(2,1)S(1)}, bf16[256,1408]{1,0:T(8,128)(2,1)S(1)}, u32[]{:S(2)}, u32[]{:S(2)}) collective-permute-start(bf16[256,1408]{1,0:T(8,128)(2,1)S(1)} %bitcast.25), channel_id=1, source_target_pairs={{0,8},{8,16},{16,24},{24,28},{28,20},{20,12},{12,4},{4,0},{1,9},{9... | collective-permute-start | bytes 2162696 | tf_op jit(solution)/shard_map/ppermute | solution.py:60
  196.1 22.0 %collective-permute-start.33 = (bf16[256,1408]{1,0:T(8,128)(2,1)S(1)}, bf16[256,1408]{1,0:T(8,128)(2,1)S(1)}, u32[]{:S(2)}, u32[]{:S(2)}) collective-permute-start(bf16[256,1408]{1,0:T(8,128)(2,1)S(1)} %bitcast.26), channel_id=1, source_target_pairs={{8,0},{16,8},{24,16},{28,24},{20,28},{12,20},{4,12},{0,4},{9,1},{1... | collective-permute-start | bytes 2162696 | tf_op jit(solution)/shard_map/ppermute | solution.py:60
  315.0 25.2 %collective-permute-start.46 = (bf16[256,1408]{1,0:T(8,128)(2,1)}, bf16[256,1408]{1,0:T(8,128)(2,1)S(1)}, u32[]{:S(2)}, u32[]{:S(2)}) collective-permute-start(bf16[256,1408]{1,0:T(8,128)(2,1)} %get-tuple-element.896), channel_id=1, source_target_pairs={{0,8},{8,16},{16,24},{24,28},{28,20},{20,12},{12,4},{4,0},{1,9},{9... | collective-permute-start | bytes 2162696 | tf_op jit(solution)/shard_map/ppermute | solution.py:60
  315.6 24.6 %collective-permute-start.47 = (bf16[256,1408]{1,0:T(8,128)(2,1)}, bf16[256,1408]{1,0:T(8,128)(2,1)S(1)}, u32[]{:S(2)}, u32[]{:S(2)}) collective-permute-start(bf16[256,1408]{1,0:T(8,128)(2,1)} %get-tuple-element.898), channel_id=1, source_target_pairs={{8,0},{16,8},{24,16},{28,24},{20,28},{12,20},{4,12},{0,4},{9,1},{1... | collective-permute-start | bytes 2162696 | tf_op jit(solution)/shard_map/ppermute | solution.py:60
  317.0 26.6 %collective-permute-start.48 = (bf16[256,1408]{1,0:T(8,128)(2,1)}, bf16[256,1408]{1,0:T(8,128)(2,1)S(1)}, u32[]{:S(2)}, u32[]{:S(2)}) collective-permute-start(bf16[256,1408]{1,0:T(8,128)(2,1)} %get-tuple-element.920), channel_id=1, source_target_pairs={{0,8},{8,16},{16,24},{24,28},{28,20},{20,12},{12,4},{4,0},{1,9},{9... | collective-permute-start | bytes 2162696 | tf_op jit(solution)/shard_map/ppermute | solution.py:60
  317.6 26.3 %collective-permute-start.49 = (bf16[256,1408]{1,0:T(8,128)(2,1)}, bf16[256,1408]{1,0:T(8,128)(2,1)S(1)}, u32[]{:S(2)}, u32[]{:S(2)}) collective-permute-start(bf16[256,1408]{1,0:T(8,128)(2,1)} %get-tuple-element.922), channel_id=1, source_target_pairs={{8,0},{16,8},{24,16},{28,24},{20,28},{12,20},{4,12},{0,4},{9,1},{1... | collective-permute-start | bytes 2162696 | tf_op jit(solution)/shard_map/ppermute | solution.py:60
  348.8 27.7 %collective-permute-start.52 = (bf16[256,2816]{1,0:T(8,128)(2,1)}, bf16[256,2816]{1,0:T(8,128)(2,1)S(1)}, u32[]{:S(2)}, u32[]{:S(2)}) collective-permute-start(bf16[256,2816]{1,0:T(8,128)(2,1)} %get-tuple-element.965), channel_id=1, source_target_pairs={{0,8},{8,16},{16,24},{24,28},{28,20},{20,12},{12,4},{4,0},{1,9},{9... | collective-permute-start | bytes 4325384 | tf_op jit(solution)/shard_map/ppermute | solution.py:60
  349.4 27.4 %collective-permute-start.53 = (bf16[256,2816]{1,0:T(8,128)(2,1)}, bf16[256,2816]{1,0:T(8,128)(2,1)S(1)}, u32[]{:S(2)}, u32[]{:S(2)}) collective-permute-start(bf16[256,2816]{1,0:T(8,128)(2,1)} %get-tuple-element.967), channel_id=1, source_target_pairs={{8,0},{16,8},{24,16},{28,24},{20,28},{12,20},{4,12},{0,4},{9,1},{1... | collective-permute-start | bytes 4325384 | tf_op jit(solution)/shard_map/ppermute | solution.py:60
  357.4 27.2 %collective-permute-start.56 = (bf16[256,2048]{1,0:T(8,128)(2,1)}, bf16[256,2048]{1,0:T(8,128)(2,1)}, u32[]{:S(2)}, u32[]{:S(2)}) collective-permute-start(bf16[256,2048]{1,0:T(8,128)(2,1)} %get-tuple-element.984), channel_id=1, source_target_pairs={{0,1},{1,0},{2,3},{3,2},{4,5},{5,4},{6,7},{7,6},{8,9},{9,8},{10,11... | collective-permute-start | bytes 3145736 | tf_op jit(solution)/shard_map/ppermute | solution.py:60
  357.5 27.1 %collective-permute-start.57 = (bf16[256,2048]{1,0:T(8,128)(2,1)}, bf16[256,2048]{1,0:T(8,128)(2,1)}, u32[]{:S(2)}, u32[]{:S(2)}) collective-permute-start(bf16[256,2048]{1,0:T(8,128)(2,1)} %plus.5), channel_id=1, source_target_pairs={{0,2},{1,3},{2,0},{3,1},{4,6},{5,7},{6,4},{7,5},{8,10},{9,11},{10,... | collective-permute-start | bytes 3145736 | tf_op jit(solution)/shard_map/ppermute | solution.py:60
  382.6 31.7 %collective-permute-start.54 = (bf16[256,2816]{1,0:T(8,128)(2,1)}, bf16[256,2816]{1,0:T(8,128)(2,1)}, u32[]{:S(2)}, u32[]{:S(2)}) collective-permute-start(bf16[256,2816]{1,0:T(8,128)(2,1)} %get-tuple-element.979), channel_id=1, source_target_pairs={{0,8},{8,16},{16,24},{24,28},{28,20},{20,12},{12,4},{4,0},{1,9},{9... | collective-permute-start | bytes 4325384 | tf_op jit(solution)/shard_map/ppermute | solution.py:60
  383.2 31.4 %collective-permute-start.55 = (bf16[256,2816]{1,0:T(8,128)(2,1)}, bf16[256,2816]{1,0:T(8,128)(2,1)}, u32[]{:S(2)}, u32[]{:S(2)}) collective-permute-start(bf16[256,2816]{1,0:T(8,128)(2,1)} %get-tuple-element.981), channel_id=1, source_target_pairs={{8,0},{16,8},{24,16},{28,24},{20,28},{12,20},{4,12},{0,4},{9,1},{1... | collective-permute-start | bytes 4325384 | tf_op jit(solution)/shard_map/ppermute | solution.py:60
  389.7 28.8 %collective-permute-start.61 = (bf16[256,2048]{1,0:T(8,128)(2,1)}, bf16[256,2048]{1,0:T(8,128)(2,1)S(1)}, u32[]{:S(2)}, u32[]{:S(2)}) collective-permute-start(bf16[256,2048]{1,0:T(8,128)(2,1)} %get-tuple-element.1050.refs_0_.own), channel_id=1, source_target_pairs={{0,2},{1,3},{2,0},{3,1},{4,6},{5,7},{6,4},{7,5},{8,10},{9,11},{10,... | collective-permute-start | bytes 3145736 | tf_op jit(solution)/shard_map/ppermute | solution.py:60
  419.1 53.7 %collective-permute-start.59 = (bf16[256,2816]{1,0:T(8,128)(2,1)}, bf16[256,2816]{1,0:T(8,128)(2,1)S(1)}, u32[]{:S(2)}, u32[]{:S(2)}) collective-permute-start(bf16[256,2816]{1,0:T(8,128)(2,1)} %get-tuple-element.1038), channel_id=1, source_target_pairs={{0,8},{8,16},{16,24},{24,28},{28,20},{20,12},{12,4},{4,0},{1,9},{9... | collective-permute-start | bytes 4325384 | tf_op jit(solution)/shard_map/ppermute | solution.py:60
  420.0 52.9 %collective-permute-start.60 = (bf16[256,2816]{1,0:T(8,128)(2,1)}, bf16[256,2816]{1,0:T(8,128)(2,1)}, u32[]{:S(2)}, u32[]{:S(2)}) collective-permute-start(bf16[256,2816]{1,0:T(8,128)(2,1)} %get-tuple-element.1040), channel_id=1, source_target_pairs={{8,0},{16,8},{24,16},{28,24},{20,28},{12,20},{4,12},{0,4},{9,1},{1... | collective-permute-start | bytes 4325384 | tf_op jit(solution)/shard_map/ppermute | solution.py:60
  461.7 24.5 %collective-permute-start.68 = (bf16[256,2048]{1,0:T(8,128)(2,1)}, bf16[256,2048]{1,0:T(8,128)(2,1)S(1)}, u32[]{:S(2)}, u32[]{:S(2)}) collective-permute-start(bf16[256,2048]{1,0:T(8,128)(2,1)} %get-tuple-element.1118), channel_id=1, source_target_pairs={{0,1},{1,0},{2,3},{3,2},{4,5},{5,4},{6,7},{7,6},{8,9},{9,8},{10,11... | collective-permute-start | bytes 3145736 | tf_op jit(solution)/shard_map/ppermute | solution.py:60
  461.9 25.8 %collective-permute-start.69 = (bf16[256,2048]{1,0:T(8,128)(2,1)}, bf16[256,2048]{1,0:T(8,128)(2,1)}, u32[]{:S(2)}, u32[]{:S(2)}) collective-permute-start(bf16[256,2048]{1,0:T(8,128)(2,1)} %plus.6), channel_id=1, source_target_pairs={{0,2},{1,3},{2,0},{3,1},{4,6},{5,7},{6,4},{7,5},{8,10},{9,11},{10,... | collective-permute-start | bytes 3145736 | tf_op jit(solution)/shard_map/ppermute | solution.py:60
  503.3 26.4 %collective-permute-start.74 = (bf16[256,2048]{1,0:T(8,128)(2,1)}, bf16[256,2048]{1,0:T(8,128)(2,1)S(1)}, u32[]{:S(2)}, u32[]{:S(2)}) collective-permute-start(bf16[256,2048]{1,0:T(8,128)(2,1)} %get-tuple-element.1169), channel_id=1, source_target_pairs={{0,1},{1,0},{2,3},{3,2},{4,5},{5,4},{6,7},{7,6},{8,9},{9,8},{10,11... | collective-permute-start | bytes 3145736 | tf_op jit(solution)/shard_map/ppermute | solution.py:60
  503.3 26.4 %collective-permute-start.75 = (bf16[256,2048]{1,0:T(8,128)(2,1)}, bf16[256,2048]{1,0:T(8,128)(2,1)S(1)}, u32[]{:S(2)}, u32[]{:S(2)}) collective-permute-start(bf16[256,2048]{1,0:T(8,128)(2,1)} %plus.7), channel_id=1, source_target_pairs={{0,2},{1,3},{2,0},{3,1},{4,6},{5,7},{6,4},{7,5},{8,10},{9,11},{10,... | collective-permute-start | bytes 3145736 | tf_op jit(solution)/shard_map/ppermute | solution.py:60
  527.6 21.4 %collective-permute-start.83 = (bf16[256,1152]{1,0:T(8,128)(2,1)}, bf16[256,1152]{1,0:T(8,128)(2,1)S(1)}, u32[]{:S(2)}, u32[]{:S(2)}) collective-permute-start(bf16[256,1152]{1,0:T(8,128)(2,1)} %get-tuple-element.1229), channel_id=1, source_target_pairs={{0,8},{8,16},{16,24},{24,28},{28,20},{20,12},{12,4},{4,0},{1,9},{9... | collective-permute-start | bytes 1769480 | tf_op jit(solution)/shard_map/ppermute | solution.py:60
  529.0 20.0 %collective-permute-start.84 = (bf16[256,1152]{1,0:T(8,128)(2,1)}, bf16[256,1152]{1,0:T(8,128)(2,1)S(1)}, u32[]{:S(2)}, u32[]{:S(2)}) collective-permute-start(bf16[256,1152]{1,0:T(8,128)(2,1)} %get-tuple-element.1231), channel_id=1, source_target_pairs={{8,0},{16,8},{24,16},{28,24},{20,28},{12,20},{4,12},{0,4},{9,1},{1... | collective-permute-start | bytes 1769480 | tf_op jit(solution)/shard_map/ppermute | solution.py:60
  (117 other events, 929.8 us)

commit v6 on v5

--- a/solution.py
+++ b/solution.py
@@ -622,6 +622,9 @@
 def grow_kernel(split, narrow, count, *refs):
     ahead_terms, behind_terms = refs[:count], refs[count : 2 * count]
     ahead, behind, ahead_out, behind_out = refs[2 * count :]
+    step = ahead_out.shape[0]
+    rows = pl.ds(pl.multiple_of(pl.program_id(0) * step, step), step)
+    ahead, behind = ahead.at[rows, :], behind.at[rows, :]
     at = 0
     for ahead_term, behind_term in zip(ahead_terms, behind_terms):
         width = ahead_term.shape[1]
@@ -684,7 +687,7 @@
     wide = sum(v.shape[1] for v in products)
     narrow = away == n // 2 - 1
     step = part // 2
-    came_specs = [by_rows(step, v.shape[1]) for v in came]
+    came_specs = [pl.BlockSpec(memory_space=pltpu.VMEM) for _ in came]
 
     def rows_at(offset):
         return [pl.BlockSpec((step, v.shape[1]), lambda i: (2 * offset + i, 0)) for v in products]

time: 564 us -> 564 us (level)
  no operation moved by 1% of the time
where the time goes in v6:
time: 564 us; the launch traced here: 554 us
  Pallas kernels  264 us (47%)
  waiting for transfers between devices  159 us (28%)
  starting transfers between devices  73.4 us (13%)
  local copies, waits for them, and re-layouts  39.9 us (7%)
  other arithmetic  16.1 us (3%)
    ppermute x85, waiting for transfers between devices, send(): return lax.ppermute(self.after(value), axis, pairs)  159 us
    ppermute x85, starting transfers between devices, send(): return lax.ppermute(self.after(value), axis, pairs)  73.4 us
    pallas_call x4, Pallas kernels, product(): pl.pallas_call(product_kernel, grid=(8,), in_specs=[by_rows(step, total),...  47.1 us
    pallas_call x2, Pallas kernels, attend_back(): pl.pallas_call(functools.partial(attention_backward, [len(group) for grou...  34.8 us
    pallas_call x2, Pallas kernels, spread(): pl.pallas_call(functools.partial(spread_kernel, n, split), grid=(4,), in_...  33.5 us
    pallas_call x9, Pallas kernels, grow(): pl.pallas_call(functools.partial(grow_kernel, split, narrow, len(products...  27.4 us
    pallas_call x4, Pallas kernels, gathered(): pl.pallas_call(functools.partial(gathered_kernel, with_all), grid=(4,), i...  23.3 us
    unnamed x136, local copies, waits for them, and re-layouts  23.2 us
  transfers between devices with their start and end apart: 85, of which 44 were waited for; matrix products, arithmetic and copies ran while one was open for 6% of the time, Pallas kernels for 45%

profile of v6, /device:TPU:0, one launch (start us, length us, event | category | flops | bytes accessed | tf_op | source)
XLA Modules:
  0.0 554.2 jit_solution(3537313697997200446)
XLA Ops:
  12.7 10.0 %collective-permute-done.refs_12_.refs_15_.refs_16_ = bf16[272,1152]{1,0:T(8,128)(2,1)S(1)} collective-permute-done((bf16[272,1152]{1,0:T(8,128)(2,1)S(1)}, bf16[272,1152]{1,0:T(8,128)(2,1)S(1)}, u32[]{:S(2)}, u32[]{:S(2)}) %collective-permute-start) | collective-permute-done | bytes 626720 | tf_op jit(solution)/shard_map/ppermute | solution.py:60
  33.0 5.9 %collective-permute-done.2.refs_11_.refs_14_.refs_15_ = bf16[272,1152]{1,0:T(8,128)(2,1)S(1)} collective-permute-done((bf16[272,1152]{1,0:T(8,128)(2,1)S(1)}, bf16[272,1152]{1,0:T(8,128)(2,1)S(1)}, u32[]{:S(2)}, u32[]{:S(2)}) %collective-permute-start.2) | collective-permute-done | bytes 626720 | tf_op jit(solution)/shard_map/ppermute | solution.py:60
  44.1 9.8 %collective-permute-done.4.refs_10_.refs_13_.refs_14_ = bf16[272,1152]{1,0:T(8,128)(2,1)S(1)} collective-permute-done((bf16[272,1152]{1,0:T(8,128)(2,1)S(1)}, bf16[272,1152]{1,0:T(8,128)(2,1)S(1)}, u32[]{:S(2)}, u32[]{:S(2)}) %collective-permute-start.4) | collective-permute-done | bytes 626720 | tf_op jit(solution)/shard_map/ppermute | solution.py:60
  60.4 5.0 gathered.4.refs_0_
  80.3 20.0 %attend.1 = (bf16[2048,1024]{1,0:T(8,128)(2,1)}, bf16[1024,512]{1,0:T(8,128)(2,1)}, bf16[1024,128]{1,0:T(8,128)(2,1)}, bf16[1024,512]{1,0:T(8,128)(2,1)}, f32[10...) custom-call(bf16[1024,2176]{1,0:T(8,128)(2,1)} %gathered.4.refs_0_, ...), custom_call_target="tpu_custom_call" | custom-call | tf_op jit(solution)/shard_map/attend/pallas_call | solution.py:301
  108.7 6.5 %gathered.5 = (bf16[1024,2048]{1,0:T(8,128)(2,1)}, bf16[2048,1024]{1,0:T(8,128)(2,1)}) custom-call(bf16[256,2048]{1,0:T(8,128)(2,1)} %shuffle.5.own.rest_ref, bf16[256,2048]{1,0:T(8,128)(2,1)} %collective-permute-done.16.pair, bf16[256,2048]{1,0:T(8,128)(2,1)} %collective-permute-done.17.core, bf16[128,2048]{1,0:T(8,128)(2,1)} %copy-done.55, ...), custom_call_target="tpu_custom_call" | custom-call | tf_op jit(solution)/shard_map/gathered/pallas_call | solution.py:481
  119.5 19.5 %collective-permute-done.22.refs_6_ = bf16[256,2816]{1,0:T(8,128)(2,1)S(1)} collective-permute-done((bf16[256,2816]{1,0:T(8,128)(2,1)}, bf16[256,2816]{1,0:T(8,128)(2,1)S(1)}, u32[]{:S(2)}, u32[]{:S(2)}) %collective-permute-start.22) | collective-permute-done | bytes 1441824 | tf_op jit(solution)/shard_map/ppermute | solution.py:60
  143.5 3.7 join.1
  148.7 24.8 %collective-permute-done.25.refs_5_ = bf16[256,2816]{1,0:T(8,128)(2,1)S(1)} collective-permute-done((bf16[256,2816]{1,0:T(8,128)(2,1)}, bf16[256,2816]{1,0:T(8,128)(2,1)S(1)}, u32[]{:S(2)}, u32[]{:S(2)}) %collective-permute-start.25) | collective-permute-done | bytes 1441824 | tf_op jit(solution)/shard_map/ppermute | solution.py:60
  182.1 6.4 %gathered.6 = (bf16[1024,2048]{1,0:T(8,128)(2,1)}, bf16[2048,1024]{1,0:T(8,128)(2,1)}) custom-call(bf16[256,2048]{1,0:T(8,128)(2,1)} %get-tuple-element.774.own, bf16[256,2048]{1,0:T(8,128)(2,1)} %copy-done.15, bf16[256,2048]{1,0:T(8,128)(2,1)} %collective-permute-done.27.core, bf16[128,2048]{1,0:T(8,128)(2,1)} %copy-done.57, bf16[128,2048]{1,0:T(8,128)(2,1)} %copy-done.58), custom_call_target="tpu_custom_call" | custom-call | tf_op jit(solution)/shard_map/gathered/pallas_call | solution.py:481
  188.4 5.5 collective-permute-done.30.refs_8_
  197.3 20.9 %feed.1 = (bf16[1024,1408]{1,0:T(8,128)(2,1)}, bf16[1024,1408]{1,0:T(8,128)(2,1)}, bf16[1024,1408]{1,0:T(8,128)(2,1)}) custom-call(bf16[1024,2048]{1,0:T(8,128)(2,1)} %get-tuple-element.790.refs_0_, bf16[256,2816]{1,0:T(8,128)(2,1)} %copy-done, bf16[256,2816]{1,0:T(8,128)(2,1)} %collective-permute-done.13.refs_2_, ...), custom_call_target="tpu_custom_call" | custom-call | tf_op jit(solution)/shard_map/feed/pallas_call | solution.py:535
  220.2 12.1 %product.4 = (bf16[2048,1408]{1,0:T(8,128)(2,1)}, bf16[256,768]{1,0:T(8,128)(2,1)}, bf16[256,640]{1,0:T(8,128)(2,1)}) custom-call(bf16[2048,1024]{1,0:T(8,128)(2,1)} %get-tuple-element.812.left, bf16[1024,1408]{1,0:T(8,128)(2,1)} %get-tuple-element.946.right.refs_0_), custom_call_target="tpu_custom_call" | custom-call | tf_op jit(solution)/shard_map/product/pallas_call | solution.py:612
  237.8 14.2 %collective-permute-done.36.refs_7_.refs_5_ = bf16[256,1408]{1,0:T(8,128)(2,1)S(1)} collective-permute-done((bf16[256,1408]{1,0:T(8,128)(2,1)}, bf16[256,1408]{1,0:T(8,128)(2,1)S(1)}, u32[]{:S(2)}, u32[]{:S(2)}) %collective-permute-start.36) | collective-permute-done | bytes 720928 | tf_op jit(solution)/shard_map/ppermute | solution.py:60
  256.2 7.0 %collective-permute-done.39.refs_11_.refs_9_ = bf16[256,640]{1,0:T(8,128)(2,1)S(1)} collective-permute-done((bf16[256,640]{1,0:T(8,128)(2,1)S(1)}, bf16[256,640]{1,0:T(8,128)(2,1)S(1)}, u32[]{:S(2)}, u32[]{:S(2)}) %collective-permute-start.39) | collective-permute-done | bytes 327712 | tf_op jit(solution)/shard_map/ppermute | solution.py:60
  273.8 12.5 %feed_back.1.right.refs_0_ = bf16[1024,2816]{1,0:T(8,128)(2,1)} custom-call(bf16[1024,2048]{1,0:T(8,128)(2,1)} %get-tuple-element.852.refs_0_, bf16[1024,1408]{1,0:T(8,128)(2,1)} %get-tuple-element.853.refs_1_, bf16[1024,1408]{1,0:T(8,128)(2,1)} %get-tuple-element.854.refs_2_, bf16[256,1408]{1,0:T(8,128)(2,1)} %bitcast.27, bf16[256,1408]{1,0:T(8,128)(2,1)} %copy-done.19, ...), custom_call_target="tpu_custom_call" | custom-call | tf_op jit(solution)/shard_map/feed_back/pallas_call | solution.py:562
  292.8 18.0 %product.5 = (bf16[2048,2816]{1,0:T(8,128)(2,1)}, bf16[256,1408]{1,0:T(8,128)(2,1)}, bf16[256,1408]{1,0:T(8,128)(2,1)}) custom-call(bf16[2048,1024]{1,0:T(8,128)(2,1)} %get-tuple-element.880.left, bf16[1024,2816]{1,0:T(8,128)(2,1)} %feed_back.1.right.refs_0_), custom_call_target="tpu_custom_call" | custom-call | tf_op jit(solution)/shard_map/product/pallas_call | solution.py:612
  319.5 20.9 %spread.2 = (bf16[256,2048]{1,0:T(8,128)(2,1)}, bf16[256,2048]{1,0:T(8,128)(2,1)}, bf16[256,2048]{1,0:T(8,128)(2,1)}, bf16[256,2048]{1,0:T(8,128)(2,1)}) custom-call(bf16[1024,2816]{1,0:T(8,128)(2,1)} %feed_back.1.right.refs_0_, bf16[256,2816]{1,0:T(8,128)(2,1)} %copy-done, bf16[256,2816]{1,0:T(8,128)(2,1)} %collective-permute-done.13.refs_2_, ...), custom_call_target="tpu_custom_call" | custom-call | tf_op jit(solution)/shard_map/spread/pallas_call | solution.py:584
  362.0 12.5 %spread.3 = (bf16[256,2048]{1,0:T(8,128)(2,1)}, bf16[256,2048]{1,0:T(8,128)(2,1)}, bf16[256,2048]{1,0:T(8,128)(2,1)}, bf16[256,2048]{1,0:T(8,128)(2,1)}) custom-call(bf16[1024,1408]{1,0:T(8,128)(2,1)} %get-tuple-element.946.right.refs_0_, bf16[256,1408]{1,0:T(8,128)(2,1)} %bitcast.28, bf16[256,1408]{1,0:T(8,128)(2,1)} %copy-done.19, ...), custom_call_target="tpu_custom_call" | custom-call | tf_op jit(solution)/shard_map/spread/pallas_call | solution.py:584
  378.9 4.0 grow.13
  385.0 5.0 norm_back.2
  393.9 17.4 %attend_back.2 = (bf16[1024,640]{1,0:T(8,128)(2,1)}, bf16[256,2048]{1,0:T(8,128)(2,1)}, bf16[256,2048]{1,0:T(8,128)(2,1)}) custom-call(bf16[256,2048]{1,0:T(8,128)(2,1)} %get-tuple-element.1050.refs_0_.own, bf16[256,2048]{1,0:T(8,128)(2,1)} %copy-done.16, bf16[1024,512]{1,0:T(8,128)(2,1)} %get-tuple-element.1066.refs_2_.refs_3_, ...), custom_call_target="tpu_custom_call" | custom-call | tf_op jit(solution)/shard_map/attend_back/pallas_call | solution.py:419
  414.9 4.0 grow.14
  423.4 5.4 gathered.7.left
  428.8 8.1 %product.6 = (bf16[2048,512]{1,0:T(8,128)(2,1)}, bf16[256,512]{1,0:T(8,128)(2,1)}) custom-call(bf16[2048,1024]{1,0:T(8,128)(2,1)} %gathered.7.left, bf16[1024,512]{1,0:T(8,128)(2,1)} %get-tuple-element.1059.right), custom_call_target="tpu_custom_call" | custom-call | tf_op jit(solution)/shard_map/product/pallas_call | solution.py:612
  437.5 17.4 %attend_back.3 = (bf16[1024,640]{1,0:T(8,128)(2,1)}, bf16[256,2048]{1,0:T(8,128)(2,1)}, bf16[256,2048]{1,0:T(8,128)(2,1)}) custom-call(bf16[256,2048]{1,0:T(8,128)(2,1)} %copy-done.3, bf16[128,2048]{1,0:T(8,128)(2,1)} %copy-done.22, bf16[128,2048]{1,0:T(8,128)(2,1)} %copy-done.23, ...), custom_call_target="tpu_custom_call", output_to_operand_aliasing={{0}: (19, {})} | custom-call | tf_op jit(solution)/shard_map/attend_back/pallas_call | solution.py:419
  464.3 9.0 %product.7 = (bf16[2048,640]{1,0:T(8,128)(2,1)}, bf16[256,640]{1,0:T(8,128)(2,1)}) custom-call(bf16[2048,1024]{1,0:T(8,128)(2,1)} %get-tuple-element.1099.left, bf16[1024,640]{1,0:T(8,128)(2,1)} %get-tuple-element.1100.right), custom_call_target="tpu_custom_call" | custom-call | tf_op jit(solution)/shard_map/product/pallas_call | solution.py:612
  476.4 3.6 last.4
  488.1 5.3 norm_back.3
  514.1 9.8 %collective-permute-done.80 = f32[2,2048]{1,0:T(2,128)S(1)} collective-permute-done((f32[2,2048]{1,0:T(2,128)S(1)}, f32[2,2048]{1,0:T(2,128)S(1)}, u32[]{:S(2)}, u32[]{:S(2)}) %collective-permute-start.80) | collective-permute-done | bytes 16416 | tf_op jit(solution)/shard_map/ppermute | solution.py:60
  532.2 4.2 shuffle.7
  537.8 6.4 %collective-permute-done.81 = f32[2,2048]{1,0:T(2,128)S(1)} collective-permute-done((f32[2,2048]{1,0:T(2,128)S(1)}, f32[2,2048]{1,0:T(2,128)S(1)}, u32[]{:S(2)}, u32[]{:S(2)}) %collective-permute-start.81) | collective-permute-done | bytes 16416 | tf_op jit(solution)/shard_map/ppermute | solution.py:60
  (377 shorter events, 217.8 us)
Async XLA Ops:
  28.7 26.6 %collective-permute-start.8 = (bf16[256,2176]{1,0:T(8,128)(2,1)}, bf16[256,2176]{1,0:T(8,128)(2,1)}, u32[]{:S(2)}, u32[]{:S(2)}) collective-permute-start(bf16[256,2176]{1,0:T(8,128)(2,1)} %pad_maximum_fusion.1.own), channel_id=1, source_target_pairs={{0,2},{1,3},{2,0},{3,1},{4,6},{5,7},{6,4},{7,5},{8,10},{9,11},{10,... | collective-permute-start | bytes 3342344 | tf_op jit(solution)/shard_map/ppermute | solution.py:60
  68.6 33.1 %collective-permute-start.12 = (bf16[256,2816]{1,0:T(8,128)(2,1)S(1)}, bf16[256,2816]{1,0:T(8,128)(2,1)}, u32[]{:S(2)}, u32[]{:S(2)}) collective-permute-start(bf16[256,2816]{1,0:T(8,128)(2,1)S(1)} %pad_maximum_fusion.refs_1_), channel_id=1, source_target_pairs={{0,8},{8,16},{16,24},{24,28},{28,20},{20,12},{12,4},{4,0},{1,9},{9... | collective-permute-start | bytes 4325384 | tf_op jit(solution)/shard_map/ppermute | solution.py:60
  70.1 32.8 %collective-permute-start.13 = (bf16[256,2816]{1,0:T(8,128)(2,1)S(1)}, bf16[256,2816]{1,0:T(8,128)(2,1)}, u32[]{:S(2)}, u32[]{:S(2)}) collective-permute-start(bf16[256,2816]{1,0:T(8,128)(2,1)S(1)} %pad_maximum_fusion.refs_1_), channel_id=1, source_target_pairs={{8,0},{16,8},{24,16},{28,24},{20,28},{12,20},{4,12},{0,4},{9,1},{1... | collective-permute-start | bytes 4325384 | tf_op jit(solution)/shard_map/ppermute | solution.py:60
  74.4 28.5 %collective-permute-start.16 = (bf16[256,2048]{1,0:T(8,128)(2,1)S(1)}, bf16[256,2048]{1,0:T(8,128)(2,1)}, u32[]{:S(2)}, u32[]{:S(2)}) collective-permute-start(bf16[256,2048]{1,0:T(8,128)(2,1)S(1)} %copy-done.2), channel_id=1, source_target_pairs={{0,2},{1,3},{2,0},{3,1},{4,6},{5,7},{6,4},{7,5},{8,10},{9,11},{10,... | collective-permute-start | bytes 3145736 | tf_op jit(solution)/shard_map/ppermute | solution.py:60
  104.8 34.1 %collective-permute-start.22 = (bf16[256,2816]{1,0:T(8,128)(2,1)}, bf16[256,2816]{1,0:T(8,128)(2,1)S(1)}, u32[]{:S(2)}, u32[]{:S(2)}) collective-permute-start(bf16[256,2816]{1,0:T(8,128)(2,1)} %collective-permute-done.12.refs_7_), channel_id=1, source_target_pairs={{0,8},{8,16},{16,24},{24,28},{28,20},{20,12},{12,4},{4,0},{1,9},{9... | collective-permute-start | bytes 4325384 | tf_op jit(solution)/shard_map/ppermute | solution.py:60
  105.6 34.4 %collective-permute-start.23 = (bf16[256,2816]{1,0:T(8,128)(2,1)}, bf16[256,2816]{1,0:T(8,128)(2,1)}, u32[]{:S(2)}, u32[]{:S(2)}) collective-permute-start(bf16[256,2816]{1,0:T(8,128)(2,1)} %collective-permute-done.13.refs_2_), channel_id=1, source_target_pairs={{8,0},{16,8},{24,16},{28,24},{20,28},{12,20},{4,12},{0,4},{9,1},{1... | collective-permute-start | bytes 4325384 | tf_op jit(solution)/shard_map/ppermute | solution.py:60
  117.6 24.5 %collective-permute-start.20 = (bf16[256,2048]{1,0:T(8,128)(2,1)}, bf16[256,2048]{1,0:T(8,128)(2,1)}, u32[]{:S(2)}, u32[]{:S(2)}) collective-permute-start(bf16[256,2048]{1,0:T(8,128)(2,1)} %get-tuple-element.738), channel_id=1, source_target_pairs={{0,1},{1,0},{2,3},{3,2},{4,5},{5,4},{6,7},{7,6},{8,9},{9,8},{10,11... | collective-permute-start | bytes 3145736 | tf_op jit(solution)/shard_map/ppermute | solution.py:60
  117.9 25.5 %collective-permute-start.21 = (bf16[256,2048]{1,0:T(8,128)(2,1)}, bf16[256,2048]{1,0:T(8,128)(2,1)}, u32[]{:S(2)}, u32[]{:S(2)}) collective-permute-start(bf16[256,2048]{1,0:T(8,128)(2,1)} %plus.4), channel_id=1, source_target_pairs={{0,2},{1,3},{2,0},{3,1},{4,6},{5,7},{6,4},{7,5},{8,10},{9,11},{10,... | collective-permute-start | bytes 3145736 | tf_op jit(solution)/shard_map/ppermute | solution.py:60
  140.0 33.5 %collective-permute-start.25 = (bf16[256,2816]{1,0:T(8,128)(2,1)}, bf16[256,2816]{1,0:T(8,128)(2,1)S(1)}, u32[]{:S(2)}, u32[]{:S(2)}) collective-permute-start(bf16[256,2816]{1,0:T(8,128)(2,1)} %copy-done.9), channel_id=1, source_target_pairs={{0,8},{8,16},{16,24},{24,28},{28,20},{20,12},{12,4},{4,0},{1,9},{9... | collective-permute-start | bytes 4325384 | tf_op jit(solution)/shard_map/ppermute | solution.py:60
  140.9 33.2 %collective-permute-start.26 = (bf16[256,2816]{1,0:T(8,128)(2,1)}, bf16[256,2816]{1,0:T(8,128)(2,1)S(1)}, u32[]{:S(2)}, u32[]{:S(2)}) collective-permute-start(bf16[256,2816]{1,0:T(8,128)(2,1)} %collective-permute-done.23.refs_3_), channel_id=1, source_target_pairs={{8,0},{16,8},{24,16},{28,24},{20,28},{12,20},{4,12},{0,4},{9,1},{1... | collective-permute-start | bytes 4325384 | tf_op jit(solution)/shard_map/ppermute | solution.py:60
  147.2 31.0 %collective-permute-start.24 = (bf16[256,2048]{1,0:T(8,128)(2,1)}, bf16[256,2048]{1,0:T(8,128)(2,1)S(1)}, u32[]{:S(2)}, u32[]{:S(2)}) collective-permute-start(bf16[256,2048]{1,0:T(8,128)(2,1)} %get-tuple-element.774.own), channel_id=1, source_target_pairs={{0,2},{1,3},{2,0},{3,1},{4,6},{5,7},{6,4},{7,5},{8,10},{9,11},{10,... | collective-permute-start | bytes 3145736 | tf_op jit(solution)/shard_map/ppermute | solution.py:60
  195.2 22.9 %collective-permute-start.32 = (bf16[256,1408]{1,0:T(8,128)(2,1)S(1)}, bf16[256,1408]{1,0:T(8,128)(2,1)S(1)}, u32[]{:S(2)}, u32[]{:S(2)}) collective-permute-start(bf16[256,1408]{1,0:T(8,128)(2,1)S(1)} %bitcast.25), channel_id=1, source_target_pairs={{0,8},{8,16},{16,24},{24,28},{28,20},{20,12},{12,4},{4,0},{1,9},{9... | collective-permute-start | bytes 2162696 | tf_op jit(solution)/shard_map/ppermute | solution.py:60
  196.1 22.0 %collective-permute-start.33 = (bf16[256,1408]{1,0:T(8,128)(2,1)S(1)}, bf16[256,1408]{1,0:T(8,128)(2,1)S(1)}, u32[]{:S(2)}, u32[]{:S(2)}) collective-permute-start(bf16[256,1408]{1,0:T(8,128)(2,1)S(1)} %bitcast.26), channel_id=1, source_target_pairs={{8,0},{16,8},{24,16},{28,24},{20,28},{12,20},{4,12},{0,4},{9,1},{1... | collective-permute-start | bytes 2162696 | tf_op jit(solution)/shard_map/ppermute | solution.py:60
  315.2 25.2 %collective-permute-start.46 = (bf16[256,1408]{1,0:T(8,128)(2,1)}, bf16[256,1408]{1,0:T(8,128)(2,1)S(1)}, u32[]{:S(2)}, u32[]{:S(2)}) collective-permute-start(bf16[256,1408]{1,0:T(8,128)(2,1)} %get-tuple-element.896), channel_id=1, source_target_pairs={{0,8},{8,16},{16,24},{24,28},{28,20},{20,12},{12,4},{4,0},{1,9},{9... | collective-permute-start | bytes 2162696 | tf_op jit(solution)/shard_map/ppermute | solution.py:60
  315.8 24.6 %collective-permute-start.47 = (bf16[256,1408]{1,0:T(8,128)(2,1)}, bf16[256,1408]{1,0:T(8,128)(2,1)S(1)}, u32[]{:S(2)}, u32[]{:S(2)}) collective-permute-start(bf16[256,1408]{1,0:T(8,128)(2,1)} %get-tuple-element.898), channel_id=1, source_target_pairs={{8,0},{16,8},{24,16},{28,24},{20,28},{12,20},{4,12},{0,4},{9,1},{1... | collective-permute-start | bytes 2162696 | tf_op jit(solution)/shard_map/ppermute | solution.py:60
  317.3 26.5 %collective-permute-start.48 = (bf16[256,1408]{1,0:T(8,128)(2,1)}, bf16[256,1408]{1,0:T(8,128)(2,1)S(1)}, u32[]{:S(2)}, u32[]{:S(2)}) collective-permute-start(bf16[256,1408]{1,0:T(8,128)(2,1)} %get-tuple-element.920), channel_id=1, source_target_pairs={{0,8},{8,16},{16,24},{24,28},{28,20},{20,12},{12,4},{4,0},{1,9},{9... | collective-permute-start | bytes 2162696 | tf_op jit(solution)/shard_map/ppermute | solution.py:60
  317.8 26.3 %collective-permute-start.49 = (bf16[256,1408]{1,0:T(8,128)(2,1)}, bf16[256,1408]{1,0:T(8,128)(2,1)S(1)}, u32[]{:S(2)}, u32[]{:S(2)}) collective-permute-start(bf16[256,1408]{1,0:T(8,128)(2,1)} %get-tuple-element.922), channel_id=1, source_target_pairs={{8,0},{16,8},{24,16},{28,24},{20,28},{12,20},{4,12},{0,4},{9,1},{1... | collective-permute-start | bytes 2162696 | tf_op jit(solution)/shard_map/ppermute | solution.py:60
  349.0 27.7 %collective-permute-start.52 = (bf16[256,2816]{1,0:T(8,128)(2,1)}, bf16[256,2816]{1,0:T(8,128)(2,1)S(1)}, u32[]{:S(2)}, u32[]{:S(2)}) collective-permute-start(bf16[256,2816]{1,0:T(8,128)(2,1)} %get-tuple-element.965), channel_id=1, source_target_pairs={{0,8},{8,16},{16,24},{24,28},{28,20},{20,12},{12,4},{4,0},{1,9},{9... | collective-permute-start | bytes 4325384 | tf_op jit(solution)/shard_map/ppermute | solution.py:60
  349.7 27.4 %collective-permute-start.53 = (bf16[256,2816]{1,0:T(8,128)(2,1)}, bf16[256,2816]{1,0:T(8,128)(2,1)S(1)}, u32[]{:S(2)}, u32[]{:S(2)}) collective-permute-start(bf16[256,2816]{1,0:T(8,128)(2,1)} %get-tuple-element.967), channel_id=1, source_target_pairs={{8,0},{16,8},{24,16},{28,24},{20,28},{12,20},{4,12},{0,4},{9,1},{1... | collective-permute-start | bytes 4325384 | tf_op jit(solution)/shard_map/ppermute | solution.py:60
  357.6 27.3 %collective-permute-start.56 = (bf16[256,2048]{1,0:T(8,128)(2,1)}, bf16[256,2048]{1,0:T(8,128)(2,1)}, u32[]{:S(2)}, u32[]{:S(2)}) collective-permute-start(bf16[256,2048]{1,0:T(8,128)(2,1)} %get-tuple-element.984), channel_id=1, source_target_pairs={{0,1},{1,0},{2,3},{3,2},{4,5},{5,4},{6,7},{7,6},{8,9},{9,8},{10,11... | collective-permute-start | bytes 3145736 | tf_op jit(solution)/shard_map/ppermute | solution.py:60
  357.8 27.2 %collective-permute-start.57 = (bf16[256,2048]{1,0:T(8,128)(2,1)}, bf16[256,2048]{1,0:T(8,128)(2,1)}, u32[]{:S(2)}, u32[]{:S(2)}) collective-permute-start(bf16[256,2048]{1,0:T(8,128)(2,1)} %plus.5), channel_id=1, source_target_pairs={{0,2},{1,3},{2,0},{3,1},{4,6},{5,7},{6,4},{7,5},{8,10},{9,11},{10,... | collective-permute-start | bytes 3145736 | tf_op jit(solution)/shard_map/ppermute | solution.py:60
  382.9 31.7 %collective-permute-start.54 = (bf16[256,2816]{1,0:T(8,128)(2,1)}, bf16[256,2816]{1,0:T(8,128)(2,1)}, u32[]{:S(2)}, u32[]{:S(2)}) collective-permute-start(bf16[256,2816]{1,0:T(8,128)(2,1)} %get-tuple-element.979), channel_id=1, source_target_pairs={{0,8},{8,16},{16,24},{24,28},{28,20},{20,12},{12,4},{4,0},{1,9},{9... | collective-permute-start | bytes 4325384 | tf_op jit(solution)/shard_map/ppermute | solution.py:60
  383.5 31.4 %collective-permute-start.55 = (bf16[256,2816]{1,0:T(8,128)(2,1)}, bf16[256,2816]{1,0:T(8,128)(2,1)}, u32[]{:S(2)}, u32[]{:S(2)}) collective-permute-start(bf16[256,2816]{1,0:T(8,128)(2,1)} %get-tuple-element.981), channel_id=1, source_target_pairs={{8,0},{16,8},{24,16},{28,24},{20,28},{12,20},{4,12},{0,4},{9,1},{1... | collective-permute-start | bytes 4325384 | tf_op jit(solution)/shard_map/ppermute | solution.py:60
  390.0 28.8 %collective-permute-start.61 = (bf16[256,2048]{1,0:T(8,128)(2,1)}, bf16[256,2048]{1,0:T(8,128)(2,1)S(1)}, u32[]{:S(2)}, u32[]{:S(2)}) collective-permute-start(bf16[256,2048]{1,0:T(8,128)(2,1)} %get-tuple-element.1050.refs_0_.own), channel_id=1, source_target_pairs={{0,2},{1,3},{2,0},{3,1},{4,6},{5,7},{6,4},{7,5},{8,10},{9,11},{10,... | collective-permute-start | bytes 3145736 | tf_op jit(solution)/shard_map/ppermute | solution.py:60
  419.5 53.7 %collective-permute-start.59 = (bf16[256,2816]{1,0:T(8,128)(2,1)}, bf16[256,2816]{1,0:T(8,128)(2,1)S(1)}, u32[]{:S(2)}, u32[]{:S(2)}) collective-permute-start(bf16[256,2816]{1,0:T(8,128)(2,1)} %get-tuple-element.1038), channel_id=1, source_target_pairs={{0,8},{8,16},{16,24},{24,28},{28,20},{20,12},{12,4},{4,0},{1,9},{9... | collective-permute-start | bytes 4325384 | tf_op jit(solution)/shard_map/ppermute | solution.py:60
  420.4 52.9 %collective-permute-start.60 = (bf16[256,2816]{1,0:T(8,128)(2,1)}, bf16[256,2816]{1,0:T(8,128)(2,1)}, u32[]{:S(2)}, u32[]{:S(2)}) collective-permute-start(bf16[256,2816]{1,0:T(8,128)(2,1)} %get-tuple-element.1040), channel_id=1, source_target_pairs={{8,0},{16,8},{24,16},{28,24},{20,28},{12,20},{4,12},{0,4},{9,1},{1... | collective-permute-start | bytes 4325384 | tf_op jit(solution)/shard_map/ppermute | solution.py:60
  462.2 24.6 %collective-permute-start.68 = (bf16[256,2048]{1,0:T(8,128)(2,1)}, bf16[256,2048]{1,0:T(8,128)(2,1)S(1)}, u32[]{:S(2)}, u32[]{:S(2)}) collective-permute-start(bf16[256,2048]{1,0:T(8,128)(2,1)} %get-tuple-element.1118), channel_id=1, source_target_pairs={{0,1},{1,0},{2,3},{3,2},{4,5},{5,4},{6,7},{7,6},{8,9},{9,8},{10,11... | collective-permute-start | bytes 3145736 | tf_op jit(solution)/shard_map/ppermute | solution.py:60
  462.3 25.8 %collective-permute-start.69 = (bf16[256,2048]{1,0:T(8,128)(2,1)}, bf16[256,2048]{1,0:T(8,128)(2,1)}, u32[]{:S(2)}, u32[]{:S(2)}) collective-permute-start(bf16[256,2048]{1,0:T(8,128)(2,1)} %plus.6), channel_id=1, source_target_pairs={{0,2},{1,3},{2,0},{3,1},{4,6},{5,7},{6,4},{7,5},{8,10},{9,11},{10,... | collective-permute-start | bytes 3145736 | tf_op jit(solution)/shard_map/ppermute | solution.py:60
  503.7 26.6 %collective-permute-start.74 = (bf16[256,2048]{1,0:T(8,128)(2,1)}, bf16[256,2048]{1,0:T(8,128)(2,1)S(1)}, u32[]{:S(2)}, u32[]{:S(2)}) collective-permute-start(bf16[256,2048]{1,0:T(8,128)(2,1)} %get-tuple-element.1169), channel_id=1, source_target_pairs={{0,1},{1,0},{2,3},{3,2},{4,5},{5,4},{6,7},{7,6},{8,9},{9,8},{10,11... | collective-permute-start | bytes 3145736 | tf_op jit(solution)/shard_map/ppermute | solution.py:60
  503.7 26.6 %collective-permute-start.75 = (bf16[256,2048]{1,0:T(8,128)(2,1)}, bf16[256,2048]{1,0:T(8,128)(2,1)S(1)}, u32[]{:S(2)}, u32[]{:S(2)}) collective-permute-start(bf16[256,2048]{1,0:T(8,128)(2,1)} %plus.7), channel_id=1, source_target_pairs={{0,2},{1,3},{2,0},{3,1},{4,6},{5,7},{6,4},{7,5},{8,10},{9,11},{10,... | collective-permute-start | bytes 3145736 | tf_op jit(solution)/shard_map/ppermute | solution.py:60
  528.2 21.4 %collective-permute-start.83 = (bf16[256,1152]{1,0:T(8,128)(2,1)}, bf16[256,1152]{1,0:T(8,128)(2,1)S(1)}, u32[]{:S(2)}, u32[]{:S(2)}) collective-permute-start(bf16[256,1152]{1,0:T(8,128)(2,1)} %get-tuple-element.1229), channel_id=1, source_target_pairs={{0,8},{8,16},{16,24},{24,28},{28,20},{20,12},{12,4},{4,0},{1,9},{9... | collective-permute-start | bytes 1769480 | tf_op jit(solution)/shard_map/ppermute | solution.py:60
  529.6 20.0 %collective-permute-start.84 = (bf16[256,1152]{1,0:T(8,128)(2,1)}, bf16[256,1152]{1,0:T(8,128)(2,1)S(1)}, u32[]{:S(2)}, u32[]{:S(2)}) collective-permute-start(bf16[256,1152]{1,0:T(8,128)(2,1)} %get-tuple-element.1231), channel_id=1, source_target_pairs={{8,0},{16,8},{24,16},{28,24},{20,28},{12,20},{4,12},{0,4},{9,1},{1... | collective-permute-start | bytes 1769480 | tf_op jit(solution)/shard_map/ppermute | solution.py:60
  (117 other events, 929.9 us)
